TPU v7x, 512 devices: a whole 4x8x8 slice. The times are simulated.
512 devices in a mesh: row: 16 (over z, y_hi), col: 32 (over x, y_lo, core).
Axes of the slice: x: 4, y: 8 (y_hi: 2, y_lo: 4; y = y_hi * 4 + y_lo), z: 8, core: 2. Of those that a mesh axis runs over, the one named last changes fastest.
Arguments:
- ainv: float32 [4096, 4096], P('row', 'col'), may hold values from -6 to 6
- lpanel: float32 [4096, 3, 512], P('row', None, 'col'), may hold values from -0.125 to 0.125
- kk_inverse: float32 [3, 512, 512], P(None, 'row'), may hold values from -6 to 6
- row_blocks: int32 [3, 32], replicated, may hold values from 0 to 31, as said below
- list_len: int32 [3], replicated, may hold values from 8 to 24
Outputs:
- ainv_ik: float32 [4096, 3, 512], P(('row', 'col'))
- ainv_kk: float32 [3, 512, 512], P(None, 'row')
- ainv_ki: float32 [3, 512, 4096], P(None, 'row', 'col')
Inputs may be any that keep to these rules, and one draw needn't show every extreme that they name: `row_blocks`: entries at positions below list_len[s] are distinct tile numbers; later entries repeat the first entry of the row.
All inputs are finite; a program needn't handle non-finite values.
Results may differ from a plain program's by a relative error of at most 0.00008.
Values sent between devices are 32-bit elements; how exact they have to be, the bound alone decides.
No kernel may reach another device: no remote copies, remote signals or barrier semaphores. Data moves between devices by JAX's collectives and lax.ppermute only.
A program may use at most 64 MiB of HBM per device.

v0:
```python
import jax
import jax.numpy as jnp
from jax import lax
from jax.sharding import PartitionSpec as P

TILE = 128


def copy_for_each(shard, axis):
    copies = jnp.broadcast_to(shard, (lax.axis_size(axis), *shard.shape))
    return lax.all_to_all(copies, axis, split_axis=0, concat_axis=0, tiled=True)


def joined_along(blocks, dim):
    blocks = jnp.moveaxis(blocks, 0, dim)
    shape = blocks.shape
    return blocks.reshape(*shape[:dim], shape[dim] * shape[dim + 1], *shape[dim + 2 :])


def gathered_copies(shard, axis, dim):
    blocks = copy_for_each(shard, axis)
    return joined_along(blocks, dim)


def picked_2(shard, axis, root):
    return lax.dynamic_index_in_dim(lax.all_gather(shard, axis), root, 0, keepdims=False)


def in_blocks(shard, dim, length):
    before, after = (shard.shape[:dim], shard.shape[dim + 1 :])
    return jnp.moveaxis(shard.reshape(*before, length, -1, *after), dim, 0)


def sum_at_owner(shard, axis, dim):
    length = lax.axis_size(axis)
    blocks = lax.all_to_all(in_blocks(shard, dim, length), axis, 0, 0, tiled=True)
    return jnp.sum(blocks, axis=0)


def tile_masks(row_blocks, list_len, ntiles):
    tiles = jnp.arange(ntiles, dtype=jnp.int32)
    valid = jnp.arange(row_blocks.shape[1], dtype=jnp.int32)[None, :] < list_len[:, None]
    hit = (row_blocks[:, :, None] == tiles[None, None, :]) & valid[:, :, None]
    return jnp.any(hit, axis=1).astype(jnp.float32).T


def shards(ainv, lpanel, kk_inverse, row_blocks, list_len):
    nrows = lax.axis_size("row")
    ncols = lax.axis_size("col")
    ratio = ncols // nrows
    row_index = lax.axis_index("row")
    col_index = lax.axis_index("col")
    rows_dev = ainv.shape[0]
    cols_dev = ainv.shape[1]
    share = rows_dev // ncols
    tile_mask = tile_masks(row_blocks, list_len, rows_dev * nrows // TILE)
    whole = gathered_copies(lpanel, "col", 2)
    picked = lax.dynamic_slice_in_dim(tile_mask, row_index * rows_dev // TILE, rows_dev // TILE, 0)
    own_mask = jnp.repeat(picked, TILE, axis=0)
    masked_rows = whole * own_mask[:, :, None]
    piece = lax.dynamic_slice_in_dim(masked_rows, col_index % ratio * cols_dev, cols_dev, 0)
    col_panel = picked_2(piece, "row", col_index // ratio)
    product = jnp.einsum("ij,jsw->isw", ainv, col_panel, precision=lax.Precision.HIGHEST)
    ainv_ik = sum_at_owner(-product * own_mask[:, :, None], "col", 0)
    own_rows = lax.dynamic_slice_in_dim(whole, col_index * share, share, 0)
    term = jnp.einsum("isv,isw->svw", own_rows, ainv_ik, precision=lax.Precision.HIGHEST)
    diag_total = lax.psum(term, ("row", "col"))
    width_rows = kk_inverse.shape[1]
    ainv_kk = kk_inverse - lax.dynamic_slice_in_dim(
        diag_total, row_index * width_rows, width_rows, 1
    )
    grid_rows = gathered_copies(ainv_ik, "col", 0)
    send_part = lax.dynamic_slice_in_dim(grid_rows, col_index % ratio * cols_dev, cols_dev, 0)
    col_rows = picked_2(send_part, "row", col_index // ratio)
    own_cols = lax.dynamic_slice_in_dim(col_rows, row_index * width_rows, width_rows, 2)
    ainv_ki = jnp.transpose(own_cols, (1, 2, 0))
    return (ainv_ik, ainv_kk, ainv_ki)


def solution(mesh):
    placed = (P("row", "col"), P("row", None, "col"), P(None, "row", None), P(), P())
    return jax.shard_map(
        shards,
        mesh=mesh,
        in_specs=placed,
        out_specs=(P(("row", "col"), None, None), P(None, "row", None), P(None, "row", "col")),
        check_vma=False,
    )
```

profile of v0, /device:TPU:1, one launch (start us, length us, event | category | flops | bytes accessed | tf_op | source)
XLA Modules:
  0.0 933.1 jit_solution(11365944872106772658)
XLA Ops:
  7.2 0.0 copy-start
  7.2 2.2 broadcast_in_dim.6
  9.4 0.0 copy-start.4
  9.4 0.0 copy-start.3
  9.4 10.6 %all-to-all-start = ((f32[32,256,3,16]{1,3,2,0:T(8,128)}), f32[32,256,3,16]{1,3,2,0:T(8,128)S(1)}, u32[]{:S(2)}, u32[]{:S(2)}) async-start(f32[32,256,3,16]{1,3,2,0:T(8,128)} %broadcast_in_dim.6), calls=%async_computation | async-start | bytes 3145728 | tf_op jit(solution)/shard_map/all_to_all | solution.py:11
  20.0 0.0 all-gather.5.cloned.1.call-start
  20.0 0.0 copy-done.4
  20.0 0.1 iota_compare_fusion.1
  20.1 0.0 copy-done.3
  20.1 0.1 fusion.5
  20.2 0.1 dynamic-slice_bitcast_fusion
  20.3 0.1 broadcast_bitcast_fusion
  20.4 38.6 %all-to-all-done = f32[32,256,3,16]{1,3,2,0:T(8,128)S(1)} async-done(((f32[32,256,3,16]{1,3,2,0:T(8,128)}), f32[32,256,3,16]{1,3,2,0:T(8,128)S(1)}, u32[]{:S(2)}, u32[]{:S(2)}) %all-to-all-start) | async-done | bytes 1572896 | tf_op jit(solution)/shard_map/all_to_all | solution.py:11
  59.0 0.1 copy.25
  59.1 0.1 constant_dynamic-slice_fusion
  59.2 0.3 copy.33
  59.5 1.1 broadcast_multiply_fusion
  60.5 0.0 all-gather.5.cloned.1.call-update
  60.6 261.6 %all-gather.5.cloned.1.call-done = f32[2048,3,512]{2,0,1:T(8,128)} async-done(((f32[128,3,512]{2,0,1:T(8,128)}), f32[2048,3,512]{2,0,1:T(8,128)}) %all-gather.5.cloned.1.call-update) | async-done | bytes 12582928 | tf_op jit(solution)/shard_map/all_gather | solution.py:26
  322.2 0.0 copy-done
  322.2 2.6 fusion
  324.8 0.1 copy.28
  324.9 44.9 %all_to_all.15 = f32[32,8,3,512]{3,1,2,0:T(8,128)S(1)} all-to-all(f32[32,8,3,512]{3,1,2,0:T(8,128)S(1)} %copy.28), channel_id=1, replica_groups=mesh['row'=16,'col'=32] {'col'}, dimensions={0} | all-to-all | bytes 3145728 | tf_op jit(solution)/shard_map/all_to_all | solution.py:36
  369.8 0.1 reduce_sum.9
  369.9 0.0 copy-start.1
  369.9 1.3 broadcast_in_dim.16
  371.3 3.8 all-to-all-start.2
  375.0 0.0 all-reduce.2.cloned.1.call-start
  375.1 1.2 constant_dynamic-slice_fusion.3
  376.2 1.4 copy.34
  377.6 0.0 copy-done.1
  377.6 4.3 fusion.7
  381.9 0.0 all-reduce.2.cloned.1.call-update
  382.0 0.0 all-gather.7.cloned.1.call-start
  382.0 34.3 %all-to-all-done.2 = f32[32,8,3,512]{3,1,2,0:T(8,128)S(1)} async-done(((f32[32,8,3,512]{3,1,2,0:T(8,128)}), f32[32,8,3,512]{3,1,2,0:T(8,128)S(1)}, u32[]{:S(2)}, u32[]{:S(2)}) %all-to-all-start.2) | async-done | bytes 1572896 | tf_op jit(solution)/shard_map/all_to_all | solution.py:11
  416.3 0.1 copy.38
  416.4 0.0 copy-start.2
  416.4 0.9 constant_dynamic-slice_fusion.2
  417.4 0.0 all-gather.7.cloned.1.call-update
  417.4 244.5 %all-reduce.2.cloned.1.call-done = f32[3,512,512]{2,1,0:T(8,128)} async-done(((f32[3,512,512]{2,1,0:T(8,128)}), f32[3,512,512]{2,1,0:T(8,128)}) %all-reduce.2.cloned.1.call-update) | async-done | bytes 3145744 | tf_op jit(solution)/shard_map/psum | solution.py:67
  662.0 0.0 copy-done.2
  662.0 1.6 dynamic-slice_subtract_fusion
  663.6 261.1 %all-gather.7.cloned.1.call-done = f32[2048,3,512]{2,0,1:T(8,128)} async-done(((f32[128,3,512]{2,0,1:T(8,128)}), f32[2048,3,512]{2,0,1:T(8,128)}) %all-gather.7.cloned.1.call-update) | async-done | bytes 12582928 | tf_op jit(solution)/shard_map/all_gather | solution.py:26
  924.7 1.1 constant_dynamic-slice_fusion.1
  925.8 0.7 copy.31
  (3 shorter events, 0.0 us)
Async XLA Ops:
  7.2 315.0 %copy-start = (f32[256,128]{1,0:T(8,128)S(1)}, f32[256,128]{1,0:T(8,128)}, u32[]{:S(2)}) copy-start(f32[256,128]{1,0:T(8,128)} %param.5) | copy-start | bytes 393220
  9.4 10.7 %copy-start.4 = (s32[3]{0:T(128)S(1)}, s32[3]{0:T(128)}, u32[]{:S(2)}) copy-start(s32[3]{0:T(128)} %param.9) | copy-start | bytes 40
  9.4 10.8 %copy-start.3 = (s32[3,32]{1,0:T(4,128)S(1)}, s32[3,32]{1,0:T(4,128)}, u32[]{:S(2)}) copy-start(s32[3,32]{1,0:T(4,128)} %param.8) | copy-start | bytes 1156
  9.4 49.6 %all-to-all-start = ((f32[32,256,3,16]{1,3,2,0:T(8,128)}), f32[32,256,3,16]{1,3,2,0:T(8,128)S(1)}, u32[]{:S(2)}, u32[]{:S(2)}) async-start(f32[32,256,3,16]{1,3,2,0:T(8,128)} %broadcast_in_dim.6), calls=%async_computation | async-start | bytes 3145728 | tf_op jit(solution)/shard_map/all_to_all | solution.py:11
  20.0 302.2 %all-gather.5.cloned.1.call-start = ((), (), s32[]{:S(2)}) async-start(), calls=%async_computation.4 | async-start | bytes 13369344 | tf_op jit(solution)/shard_map/all_gather | solution.py:26
  369.9 7.7 copy-start.1
  371.3 45.0 %all-to-all-start.2 = ((f32[32,8,3,512]{3,1,2,0:T(8,128)}), f32[32,8,3,512]{3,1,2,0:T(8,128)S(1)}, u32[]{:S(2)}, u32[]{:S(2)}) async-start(f32[32,8,3,512]{3,1,2,0:T(8,128)} %broadcast_in_dim.16), calls=%async_computation.2 | async-start | bytes 3145728 | tf_op jit(solution)/shard_map/all_to_all | solution.py:11
  375.0 286.9 %all-reduce.2.cloned.1.call-start = ((), (), s32[]{:S(2)}) async-start(), calls=%async_computation.3 | async-start | bytes 6291456 | tf_op jit(solution)/shard_map/psum | solution.py:67
  382.0 542.8 %all-gather.7.cloned.1.call-start = ((), (), s32[]{:S(2)}) async-start(), calls=%async_computation.5 | async-start | bytes 13369344 | tf_op jit(solution)/shard_map/all_gather | solution.py:26
  416.4 245.5 %copy-start.2 = (f32[3,32,512]{2,1,0:T(8,128)S(1)}, f32[3,32,512]{2,1,0:T(8,128)}, u32[]{:S(2)}) copy-start(f32[3,32,512]{2,1,0:T(8,128)} %param.7) | copy-start | bytes 589828
Sparse Core Ops, SparseCore 0:
  60.7 261.4 all-gather.4
  382.1 279.8 all-reduce.1
  665.1 259.5 all-gather.6
where the time goes:
time: 934 us; the launch traced here: 933 us
  waiting for transfers between devices  840 us (90%)
  blocking collectives  44.9 us (5%)
  starting transfers between devices  14.5 us (2%)
  between operations  13.9 us (1%)
  local copies, waits for them, and re-layouts  9.72 us (1%)
    all_gather x2, waiting for transfers between devices, picked_2(): lax.all_gather(shard, axis)  523 us
    psum x1, waiting for transfers between devices, shards(): diag_total = lax.psum(term, ('row', 'col'))  245 us
    all_to_all x2, waiting for transfers between devices, copy_for_each(): return lax.all_to_all(copies, axis, split_axis=0, concat_axis=0, tiled=True)  72.8 us
    all_to_all x1, blocking collectives, sum_at_owner(): lax.all_to_all(in_blocks(shard, dim, length), axis, 0, 0, tiled=True)  44.9 us
  transfers between devices with their start and end apart: 5, of which 5 were waited for; matrix products, arithmetic and copies ran while one was open for 1% of the time, Pallas kernels for 0%

commit v1 on v0

v1 whole, which is shorter than its diff:
```python
import jax
import jax.numpy as jnp
from jax import lax
from jax.sharding import Mesh, PartitionSpec as P

TILE = 128
ROW = ("z", "yh")
COL = ("x", "yl", "core")
HIGHEST = lax.Precision.HIGHEST


def tile_masks(row_blocks, list_len, ntiles):
    tiles = jnp.arange(ntiles, dtype=jnp.int32)
    valid = jnp.arange(row_blocks.shape[1], dtype=jnp.int32)[None, :] < list_len[:, None]
    hit = (row_blocks[:, :, None] == tiles[None, None, :]) & valid[:, :, None]
    return jnp.any(hit, axis=1).astype(jnp.float32)


def exchange(blocks, axes):
    return lax.all_to_all(blocks, axes, split_axis=0, concat_axis=0, tiled=True)


def copies(shard, axes):
    count = lax.axis_size(axes)
    return exchange(jnp.broadcast_to(shard, (count, *shard.shape)), axes)


def shards(ainv, lpanel, kk_inverse, row_blocks, list_len):
    nx, nyl, nrows = lax.axis_size("x"), lax.axis_size("yl"), lax.axis_size(ROW)
    ncore = 2
    nchips = nx * nyl
    groups = nx * ncore
    rows, sibs, width = lpanel.shape
    cols = ainv.shape[1]
    part = cols // nx
    wide = sibs * width
    row_index = lax.axis_index(ROW)
    core = lax.axis_index("core")

    tile_mask = tile_masks(row_blocks, list_len, rows * nrows // TILE)
    picked = lax.dynamic_slice_in_dim(tile_mask, row_index * (rows // TILE), rows // TILE, 1)
    own_mask = jnp.repeat(picked, TILE, axis=1)
    panel_t = jnp.transpose(lpanel, (1, 2, 0)) * own_mask[:, None, :]
    panel_t = panel_t.reshape(wide, rows)

    pieces = panel_t.reshape(wide, ncore, nx, part).transpose(2, 1, 3, 0)
    mine = exchange(pieces.reshape(groups, part, wide), ("x", "core"))
    mine = mine.transpose(1, 0, 2).reshape(part, groups * wide)
    factor = copies(mine, ROW).reshape(nrows * part, groups * wide)

    ainv_t = ainv.T.reshape(nx, 1, part, rows)
    ainv_t = jnp.broadcast_to(ainv_t, (nx, nyl, part, rows)).reshape(nchips, part, rows)
    ainv_t = exchange(ainv_t, ("x", "yl")).reshape(nchips * part, rows)

    panel_all = copies(panel_t, ("x", "yl")).reshape(nchips, sibs, width, rows)

    product = lax.dot_general(factor, ainv_t, (((0,), (0,)), ((), ())), precision=HIGHEST)
    product = exchange(product.reshape(groups, wide, rows), ("x", "core"))
    inv_t = jnp.sum(product, axis=0).reshape(sibs, width, rows) * -own_mask[:, None, :]

    other = lax.ppermute(inv_t, "core", [(0, 1), (1, 0)])
    both = jnp.where(core == 0, jnp.stack([inv_t, other], 1), jnp.stack([other, inv_t], 1))
    both = both.reshape(sibs, ncore * width, rows)

    term = jnp.einsum("rsvi,swi->rsvw", panel_all, both, precision=HIGHEST)
    diag = jnp.sum(exchange(term, ROW), axis=0)
    diag = copies(diag, COL).reshape(nchips, ncore, sibs, width, ncore * width)
    ainv_kk = kk_inverse - diag.transpose(2, 1, 3, 0, 4).reshape(kk_inverse.shape)

    half = lax.dynamic_slice_in_dim(both, core * cols, cols, 2)
    swap = [
        (r * nchips * ncore + 2 * q + h, q * nchips * ncore + 2 * r + h)
        for r in range(nrows)
        for q in range(nchips)
        for h in range(ncore)
    ]
    ainv_ki = lax.ppermute(half, ROW + COL, swap)

    share = rows // (nchips * ncore)
    split = both.reshape(sibs, ncore * width, nchips, ncore, share)
    split = lax.dynamic_index_in_dim(split, core, 3, keepdims=False)
    split = exchange(split.transpose(2, 3, 0, 1), ("x", "yl"))
    ainv_ik = split.transpose(1, 2, 0, 3).reshape(share, sibs, -1)
    return ainv_ik, ainv_kk, ainv_ki


def solution(mesh):
    devices = mesh.devices.reshape(8, 2, 4, 4, 2)
    fine = Mesh(devices, ROW + COL)
    placed = (P(ROW, COL), P(ROW, None, COL), P(None, ROW, None), P(), P())
    return jax.shard_map(
        shards,
        mesh=fine,
        in_specs=placed,
        out_specs=(P(ROW + COL, None, None), P(None, ROW, None), P(None, ROW, COL)),
        check_vma=False,
    )
```

time: 934 us -> 182 us (0.19)
  the two profiles are of different devices: /device:TPU:1 before, /device:TPU:12 now
where the time goes in v1:
time: 182 us; the launch traced here: 181 us
  waiting for transfers between devices  89.7 us (49%)
  starting transfers between devices  52.8 us (29%)
  blocking collectives  18.5 us (10%)
  local copies, waits for them, and re-layouts  11.5 us (6%)
  other arithmetic  5.77 us (3%)
    all_to_all x6, waiting for transfers between devices, exchange(): return lax.all_to_all(blocks, axes, split_axis=0, concat_axis=0, tiled=True)  74.3 us
    all_to_all x6, starting transfers between devices, exchange(): return lax.all_to_all(blocks, axes, split_axis=0, concat_axis=0, tiled=True)  48.9 us
    all_to_all x2, blocking collectives, exchange(): return lax.all_to_all(blocks, axes, split_axis=0, concat_axis=0, tiled=True)  18.5 us
    ppermute x1, waiting for transfers between devices, shards(): ainv_ki = lax.ppermute(half, ROW + COL, swap)  14.2 us
    unnamed x19, local copies, waits for them, and re-layouts  4.78 us
  transfers between devices with their start and end apart: 8, of which 7 were waited for; matrix products, arithmetic and copies ran while one was open for 3% of the time, Pallas kernels for 0%

profile of v1, /device:TPU:12, one launch (start us, length us, event | category | flops | bytes accessed | tf_op | source)
XLA Modules:
  0.0 180.7 jit_solution(13074276564782903014)
XLA Ops:
  0.6 0.0 copy-start.2
  0.6 0.7 iota_compare_fusion.1
  1.4 0.8 fusion.2
  2.2 0.1 constant_dynamic-slice_fusion.1
  2.3 0.1 broadcast_bitcast_fusion
  2.3 0.0 copy-done.2
  2.3 0.1 reshape_reshape.4
  2.5 0.1 copy.42
  2.6 0.2 reshape.108
  2.8 7.6 %all_to_all.40 = f32[8,1,1536]{2,1,0:T(1,128)S(1)} all-to-all(f32[8,1,1536]{2,1,0:T(1,128)S(1)} %reshape.108), channel_id=1, replica_groups=mesh['z'=8,'yh'=2,'x'=4,'yl'=4,'core'=2] {'x','core'}, dimensions={0} | all-to-all | bytes 98304 | tf_op jit(solution)/shard_map/all_to_all | solution.py:20
  10.4 0.6 broadcast.28
  11.0 0.7 reduce
  11.8 0.1 reshape.109
  11.9 0.1 copy.43
  11.9 0.1 reshape.95
  12.0 1.0 broadcast_in_dim.25
  13.0 0.0 copy-start.1
  13.0 14.9 %all-to-all-start.1 = ((f32[16,32,384]{2,1,0:T(8,128)}), f32[16,32,384]{2,1,0:T(8,128)S(1)}, u32[]{:S(2)}, u32[]{:S(2)}) async-start(f32[16,32,384]{2,1,0:T(8,128)} %broadcast_in_dim.25), calls=%async_computation.1 | async-start | bytes 1572864 | tf_op jit(solution)/shard_map/all_to_all | solution.py:20
  27.9 0.0 copy-done.1
  27.9 0.1 copy.45
  28.0 33.2 %all-to-all-done.1 = f32[16,32,384]{2,1,0:T(8,128)S(1)} async-done(((f32[16,32,384]{2,1,0:T(8,128)}), f32[16,32,384]{2,1,0:T(8,128)S(1)}, u32[]{:S(2)}, u32[]{:S(2)}) %all-to-all-start.1) | async-done | bytes 786464 | tf_op jit(solution)/shard_map/all_to_all | solution.py:20
  61.3 0.8 broadcast_in_dim.27
  62.1 5.8 %all-to-all-start.2 = ((f32[16,32,256]{2,1,0:T(8,128)}), f32[16,32,256]{2,1,0:T(8,128)S(1)}, u32[]{:S(2)}, u32[]{:S(2)}) async-start(f32[16,32,256]{2,1,0:T(8,128)} %bitcast.9), calls=%async_computation.2 | async-start | bytes 1048576 | tf_op jit(solution)/shard_map/all_to_all | solution.py:20
  67.9 0.3 copy.44
  68.2 11.9 %all-to-all-done.2 = f32[16,32,256]{2,1,0:T(8,128)S(1)} async-done(((f32[16,32,256]{2,1,0:T(8,128)}), f32[16,32,256]{2,1,0:T(8,128)S(1)}, u32[]{:S(2)}, u32[]{:S(2)}) %all-to-all-start.2) | async-done | bytes 524320 | tf_op jit(solution)/shard_map/all_to_all | solution.py:20
  80.1 0.8 fusion.4
  80.9 10.8 %all_to_all.41 = f32[8,48,256]{2,1,0:T(8,128)S(1)} all-to-all(f32[8,48,256]{2,1,0:T(8,128)S(1)} %fusion.4), channel_id=1, replica_groups=mesh['z'=8,'yh'=2,'x'=4,'yl'=4,'core'=2] {'x','core'}, dimensions={0} | all-to-all | bytes 786432 | tf_op jit(solution)/shard_map/all_to_all | solution.py:20
  91.7 1.0 broadcast_in_dim.28
  92.6 7.6 %all-to-all-start.5 = ((f32[16,48,256]{2,1,0:T(8,128)}), f32[16,48,256]{2,1,0:T(8,128)S(1)}, u32[]{:S(2)}, u32[]{:S(2)}) async-start(f32[16,48,256]{2,1,0:T(8,128)} %broadcast_in_dim.28), calls=%async_computation.5 | async-start | bytes 1572864 | tf_op jit(solution)/shard_map/all_to_all | solution.py:20
  100.3 1.9 %collective-permute-start = (f32[3,16,256]{2,1,0:T(8,128)S(1)}, f32[3,16,256]{2,1,0:T(8,128)S(1)}, u32[]{:S(2)}, u32[]{:S(2)}) collective-permute-start(f32[3,16,256]{2,1,0:T(8,128)S(1)} %broadcast_multiply_fusion), channel_id=1, source_target_pairs={{0,1},{1,0},{2,3},{3,2},{4,5},{5,4},{6,7},{7,6},{8,9},{9,8},{10,11... | collective-permute-start | bytes 147464 | tf_op jit(solution)/shard_map/ppermute | solution.py:61
  102.2 1.2 collective-permute-done
  103.4 15.1 %all-to-all-done.5 = f32[16,48,256]{2,1,0:T(8,128)S(1)} async-done(((f32[16,48,256]{2,1,0:T(8,128)}), f32[16,48,256]{2,1,0:T(8,128)S(1)}, u32[]{:S(2)}, u32[]{:S(2)}) %all-to-all-start.5) | async-done | bytes 786464 | tf_op jit(solution)/shard_map/all_to_all | solution.py:20
  118.6 0.8 convolution_bitcast_fusion
  119.4 0.8 reshape.112
  120.2 6.4 %all-to-all-start.6 = ((f32[16,1,1536]{2,1,0:T(1,128)}), f32[16,1,1536]{2,1,0:T(1,128)S(1)}, u32[]{:S(2)}, u32[]{:S(2)}) async-start(f32[16,1,1536]{2,1,0:T(1,128)} %reshape.112), calls=%async_computation.6 | async-start | bytes 196608 | tf_op jit(solution)/shard_map/all_to_all | solution.py:20
  126.6 0.5 copy.46
  127.1 0.4 select_n.29
  127.6 0.8 reshape.110
  128.4 11.5 %all-to-all-done.6 = f32[16,1,1536]{2,1,0:T(1,128)S(1)} async-done(((f32[16,1,1536]{2,1,0:T(1,128)}), f32[16,1,1536]{2,1,0:T(1,128)S(1)}, u32[]{:S(2)}, u32[]{:S(2)}) %all-to-all-start.6) | async-done | bytes 98336 | tf_op jit(solution)/shard_map/all_to_all | solution.py:20
  139.8 7.0 %all-to-all-start.4 = ((f32[16,1,768]{2,1,0:T(1,128)}), f32[16,1,768]{2,1,0:T(1,128)S(1)}, u32[]{:S(2)}, u32[]{:S(2)}) async-start(f32[16,1,768]{2,1,0:T(1,128)} %reshape.110), calls=%async_computation.4 | async-start | bytes 98304 | tf_op jit(solution)/shard_map/all_to_all | solution.py:20
  146.9 0.9 reduce.2
  147.8 0.1 reshape.113
  148.0 0.1 broadcast_in_dim.29
  148.0 1.0 reshape.114
  149.0 2.7 %all-to-all-done.4 = f32[16,1,768]{2,1,0:T(1,128)S(1)} async-done(((f32[16,1,768]{2,1,0:T(1,128)}), f32[16,1,768]{2,1,0:T(1,128)S(1)}, u32[]{:S(2)}, u32[]{:S(2)}) %all-to-all-start.4) | async-done | bytes 49184 | tf_op jit(solution)/shard_map/all_to_all | solution.py:20
  151.7 7.0 %all-to-all-start.7 = ((f32[32,1,1536]{2,1,0:T(1,128)}), f32[32,1,1536]{2,1,0:T(1,128)S(1)}, u32[]{:S(2)}, u32[]{:S(2)}) async-start(f32[32,1,1536]{2,1,0:T(1,128)} %reshape.114), calls=%async_computation.7 | async-start | bytes 393216 | tf_op jit(solution)/shard_map/all_to_all | solution.py:20
  158.7 2.0 %collective-permute-start.1 = (f32[3,32,128]{2,1,0:T(8,128)S(1)}, f32[3,32,128]{2,1,0:T(8,128)S(1)}, u32[]{:S(2)}, u32[]{:S(2)}) collective-permute-start(f32[3,32,128]{2,1,0:T(8,128)S(1)} %constant_dynamic-slice_fusion), channel_id=1, source_target_pairs={{0,0},{1,1},{2,32},{3,33},{4,64},{5,65},{6,96},{7,97},{8,128},{9,1... | collective-permute-start | bytes 147464 | tf_op jit(solution)/shard_map/ppermute | solution.py:77
  160.8 14.2 %collective-permute-done.1 = f32[3,32,128]{2,1,0:T(8,128)S(1)} collective-permute-done((f32[3,32,128]{2,1,0:T(8,128)S(1)}, f32[3,32,128]{2,1,0:T(8,128)S(1)}, u32[]{:S(2)}, u32[]{:S(2)}) %collective-permute-start.1) | collective-permute-done | bytes 49184 | tf_op jit(solution)/shard_map/ppermute | solution.py:77
  174.9 0.7 reduce.1
  175.7 0.1 reshape.111
  175.9 0.7 reshape.101
  176.6 0.0 all-to-all-done.7
  176.6 1.1 reduce.3
  177.7 0.2 reshape.115
  177.9 0.5 copy.52
  178.4 0.0 copy-start
  178.4 0.3 reshape.105
  178.7 0.6 copy-done
  179.3 0.7 sub.3
  180.0 0.6 copy.63
  (15 shorter events, 0.2 us)
Async XLA Ops:
  0.6 1.7 copy-start.2
  13.0 14.9 %copy-start.1 = (f32[256,128]{1,0:T(8,128)S(1)}, f32[256,128]{1,0:T(8,128)}, u32[]{:S(2)}) copy-start(f32[256,128]{1,0:T(8,128)} %param.5) | copy-start | bytes 393220
  13.0 48.2 %all-to-all-start.1 = ((f32[16,32,384]{2,1,0:T(8,128)}), f32[16,32,384]{2,1,0:T(8,128)S(1)}, u32[]{:S(2)}, u32[]{:S(2)}) async-start(f32[16,32,384]{2,1,0:T(8,128)} %broadcast_in_dim.25), calls=%async_computation.1 | async-start | bytes 1572864 | tf_op jit(solution)/shard_map/all_to_all | solution.py:20
  62.1 18.0 %all-to-all-start.2 = ((f32[16,32,256]{2,1,0:T(8,128)}), f32[16,32,256]{2,1,0:T(8,128)S(1)}, u32[]{:S(2)}, u32[]{:S(2)}) async-start(f32[16,32,256]{2,1,0:T(8,128)} %bitcast.9), calls=%async_computation.2 | async-start | bytes 1048576 | tf_op jit(solution)/shard_map/all_to_all | solution.py:20
  92.6 25.9 %all-to-all-start.5 = ((f32[16,48,256]{2,1,0:T(8,128)}), f32[16,48,256]{2,1,0:T(8,128)S(1)}, u32[]{:S(2)}, u32[]{:S(2)}) async-start(f32[16,48,256]{2,1,0:T(8,128)} %broadcast_in_dim.28), calls=%async_computation.5 | async-start | bytes 1572864 | tf_op jit(solution)/shard_map/all_to_all | solution.py:20
  100.3 3.1 %collective-permute-start = (f32[3,16,256]{2,1,0:T(8,128)S(1)}, f32[3,16,256]{2,1,0:T(8,128)S(1)}, u32[]{:S(2)}, u32[]{:S(2)}) collective-permute-start(f32[3,16,256]{2,1,0:T(8,128)S(1)} %broadcast_multiply_fusion), channel_id=1, source_target_pairs={{0,1},{1,0},{2,3},{3,2},{4,5},{5,4},{6,7},{7,6},{8,9},{9,8},{10,11... | collective-permute-start | bytes 147464 | tf_op jit(solution)/shard_map/ppermute | solution.py:61
  120.2 19.6 %all-to-all-start.6 = ((f32[16,1,1536]{2,1,0:T(1,128)}), f32[16,1,1536]{2,1,0:T(1,128)S(1)}, u32[]{:S(2)}, u32[]{:S(2)}) async-start(f32[16,1,1536]{2,1,0:T(1,128)} %reshape.112), calls=%async_computation.6 | async-start | bytes 196608 | tf_op jit(solution)/shard_map/all_to_all | solution.py:20
  139.8 11.9 %all-to-all-start.4 = ((f32[16,1,768]{2,1,0:T(1,128)}), f32[16,1,768]{2,1,0:T(1,128)S(1)}, u32[]{:S(2)}, u32[]{:S(2)}) async-start(f32[16,1,768]{2,1,0:T(1,128)} %reshape.110), calls=%async_computation.4 | async-start | bytes 98304 | tf_op jit(solution)/shard_map/all_to_all | solution.py:20
  151.7 24.9 %all-to-all-start.7 = ((f32[32,1,1536]{2,1,0:T(1,128)}), f32[32,1,1536]{2,1,0:T(1,128)S(1)}, u32[]{:S(2)}, u32[]{:S(2)}) async-start(f32[32,1,1536]{2,1,0:T(1,128)} %reshape.114), calls=%async_computation.7 | async-start | bytes 393216 | tf_op jit(solution)/shard_map/all_to_all | solution.py:20
  158.7 16.2 %collective-permute-start.1 = (f32[3,32,128]{2,1,0:T(8,128)S(1)}, f32[3,32,128]{2,1,0:T(8,128)S(1)}, u32[]{:S(2)}, u32[]{:S(2)}) collective-permute-start(f32[3,32,128]{2,1,0:T(8,128)S(1)} %constant_dynamic-slice_fusion), channel_id=1, source_target_pairs={{0,0},{1,1},{2,32},{3,33},{4,64},{5,65},{6,96},{7,97},{8,128},{9,1... | collective-permute-start | bytes 147464 | tf_op jit(solution)/shard_map/ppermute | solution.py:77
  178.4 0.9 copy-start

commit v2 on v1

v2 whole, which is shorter than its diff:
```python
import jax
import jax.numpy as jnp
from jax import lax
from jax.sharding import Mesh, PartitionSpec as P

TILE = 128
NCORE = 2
ROW = ("zh", "zl", "yh")
COL = ("x", "yl", "core")
HIGHEST = lax.Precision.HIGHEST


def tile_masks(row_blocks, list_len, ntiles):
    tiles = jnp.arange(ntiles, dtype=jnp.int32)
    valid = jnp.arange(row_blocks.shape[1], dtype=jnp.int32)[None, :] < list_len[:, None]
    hit = (row_blocks[:, :, None] == tiles[None, None, :]) & valid[:, :, None]
    return jnp.any(hit, axis=1).astype(jnp.float32)


def exchange(blocks, axes):
    return lax.all_to_all(blocks, axes, split_axis=0, concat_axis=0, tiled=True)


def copies(shard, axes):
    count = lax.axis_size(axes)
    return exchange(jnp.broadcast_to(shard, (count, *shard.shape)), axes)


def with_partner(block, core, dim):
    other = lax.ppermute(block, "core", [(0, 1), (1, 0)])
    first = jnp.where(core == 0, block, other)
    second = jnp.where(core == 0, other, block)
    return jnp.stack([first, second], dim)


def digit_swap():
    zh, zl, yh, x, yl = (lax.axis_size(a) for a in ("zh", "zl", "yh", "x", "yl"))
    pairs = []
    for a in range(zh):
        for b in range(zl * yh):
            for c in range(x):
                for d in range(yl * NCORE):
                    source = ((a * zl * yh + b) * x + c) * yl * NCORE + d
                    target = ((c * zl * yh + b) * x + a) * yl * NCORE + d
                    pairs.append((source, target))
    return pairs


def transposed(nrows):
    return [
        ((r * nrows + q) * NCORE + h, (q * nrows + r) * NCORE + h)
        for r in range(nrows)
        for q in range(nrows)
        for h in range(NCORE)
    ]


def shards(ainv, lpanel, kk_inverse, row_blocks, list_len):
    nx, nyl, nrows = lax.axis_size("x"), lax.axis_size("yl"), lax.axis_size(ROW)
    nchips = nx * nyl
    groups = nx * NCORE
    rows, sibs, width = lpanel.shape
    cols = ainv.shape[1]
    wide = sibs * width
    row_index = lax.axis_index(ROW)
    core = lax.axis_index("core")
    yl = lax.axis_index("yl")

    tile_mask = tile_masks(row_blocks, list_len, rows * nrows // TILE)
    picked = lax.dynamic_slice_in_dim(tile_mask, row_index * (rows // TILE), rows // TILE, 1)
    own_mask = jnp.repeat(picked, TILE, axis=1)
    panel_t = jnp.transpose(lpanel, (1, 2, 0)) * own_mask[:, None, :]
    panel_t = panel_t.reshape(wide, rows)

    panel_all = copies(panel_t, ("x", "yl")).reshape(nchips, sibs, width, rows)

    low, high = panel_t[:, :cols], panel_t[:, cols:]
    keep = jnp.where(core == 0, low, high)
    give = jnp.where(core == 0, high, low)
    got = lax.ppermute(give, "core", [(0, 1), (1, 0)])
    pair = jnp.stack([jnp.where(core == 0, keep, got), jnp.where(core == 0, got, keep)])
    pair = lax.ppermute(pair.reshape(NCORE * wide, cols), ROW + COL, digit_swap())
    pair, panel_all = lax.optimization_barrier((pair, panel_all))
    factor = copies(pair, ROW).reshape(nx, nyl, NCORE * wide, cols)

    product = 0.0
    for step in range(nyl):
        block = ainv
        if step > 0:
            block = lax.ppermute(ainv, "yl", [(i, i ^ step) for i in range(nyl)])
        part = lax.dynamic_index_in_dim(factor, yl ^ step, 1, keepdims=False)
        part = part.reshape(nx * NCORE * wide, cols)
        product += lax.dot_general(part, block, (((1,), (1,)), ((), ())), precision=HIGHEST)

    product = exchange(product.reshape(groups, wide, rows), ("x", "core"))
    inv_t = jnp.sum(product, axis=0).reshape(sibs, width, rows) * -own_mask[:, None, :]
    both = with_partner(inv_t, core, 1).reshape(sibs, NCORE * width, rows)

    half = lax.dynamic_slice_in_dim(both, core * cols, cols, 2)
    ainv_ki = lax.ppermute(half, ROW + COL, transposed(nrows))

    term = jnp.einsum("rsvi,swi->rsvw", panel_all, both, precision=HIGHEST)
    diag = jnp.sum(exchange(term.reshape(nrows, -1), ROW), axis=0)

    diag, ainv_ki = lax.optimization_barrier((diag, ainv_ki))

    ncols = nchips * NCORE
    share = rows // ncols
    split = inv_t.reshape(wide, ncols, share).transpose(1, 0, 2).reshape(ncols, wide * share)
    joined = jnp.concatenate([jnp.broadcast_to(diag, (ncols, diag.size)), split], 1)
    joined = exchange(joined, COL)
    diag = joined[:, : diag.size].reshape(nchips, NCORE, sibs, width, NCORE * width)
    ainv_kk = kk_inverse - diag.transpose(2, 1, 3, 0, 4).reshape(kk_inverse.shape)
    split = joined[:, diag.size // ncols :].reshape(ncols, sibs, width, share)
    ainv_ik = split.transpose(3, 1, 0, 2).reshape(share, sibs, -1)
    return ainv_ik, ainv_kk, ainv_ki


def solution(mesh):
    devices = mesh.devices.reshape(4, 2, 2, 4, 4, 2)
    fine = Mesh(devices, ROW + COL)
    placed = (P(ROW, COL), P(ROW, None, COL), P(None, ROW, None), P(), P())
    return jax.shard_map(
        shards,
        mesh=fine,
        in_specs=placed,
        out_specs=(P(ROW + COL, None, None), P(None, ROW, None), P(None, ROW, COL)),
        check_vma=False,
    )
```

time: 182 us -> 142 us (0.78)
  the two profiles are of different devices: /device:TPU:12 before, /device:TPU:1 now
where the time goes in v2:
time: 142 us; the launch traced here: 141 us
  waiting for transfers between devices  64.5 us (45%)
  starting transfers between devices  61.3 us (43%)
  local copies, waits for them, and re-layouts  9.49 us (7%)
  matrix products  3.45 us (2%)
    all_to_all x5, waiting for transfers between devices, exchange(): return lax.all_to_all(blocks, axes, split_axis=0, concat_axis=0, tiled=True)  54.7 us
    all_to_all x5, starting transfers between devices, exchange(): return lax.all_to_all(blocks, axes, split_axis=0, concat_axis=0, tiled=True)  43.2 us
    ppermute x3, starting transfers between devices, shards(): block = lax.ppermute(ainv, 'yl', [(i, i ^ step) for i in range(nyl)])  9.27 us
    ppermute x3, waiting for transfers between devices, shards(): block = lax.ppermute(ainv, 'yl', [(i, i ^ step) for i in range(nyl)])  8.91 us
    ppermute x1, starting transfers between devices, shards(): got = lax.ppermute(give, 'core', [(0, 1), (1, 0)])  4.38 us
    ppermute x1, starting transfers between devices, with_partner(): other = lax.ppermute(block, 'core', [(0, 1), (1, 0)])  3.12 us
  transfers between devices with their start and end apart: 12, of which 9 were waited for; matrix products, arithmetic and copies ran while one was open for 2% of the time, Pallas kernels for 0%

profile of v2, /device:TPU:1, one launch (start us, length us, event | category | flops | bytes accessed | tf_op | source)
XLA Modules:
  0.0 140.8 jit_solution(533938311187294605)
XLA Ops:
  0.6 0.0 copy-start.4
  0.6 0.0 copy-start.3
  0.7 0.0 copy-start.2
  0.7 0.6 copy-done.4
  1.3 0.1 iota_compare_fusion.1
  1.4 0.0 copy-done.3
  1.4 0.1 fusion.4
  1.5 0.1 constant_dynamic-slice_fusion.5
  1.6 0.1 broadcast_bitcast_fusion
  1.6 0.0 copy-done.2
  1.7 1.0 broadcast_in_dim.18
  2.6 8.0 %all-to-all-start = ((f32[16,48,256]{2,1,0:T(8,128)}), f32[16,48,256]{2,1,0:T(8,128)S(1)}, u32[]{:S(2)}, u32[]{:S(2)}) async-start(f32[16,48,256]{2,1,0:T(8,128)} %broadcast_in_dim.18), calls=%async_computation | async-start | bytes 1572864 | tf_op jit(solution)/shard_map/all_to_all | solution.py:21
  10.6 4.4 %collective-permute-start = (f32[48,128]{1,0:T(8,128)S(1)}, f32[48,128]{1,0:T(8,128)S(1)}, u32[]{:S(2)}, u32[]{:S(2)}) collective-permute-start(f32[48,128]{1,0:T(8,128)S(1)} %slice_select_fusion), channel_id=1, source_target_pairs={{0,1},{1,0},{2,3},{3,2},{4,5},{5,4},{6,7},{7,6},{8,9},{9,8},{10,11... | collective-permute-start | bytes 73736 | tf_op jit(solution)/shard_map/ppermute | solution.py:80
  15.0 0.8 collective-permute-done
  15.9 0.7 collective-permute-start.1
  16.5 0.0 collective-permute-done.1
  16.6 15.5 %all-to-all-done = f32[16,48,256]{2,1,0:T(8,128)S(1)} async-done(((f32[16,48,256]{2,1,0:T(8,128)}), f32[16,48,256]{2,1,0:T(8,128)S(1)}, u32[]{:S(2)}, u32[]{:S(2)}) %all-to-all-start) | async-done | bytes 786464 | tf_op jit(solution)/shard_map/all_to_all | solution.py:21
  32.1 1.0 broadcast_in_dim.19
  33.0 12.8 %all-to-all-start.1 = ((f32[16,96,128]{2,1,0:T(8,128)}), f32[16,96,128]{2,1,0:T(8,128)S(1)}, u32[]{:S(2)}, u32[]{:S(2)}) async-start(f32[16,96,128]{2,1,0:T(8,128)} %broadcast_in_dim.19), calls=%async_computation.1 | async-start | bytes 1572864 | tf_op jit(solution)/shard_map/all_to_all | solution.py:21
  45.9 0.0 copy-done.1
  45.9 1.9 %collective-permute-start.4 = (f32[256,128]{1,0:T(8,128)S(1)}, f32[256,128]{1,0:T(8,128)S(1)}, u32[]{:S(2)}, u32[]{:S(2)}) collective-permute-start(f32[256,128]{1,0:T(8,128)S(1)} %copy-done.1), channel_id=1, source_target_pairs={{0,6},{2,4},{4,2},{6,0},{1,7},{3,5},{5,3},{7,1},{8,14},{10,12},{12... | collective-permute-start | bytes 393224 | tf_op jit(solution)/shard_map/ppermute | solution.py:90
  47.8 1.9 %collective-permute-start.2 = (f32[256,128]{1,0:T(8,128)S(1)}, f32[256,128]{1,0:T(8,128)S(1)}, u32[]{:S(2)}, u32[]{:S(2)}) collective-permute-start(f32[256,128]{1,0:T(8,128)S(1)} %copy-done.1), channel_id=1, source_target_pairs={{0,2},{2,0},{4,6},{6,4},{1,3},{3,1},{5,7},{7,5},{8,10},{10,8},{12,... | collective-permute-start | bytes 393224 | tf_op jit(solution)/shard_map/ppermute | solution.py:90
  49.7 5.4 %collective-permute-start.3 = (f32[256,128]{1,0:T(8,128)S(1)}, f32[256,128]{1,0:T(8,128)S(1)}, u32[]{:S(2)}, u32[]{:S(2)}) collective-permute-start(f32[256,128]{1,0:T(8,128)S(1)} %copy-done.1), channel_id=1, source_target_pairs={{0,4},{2,6},{4,0},{6,2},{1,5},{3,7},{5,1},{7,3},{8,12},{10,14},{12... | collective-permute-start | bytes 393224 | tf_op jit(solution)/shard_map/ppermute | solution.py:90
  55.2 9.6 %all-to-all-done.1 = f32[16,96,128]{2,1,0:T(8,128)S(1)} async-done(((f32[16,96,128]{2,1,0:T(8,128)}), f32[16,96,128]{2,1,0:T(8,128)S(1)}, u32[]{:S(2)}, u32[]{:S(2)}) %all-to-all-start.1) | async-done | bytes 786464 | tf_op jit(solution)/shard_map/all_to_all | solution.py:21
  64.8 0.1 constant_dynamic-slice_fusion.2
  64.9 0.5 fusion.6
  65.4 1.6 %collective-permute-done.2 = f32[256,128]{1,0:T(8,128)S(1)} collective-permute-done((f32[256,128]{1,0:T(8,128)S(1)}, f32[256,128]{1,0:T(8,128)S(1)}, u32[]{:S(2)}, u32[]{:S(2)}) %collective-permute-start.2) | collective-permute-done | bytes 131104 | tf_op jit(solution)/shard_map/ppermute | solution.py:90
  67.0 0.5 convolution_add_fusion.1
  67.5 0.0 collective-permute-done.4
  67.5 0.5 fusion.7
  68.0 7.3 %collective-permute-done.3 = f32[256,128]{1,0:T(8,128)S(1)} collective-permute-done((f32[256,128]{1,0:T(8,128)S(1)}, f32[256,128]{1,0:T(8,128)S(1)}, u32[]{:S(2)}, u32[]{:S(2)}) %collective-permute-start.3) | collective-permute-done | bytes 131104 | tf_op jit(solution)/shard_map/ppermute | solution.py:90
  75.3 1.2 fusion
  76.5 5.0 %all-to-all-start.2 = ((f32[8,48,256]{2,1,0:T(8,128)}), f32[8,48,256]{2,1,0:T(8,128)S(1)}, u32[]{:S(2)}, u32[]{:S(2)}) async-start(f32[8,48,256]{2,1,0:T(8,128)} %bitcast.11), calls=%async_computation.2 | async-start | bytes 786432 | tf_op jit(solution)/shard_map/all_to_all | solution.py:21
  81.5 7.7 %all-to-all-done.2 = f32[8,48,256]{2,1,0:T(8,128)S(1)} async-done(((f32[8,48,256]{2,1,0:T(8,128)}), f32[8,48,256]{2,1,0:T(8,128)S(1)}, u32[]{:S(2)}, u32[]{:S(2)}) %all-to-all-start.2) | async-done | bytes 393248 | tf_op jit(solution)/shard_map/all_to_all | solution.py:21
  89.2 3.1 %collective-permute-start.5 = (f32[3,16,256]{2,1,0:T(8,128)S(1)}, f32[3,16,256]{2,1,0:T(8,128)S(1)}, u32[]{:S(2)}, u32[]{:S(2)}) collective-permute-start(f32[3,16,256]{2,1,0:T(8,128)S(1)} %broadcast_multiply_fusion), channel_id=1, source_target_pairs={{0,1},{1,0},{2,3},{3,2},{4,5},{5,4},{6,7},{7,6},{8,9},{9,8},{10,11... | collective-permute-start | bytes 147464 | tf_op jit(solution)/shard_map/ppermute | solution.py:30
  92.4 0.1 copy.50
  92.5 0.3 mul.41.clone
  92.8 0.2 mul.44
  93.1 0.1 copy.41
  93.2 0.1 collective-permute-done.5
  93.3 0.8 convolution_bitcast_fusion
  94.1 0.8 all_to_all.31
  94.9 9.2 %all-to-all-start.3 = ((f32[16,1,1536]{2,1,0:T(1,128)}), f32[16,1,1536]{2,1,0:T(1,128)S(1)}, u32[]{:S(2)}, u32[]{:S(2)}) async-start(f32[16,1,1536]{2,1,0:T(1,128)} %all_to_all.31), calls=%async_computation.3 | async-start | bytes 196608 | tf_op jit(solution)/shard_map/all_to_all | solution.py:21
  104.2 0.7 collective-permute-start.6
  104.8 0.1 copy.43
  105.0 0.1 copy.44
  105.1 10.9 %all-to-all-done.3 = f32[16,1,1536]{2,1,0:T(1,128)S(1)} async-done(((f32[16,1,1536]{2,1,0:T(1,128)}), f32[16,1,1536]{2,1,0:T(1,128)S(1)}, u32[]{:S(2)}, u32[]{:S(2)}) %all-to-all-start.3) | async-done | bytes 98336 | tf_op jit(solution)/shard_map/all_to_all | solution.py:21
  116.0 0.1 reduce_sum.19
  116.1 0.0 collective-permute-done.6
  116.1 0.9 all_to_all.28
  117.0 8.2 %all-to-all-start.4 = ((f32[32,1,1920]{2,1,0:T(1,128)}), f32[32,1,1920]{2,1,0:T(1,128)S(1)}, u32[]{:S(2)}, u32[]{:S(2)}) async-start(f32[32,1,1920]{2,1,0:T(1,128)} %all_to_all.28), calls=%async_computation.4 | async-start | bytes 491520 | tf_op jit(solution)/shard_map/all_to_all | solution.py:21
  125.2 10.9 %all-to-all-done.4 = f32[32,1,1920]{2,1,0:T(1,128)S(1)} async-done(((f32[32,1,1920]{2,1,0:T(1,128)}), f32[32,1,1920]{2,1,0:T(1,128)S(1)}, u32[]{:S(2)}, u32[]{:S(2)}) %all-to-all-start.4) | async-done | bytes 245792 | tf_op jit(solution)/shard_map/all_to_all | solution.py:21
  136.1 0.3 copy.45
  136.5 0.1 slice.19
  136.5 0.2 copy.46
  136.7 0.8 reshape.113
  137.6 0.2 copy.47
  137.8 0.2 reshape.114
  138.1 0.5 copy.48
  138.5 0.0 copy-start
  138.5 0.3 reshape.115
  138.9 0.6 copy-done
  139.4 0.7 sub.3
  140.2 0.6 copy.59
  (19 shorter events, 0.2 us)
Async XLA Ops:
  0.6 0.7 copy-start.4
  0.6 0.7 copy-start.3
  0.7 1.0 copy-start.2
  2.6 29.4 %all-to-all-start = ((f32[16,48,256]{2,1,0:T(8,128)}), f32[16,48,256]{2,1,0:T(8,128)S(1)}, u32[]{:S(2)}, u32[]{:S(2)}) async-start(f32[16,48,256]{2,1,0:T(8,128)} %broadcast_in_dim.18), calls=%async_computation | async-start | bytes 1572864 | tf_op jit(solution)/shard_map/all_to_all | solution.py:21
  10.6 5.2 %collective-permute-start = (f32[48,128]{1,0:T(8,128)S(1)}, f32[48,128]{1,0:T(8,128)S(1)}, u32[]{:S(2)}, u32[]{:S(2)}) collective-permute-start(f32[48,128]{1,0:T(8,128)S(1)} %slice_select_fusion), channel_id=1, source_target_pairs={{0,1},{1,0},{2,3},{3,2},{4,5},{5,4},{6,7},{7,6},{8,9},{9,8},{10,11... | collective-permute-start | bytes 73736 | tf_op jit(solution)/shard_map/ppermute | solution.py:80
  15.9 0.7 collective-permute-start.1
  33.0 12.8 %copy-start.1 = (f32[256,128]{1,0:T(8,128)S(1)}, f32[256,128]{1,0:T(8,128)}, u32[]{:S(2)}) copy-start(f32[256,128]{1,0:T(8,128)} %param.5) | copy-start | bytes 393220
  33.0 31.8 %all-to-all-start.1 = ((f32[16,96,128]{2,1,0:T(8,128)}), f32[16,96,128]{2,1,0:T(8,128)S(1)}, u32[]{:S(2)}, u32[]{:S(2)}) async-start(f32[16,96,128]{2,1,0:T(8,128)} %broadcast_in_dim.19), calls=%async_computation.1 | async-start | bytes 1572864 | tf_op jit(solution)/shard_map/all_to_all | solution.py:21
  45.9 21.6 %collective-permute-start.4 = (f32[256,128]{1,0:T(8,128)S(1)}, f32[256,128]{1,0:T(8,128)S(1)}, u32[]{:S(2)}, u32[]{:S(2)}) collective-permute-start(f32[256,128]{1,0:T(8,128)S(1)} %copy-done.1), channel_id=1, source_target_pairs={{0,6},{2,4},{4,2},{6,0},{1,7},{3,5},{5,3},{7,1},{8,14},{10,12},{12... | collective-permute-start | bytes 393224 | tf_op jit(solution)/shard_map/ppermute | solution.py:90
  47.8 19.2 %collective-permute-start.2 = (f32[256,128]{1,0:T(8,128)S(1)}, f32[256,128]{1,0:T(8,128)S(1)}, u32[]{:S(2)}, u32[]{:S(2)}) collective-permute-start(f32[256,128]{1,0:T(8,128)S(1)} %copy-done.1), channel_id=1, source_target_pairs={{0,2},{2,0},{4,6},{6,4},{1,3},{3,1},{5,7},{7,5},{8,10},{10,8},{12,... | collective-permute-start | bytes 393224 | tf_op jit(solution)/shard_map/ppermute | solution.py:90
  49.7 25.5 %collective-permute-start.3 = (f32[256,128]{1,0:T(8,128)S(1)}, f32[256,128]{1,0:T(8,128)S(1)}, u32[]{:S(2)}, u32[]{:S(2)}) collective-permute-start(f32[256,128]{1,0:T(8,128)S(1)} %copy-done.1), channel_id=1, source_target_pairs={{0,4},{2,6},{4,0},{6,2},{1,5},{3,7},{5,1},{7,3},{8,12},{10,14},{12... | collective-permute-start | bytes 393224 | tf_op jit(solution)/shard_map/ppermute | solution.py:90
  76.5 12.7 %all-to-all-start.2 = ((f32[8,48,256]{2,1,0:T(8,128)}), f32[8,48,256]{2,1,0:T(8,128)S(1)}, u32[]{:S(2)}, u32[]{:S(2)}) async-start(f32[8,48,256]{2,1,0:T(8,128)} %bitcast.11), calls=%async_computation.2 | async-start | bytes 786432 | tf_op jit(solution)/shard_map/all_to_all | solution.py:21
  89.2 4.0 %collective-permute-start.5 = (f32[3,16,256]{2,1,0:T(8,128)S(1)}, f32[3,16,256]{2,1,0:T(8,128)S(1)}, u32[]{:S(2)}, u32[]{:S(2)}) collective-permute-start(f32[3,16,256]{2,1,0:T(8,128)S(1)} %broadcast_multiply_fusion), channel_id=1, source_target_pairs={{0,1},{1,0},{2,3},{3,2},{4,5},{5,4},{6,7},{7,6},{8,9},{9,8},{10,11... | collective-permute-start | bytes 147464 | tf_op jit(solution)/shard_map/ppermute | solution.py:30
  94.9 21.1 %all-to-all-start.3 = ((f32[16,1,1536]{2,1,0:T(1,128)}), f32[16,1,1536]{2,1,0:T(1,128)S(1)}, u32[]{:S(2)}, u32[]{:S(2)}) async-start(f32[16,1,1536]{2,1,0:T(1,128)} %all_to_all.31), calls=%async_computation.3 | async-start | bytes 196608 | tf_op jit(solution)/shard_map/all_to_all | solution.py:21
  104.2 11.9 %collective-permute-start.6 = (f32[3,32,128]{2,1,0:T(8,128)S(1)}, f32[3,32,128]{2,1,0:T(8,128)S(1)}, u32[]{:S(2)}, u32[]{:S(2)}) collective-permute-start(f32[3,32,128]{2,1,0:T(8,128)S(1)} %constant_dynamic-slice_fusion), channel_id=1, source_target_pairs={{0,0},{1,1},{2,32},{3,33},{4,64},{5,65},{6,96},{7,97},{8,128},{9,1... | collective-permute-start | bytes 147464 | tf_op jit(solution)/shard_map/ppermute | solution.py:100
  117.0 19.1 %all-to-all-start.4 = ((f32[32,1,1920]{2,1,0:T(1,128)}), f32[32,1,1920]{2,1,0:T(1,128)S(1)}, u32[]{:S(2)}, u32[]{:S(2)}) async-start(f32[32,1,1920]{2,1,0:T(1,128)} %all_to_all.28), calls=%async_computation.4 | async-start | bytes 491520 | tf_op jit(solution)/shard_map/all_to_all | solution.py:21
  138.5 0.9 copy-start

commit v3 on v2

v3 whole, which is shorter than its diff:
```python
import jax
import jax.numpy as jnp
from jax import lax
from jax.sharding import Mesh, PartitionSpec as P

TILE = 128
NCORE = 2
ROW = ("zh", "zl", "yh")
COL = ("xh", "xl", "ylh", "yll", "core")
HIGHEST = lax.Precision.HIGHEST


def tile_masks(row_blocks, list_len, ntiles):
    tiles = jnp.arange(ntiles, dtype=jnp.int32)
    valid = jnp.arange(row_blocks.shape[1], dtype=jnp.int32)[None, :] < list_len[:, None]
    hit = (row_blocks[:, :, None] == tiles[None, None, :]) & valid[:, :, None]
    return jnp.any(hit, axis=1).astype(jnp.float32)


def exchange(blocks, axes):
    return lax.all_to_all(blocks, axes, split_axis=0, concat_axis=0, tiled=True)


def copies(shard, axes):
    count = lax.axis_size(axes)
    return exchange(jnp.broadcast_to(shard, (count, *shard.shape)), axes)


def doubled(block, axis, dim):
    other = lax.ppermute(block, axis, [(0, 1), (1, 0)])
    side = lax.axis_index(axis)
    first = jnp.where(side == 0, block, other)
    second = jnp.where(side == 0, other, block)
    return jnp.concatenate([first, second], dim)


def digit_swap():
    zh, zl, yh = (lax.axis_size(a) for a in ROW)
    x, rest = lax.axis_size(COL[:2]), lax.axis_size(COL[2:])
    pairs = []
    for a in range(zh):
        for b in range(zl * yh):
            for c in range(x):
                for d in range(rest):
                    source = ((a * zl * yh + b) * x + c) * rest + d
                    target = ((c * zl * yh + b) * x + a) * rest + d
                    pairs.append((source, target))
    return pairs


def transposed(nrows, flip):
    return [
        ((r * nrows + q) * NCORE + h, (q * nrows + r) * NCORE + (h ^ flip))
        for r in range(nrows)
        for q in range(nrows)
        for h in range(NCORE)
    ]


def shards(ainv, lpanel, kk_inverse, row_blocks, list_len):
    nx, nyl = lax.axis_size(COL[:2]), lax.axis_size(COL[2:4])
    nrows, ncols = lax.axis_size(ROW), lax.axis_size(COL)
    rows, sibs, width = lpanel.shape
    cols = ainv.shape[1]
    wide = sibs * width
    row_index = lax.axis_index(ROW)
    core = lax.axis_index("core")

    tile_mask = tile_masks(row_blocks, list_len, rows * nrows // TILE)
    picked = lax.dynamic_slice_in_dim(tile_mask, row_index * (rows // TILE), rows // TILE, 1)
    own_mask = jnp.repeat(picked, TILE, axis=1)
    panel = jnp.transpose(lpanel, (1, 2, 0)) * own_mask[:, None, :]
    panel = panel.reshape(wide, rows)

    swapped = lax.ppermute(panel, ROW + COL, digit_swap())
    factor = copies(swapped, ROW)
    factor = factor.reshape(nx, 2, 2, wide, NCORE, cols)
    factor = factor.transpose(0, 3, 4, 2, 1, 5).reshape(nx * wide, nyl * rows)

    for axis in ("ylh", "yll", "core"):
        ainv = doubled(ainv, axis, 1)

    panel_all = panel[None]
    for axis in ("xh", "ylh", "xl", "yll", "core"):
        panel_all = doubled(panel_all, axis, 0)
    panel_all = panel_all.reshape(2, 2, 2, 2, NCORE, sibs, width, rows)

    product = lax.dot_general(factor, ainv, (((1,), (1,)), ((), ())), precision=HIGHEST)
    product = exchange(product.reshape(nx, wide, rows), COL[:2])
    inv_t = jnp.sum(product, axis=0).reshape(sibs, width, rows) * -own_mask[:, None, :]

    low, high = inv_t[:, :, :cols], inv_t[:, :, cols:]
    same = lax.ppermute(jnp.where(core == 0, low, high), ROW + COL, transposed(nrows, 0))
    flip = lax.ppermute(jnp.where(core == 0, high, low), ROW + COL, transposed(nrows, 1))
    ainv_ki = [jnp.where(core == 0, same, flip), jnp.where(core == 0, flip, same)]
    ainv_ki = jnp.concatenate(ainv_ki, 1)

    term = jnp.einsum("abcdesvi,swi->ecdbsavw", panel_all, inv_t, precision=HIGHEST)
    diag = jnp.sum(exchange(term.reshape(nrows, -1), ROW), axis=0)
    diag, ainv_ki = lax.optimization_barrier((diag, ainv_ki))

    share = rows // ncols
    split = inv_t.reshape(wide, ncols, share).transpose(1, 0, 2).reshape(ncols, wide * share)
    joined = jnp.concatenate([jnp.broadcast_to(diag, (ncols, diag.size)), split], 1)
    joined = exchange(joined, COL)
    diag = joined[:, : diag.size].reshape(ncols, sibs, -1, width)
    ainv_kk = kk_inverse - diag.transpose(1, 2, 0, 3).reshape(kk_inverse.shape)
    split = joined[:, diag.size // ncols :].reshape(ncols, sibs, width, share)
    ainv_ik = split.transpose(3, 1, 0, 2).reshape(share, sibs, -1)
    return ainv_ik, ainv_kk, ainv_ki


def solution(mesh):
    devices = mesh.devices.reshape(4, 2, 2, 2, 2, 2, 2, 2)
    fine = Mesh(devices, ROW + COL)
    placed = (P(ROW, COL), P(ROW, None, COL), P(None, ROW, None), P(), P())

    return jax.shard_map(
        shards,
        mesh=fine,
        in_specs=placed,
        out_specs=(P(ROW + COL, None, None), P(None, ROW, None), P(None, ROW, COL)),
        check_vma=False,
    )
```

time: 142 us -> 161 us (1.13)
  starting transfers between devices: 61.3 us -> 92.2 us
  waiting for transfers between devices: 64.5 us -> 42.1 us
  other arithmetic: 1.08 us -> 7.95 us
  matrix products: 3.45 us -> 7.45 us
    all_to_all x5 -> x4, waiting for transfers between devices: 54.7 us -> 26.5 us  [exchange(): return lax.all_to_all(blocks, axes, split_axis=0, concat_axis=0, tiled=True)]
    ppermute x7 -> x11, starting transfers between devices: 18.1 us -> 38.3 us  [the longest x8 34.3 us: doubled(): other = lax.ppermute(block, axis, [(0, 1), (1, 0)])]
    all_to_all x5 -> x4, starting transfers between devices: 43.2 us -> 53.9 us  [exchange(): return lax.all_to_all(blocks, axes, split_axis=0, concat_axis=0, tiled=True)]
    ppermute x7 -> x11, waiting for transfers between devices: 9.8 us -> 15.5 us  [the longest x8 15.5 us: doubled(): other = lax.ppermute(block, axis, [(0, 1), (1, 0)])]
    dot_general x5 -> x2, matrix products: 3.45 us -> 7.45 us  [the longest x1 5.58 us: shards(): jnp.einsum('abcdesvi,swi->ecdbsavw', panel_all, inv_t, precision=HIGHEST)]
    select_n x1 -> x10, other arithmetic: 0.01 us -> 3.6 us  [the longest x8 3.58 us: doubled(): first = jnp.where(side == 0, block, other)]
    concatenate x0 -> x8, other arithmetic: none -> 1.82 us  [the longest x7 1.2 us: doubled(): return jnp.concatenate([first, second], dim)]
  transfers between devices with their start and end apart: 12 -> 15, of which waited for: 9 -> 6; matrix products, arithmetic and copies ran while one was open for 2% -> 7% of each run, Pallas kernels for 0% -> 0%
where the time goes in v3:
time: 161 us; the launch traced here: 160 us
  starting transfers between devices  92.2 us (57%)
  waiting for transfers between devices  42.1 us (26%)
  local copies, waits for them, and re-layouts  9.03 us (6%)
  other arithmetic  7.95 us (5%)
  matrix products  7.45 us (5%)
    all_to_all x4, starting transfers between devices, exchange(): return lax.all_to_all(blocks, axes, split_axis=0, concat_axis=0, tiled=True)  53.9 us
    ppermute x8, starting transfers between devices, doubled(): other = lax.ppermute(block, axis, [(0, 1), (1, 0)])  34.3 us
    all_to_all x4, waiting for transfers between devices, exchange(): return lax.all_to_all(blocks, axes, split_axis=0, concat_axis=0, tiled=True)  26.5 us
    ppermute x8, waiting for transfers between devices, doubled(): other = lax.ppermute(block, axis, [(0, 1), (1, 0)])  15.5 us
    dot_general x1, matrix products, shards(): jnp.einsum('abcdesvi,swi->ecdbsavw', panel_all, inv_t, precision=HIGHEST)  5.58 us
    select_n x8, other arithmetic, doubled(): first = jnp.where(side == 0, block, other)  3.58 us
  transfers between devices with their start and end apart: 15, of which 6 were waited for; matrix products, arithmetic and copies ran while one was open for 7% of the time, Pallas kernels for 0%

profile of v3, /device:TPU:1, one launch (start us, length us, event | category | flops | bytes accessed | tf_op | source)
XLA Modules:
  0.0 159.9 jit_solution(916646390448967513)
XLA Ops:
  0.6 0.7 iota_compare_fusion.1
  1.4 0.8 fusion.11
  2.2 0.1 constant_dynamic-slice_fusion
  2.2 0.1 broadcast_bitcast_fusion
  2.3 0.8 bitcast_multiply_fusion.1
  3.1 5.5 %collective-permute-start.4 = (f32[1,48,256]{2,1,0:T(8,128)S(1)}, f32[1,48,256]{2,1,0:T(8,128)S(1)}, u32[]{:S(2)}, u32[]{:S(2)}) collective-permute-start(f32[1,48,256]{2,1,0:T(8,128)S(1)} %bitcast.60), channel_id=1, source_target_pairs={{0,16},{16,0},{1,17},{17,1},{2,18},{18,2},{3,19},{19,3},{4,20},{20... | collective-permute-start | bytes 147464 | tf_op jit(solution)/shard_map/ppermute | solution.py:30
  8.6 1.5 collective-permute-done.4
  10.1 4.4 %collective-permute-start.5 = (f32[2,48,256]{2,1,0:T(8,128)S(1)}, f32[2,48,256]{2,1,0:T(8,128)S(1)}, u32[]{:S(2)}, u32[]{:S(2)}) collective-permute-start(f32[2,48,256]{2,1,0:T(8,128)S(1)} %pad_maximum_fusion.7), channel_id=1, source_target_pairs={{0,4},{4,0},{1,5},{5,1},{2,6},{6,2},{3,7},{7,3},{8,12},{12,8},{9,1... | collective-permute-start | bytes 294920 | tf_op jit(solution)/shard_map/ppermute | solution.py:30
  14.5 0.7 collective-permute-start
  15.2 1.9 %collective-permute-start.1 = (f32[256,128]{1,0:T(8,128)}, f32[256,128]{1,0:T(8,128)S(1)}, u32[]{:S(2)}, u32[]{:S(2)}) collective-permute-start(f32[256,128]{1,0:T(8,128)} %param.5), channel_id=1, source_target_pairs={{0,4},{4,0},{1,5},{5,1},{2,6},{6,2},{3,7},{7,3},{8,12},{12,8},{9,1... | collective-permute-start | bytes 393224 | tf_op jit(solution)/shard_map/ppermute | solution.py:30
  17.1 0.0 copy-start.1
  17.2 1.0 broadcast_in_dim.7
  18.1 22.4 %all-to-all-start = ((f32[16,48,256]{2,1,0:T(8,128)}), f32[16,48,256]{2,1,0:T(8,128)S(1)}, u32[]{:S(2)}, u32[]{:S(2)}) async-start(f32[16,48,256]{2,1,0:T(8,128)} %broadcast_in_dim.7), calls=%async_computation | async-start | bytes 1572864 | tf_op jit(solution)/shard_map/all_to_all | solution.py:21
  40.5 0.0 collective-permute-done.5
  40.6 3.0 %collective-permute-start.6 = (f32[4,48,256]{2,1,0:T(8,128)S(1)}, f32[4,48,256]{2,1,0:T(8,128)S(1)}, u32[]{:S(2)}, u32[]{:S(2)}) collective-permute-start(f32[4,48,256]{2,1,0:T(8,128)S(1)} %pad_maximum_fusion.6), channel_id=1, source_target_pairs={{0,8},{8,0},{1,9},{9,1},{2,10},{10,2},{3,11},{11,3},{4,12},{12,4},... | collective-permute-start | bytes 589832 | tf_op jit(solution)/shard_map/ppermute | solution.py:30
  43.6 2.3 %collective-permute-start.2 = (f32[256,256]{1,0:T(8,128)S(1)}, f32[256,256]{1,0:T(8,128)S(1)}, u32[]{:S(2)}, u32[]{:S(2)}) collective-permute-start(f32[256,256]{1,0:T(8,128)S(1)} %pad_maximum_fusion.4), channel_id=1, source_target_pairs={{0,2},{2,0},{1,3},{3,1},{4,6},{6,4},{5,7},{7,5},{8,10},{10,8},{9,1... | collective-permute-start | bytes 786440 | tf_op jit(solution)/shard_map/ppermute | solution.py:30
  46.0 1.0 collective-permute-done.6
  47.0 2.3 %collective-permute-start.7 = (f32[8,48,256]{2,1,0:T(8,128)S(1)}, f32[8,48,256]{2,1,0:T(8,128)}, u32[]{:S(2)}, u32[]{:S(2)}) collective-permute-start(f32[8,48,256]{2,1,0:T(8,128)S(1)} %pad_maximum_fusion.3), channel_id=1, source_target_pairs={{0,2},{2,0},{1,3},{3,1},{4,6},{6,4},{5,7},{7,5},{8,10},{10,8},{9,1... | collective-permute-start | bytes 1179656 | tf_op jit(solution)/shard_map/ppermute | solution.py:30
  49.4 13.0 %collective-permute-done.2 = f32[256,256]{1,0:T(8,128)S(1)} collective-permute-done((f32[256,256]{1,0:T(8,128)S(1)}, f32[256,256]{1,0:T(8,128)S(1)}, u32[]{:S(2)}, u32[]{:S(2)}) %collective-permute-start.2) | collective-permute-done | bytes 262176 | tf_op jit(solution)/shard_map/ppermute | solution.py:30
  62.5 0.1 pad_maximum_fusion.2
  62.5 10.0 %collective-permute-start.3 = (f32[256,512]{1,0:T(8,128)S(1)}, f32[256,512]{1,0:T(8,128)}, u32[]{:S(2)}, u32[]{:S(2)}) collective-permute-start(f32[256,512]{1,0:T(8,128)S(1)} %pad_maximum_fusion.2), channel_id=1, source_target_pairs={{0,1},{1,0},{2,3},{3,2},{4,5},{5,4},{6,7},{7,6},{8,9},{9,8},{10,11... | collective-permute-start | bytes 1572872 | tf_op jit(solution)/shard_map/ppermute | solution.py:30
  72.5 1.1 broadcast_select_fusion.5
  73.6 1.0 pad_maximum_fusion.1
  74.6 4.8 %collective-permute-start.8 = (f32[16,48,256]{2,1,0:T(8,128)}, f32[16,48,256]{2,1,0:T(8,128)}, u32[]{:S(2)}, u32[]{:S(2)}) collective-permute-start(f32[16,48,256]{2,1,0:T(8,128)} %pad_maximum_fusion.1), channel_id=1, source_target_pairs={{0,1},{1,0},{2,3},{3,2},{4,5},{5,4},{6,7},{7,6},{8,9},{9,8},{10,11... | collective-permute-start | bytes 2359304 | tf_op jit(solution)/shard_map/ppermute | solution.py:30
  79.4 0.1 copy.55
  79.6 0.3 mul.38.clone
  79.9 0.2 mul.40
  80.1 0.0 collective-permute-done.3
  80.1 1.2 broadcast_select_fusion.3
  81.3 0.0 all-to-all-done
  81.3 0.4 reshape.79
  81.7 0.6 copy.41
  82.3 0.6 dot_general.8
  83.0 1.9 %fusion.5 = f32[4,48,256]{2,1,0:T(8,128)} fusion(f32[4,48,1024]{2,1,0:T(8,128)S(1)} %dot_general.8, f32[256,512]{1,0:T(8,128)S(1)} %get-tuple-element.22, f32[256,512]{1,0:T(8,128)S(1)} %get-tuple-element.21), kind=kOutput, calls=%fused_computation.5 | convolution fusion | flops 604241920 | bytes 2031616 | tf_op jit(solution)/shard_map/dot_general | solution.py:88
  84.9 3.4 %all-to-all-start.1 = ((f32[4,48,256]{2,1,0:T(8,128)}), f32[4,48,256]{2,1,0:T(8,128)S(1)}, u32[]{:S(2)}, u32[]{:S(2)}) async-start(f32[4,48,256]{2,1,0:T(8,128)} %fusion.5), calls=%async_computation.1 | async-start | bytes 393216 | tf_op jit(solution)/shard_map/all_to_all | solution.py:21
  88.2 0.0 collective-permute-done.8
  88.2 1.2 broadcast_select_fusion.1
  89.5 0.1 pad_maximum_fusion
  89.6 4.6 %all-to-all-done.1 = f32[4,48,256]{2,1,0:T(8,128)S(1)} async-done(((f32[4,48,256]{2,1,0:T(8,128)}), f32[4,48,256]{2,1,0:T(8,128)S(1)}, u32[]{:S(2)}, u32[]{:S(2)}) %all-to-all-start.1) | async-done | bytes 196640 | tf_op jit(solution)/shard_map/all_to_all | solution.py:21
  94.3 0.1 copy.45
  94.4 5.6 %fusion.2 = f32[2,2,2,2,3,2,16,16]{6,7,0,2,1,3,5,4:T(8,128)S(1)} fusion(f32[2,2,2,2,2,3,16,256]{7,6,5,4,3,2,1,0:T(8,128)S(1)} %bitcast.52, f32[3,16,256]{2,1,0:T(8,128)S(1)} %broadcast_multiply_fusion), kind=kOutput, calls=%fused_computation.3 | convolution fusion | flops 75497472 | bytes 1720320 | tf_op jit(solution)/shard_map/abcdesvi,swi->ecdbsavw/dot_general | solution.py:98
  100.0 0.7 collective-permute-start.9
  100.6 2.8 %collective-permute-start.10 = (f32[3,16,128]{2,1,0:T(8,128)S(1)}, f32[3,16,128]{2,1,0:T(8,128)S(1)}, u32[]{:S(2)}, u32[]{:S(2)}) collective-permute-start(f32[3,16,128]{2,1,0:T(8,128)S(1)} %get-tuple-element.38), channel_id=1, source_target_pairs={{0,1},{1,0},{2,33},{3,32},{4,65},{5,64},{6,97},{7,96},{8,129},{9,1... | collective-permute-start | bytes 73736 | tf_op jit(solution)/shard_map/ppermute | solution.py:94
  103.4 0.1 copy.47
  103.6 0.1 copy.48
  103.7 0.3 copy.43
  104.0 0.0 copy-start
  104.0 0.9 all_to_all.27
  104.9 22.8 %all-to-all-start.2 = ((f32[16,1,1536]{2,1,0:T(1,128)}), f32[16,1,1536]{2,1,0:T(1,128)S(1)}, u32[]{:S(2)}, u32[]{:S(2)}) async-start(f32[16,1,1536]{2,1,0:T(1,128)} %all_to_all.27), calls=%async_computation.2 | async-start | bytes 196608 | tf_op jit(solution)/shard_map/all_to_all | solution.py:21
  127.8 0.0 collective-permute-done.9
  127.8 0.6 pad_maximum_fusion.8
  128.4 11.3 %all-to-all-done.2 = f32[16,1,1536]{2,1,0:T(1,128)S(1)} async-done(((f32[16,1,1536]{2,1,0:T(1,128)}), f32[16,1,1536]{2,1,0:T(1,128)S(1)}, u32[]{:S(2)}, u32[]{:S(2)}) %all-to-all-start.2) | async-done | bytes 98336 | tf_op jit(solution)/shard_map/all_to_all | solution.py:21
  139.7 0.1 reduce_sum.19
  139.8 0.9 all_to_all.24
  140.7 5.3 %all-to-all-start.3 = ((f32[32,1,1920]{2,1,0:T(1,128)}), f32[32,1,1920]{2,1,0:T(1,128)S(1)}, u32[]{:S(2)}, u32[]{:S(2)}) async-start(f32[32,1,1920]{2,1,0:T(1,128)} %all_to_all.24), calls=%async_computation.3 | async-start | bytes 491520 | tf_op jit(solution)/shard_map/all_to_all | solution.py:21
  146.0 0.3 copy.52
  146.3 10.6 %all-to-all-done.3 = f32[32,1,1920]{2,1,0:T(1,128)S(1)} async-done(((f32[32,1,1920]{2,1,0:T(1,128)}), f32[32,1,1920]{2,1,0:T(1,128)S(1)}, u32[]{:S(2)}, u32[]{:S(2)}) %all-to-all-start.3) | async-done | bytes 245792 | tf_op jit(solution)/shard_map/all_to_all | solution.py:21
  156.9 0.3 copy.49
  157.3 0.1 slice.19
  157.3 0.2 copy.50
  157.5 0.8 reshape.85
  158.4 0.5 copy.51
  158.9 0.1 bitcast_subtract_fusion
  159.0 0.9 copy.53
  (26 shorter events, 0.3 us)
Async XLA Ops:
  3.1 6.9 %collective-permute-start.4 = (f32[1,48,256]{2,1,0:T(8,128)S(1)}, f32[1,48,256]{2,1,0:T(8,128)S(1)}, u32[]{:S(2)}, u32[]{:S(2)}) collective-permute-start(f32[1,48,256]{2,1,0:T(8,128)S(1)} %bitcast.60), channel_id=1, source_target_pairs={{0,16},{16,0},{1,17},{17,1},{2,18},{18,2},{3,19},{19,3},{4,20},{20... | collective-permute-start | bytes 147464 | tf_op jit(solution)/shard_map/ppermute | solution.py:30
  10.1 30.4 %collective-permute-start.5 = (f32[2,48,256]{2,1,0:T(8,128)S(1)}, f32[2,48,256]{2,1,0:T(8,128)S(1)}, u32[]{:S(2)}, u32[]{:S(2)}) collective-permute-start(f32[2,48,256]{2,1,0:T(8,128)S(1)} %pad_maximum_fusion.7), channel_id=1, source_target_pairs={{0,4},{4,0},{1,5},{5,1},{2,6},{6,2},{3,7},{7,3},{8,12},{12,8},{9,1... | collective-permute-start | bytes 294920 | tf_op jit(solution)/shard_map/ppermute | solution.py:30
  14.5 2.6 %collective-permute-start = (f32[48,256]{1,0:T(8,128)S(1)}, f32[48,256]{1,0:T(8,128)S(1)}, u32[]{:S(2)}, u32[]{:S(2)}) collective-permute-start(f32[48,256]{1,0:T(8,128)S(1)} %bitcast.62), channel_id=1, source_target_pairs={{0,0},{1,1},{2,2},{3,3},{4,4},{5,5},{6,6},{7,7},{8,128},{9,129},{1... | collective-permute-start | bytes 147464 | tf_op jit(solution)/shard_map/ppermute | solution.py:75
  15.2 28.4 %collective-permute-start.1 = (f32[256,128]{1,0:T(8,128)}, f32[256,128]{1,0:T(8,128)S(1)}, u32[]{:S(2)}, u32[]{:S(2)}) collective-permute-start(f32[256,128]{1,0:T(8,128)} %param.5), channel_id=1, source_target_pairs={{0,4},{4,0},{1,5},{5,1},{2,6},{6,2},{3,7},{7,3},{8,12},{12,8},{9,1... | collective-permute-start | bytes 393224 | tf_op jit(solution)/shard_map/ppermute | solution.py:30
  17.1 26.4 %copy-start.1 = (f32[256,128]{1,0:T(8,128)S(1)}, f32[256,128]{1,0:T(8,128)}, u32[]{:S(2)}) copy-start(f32[256,128]{1,0:T(8,128)} %param.5) | copy-start | bytes 393220
  18.1 63.2 %all-to-all-start = ((f32[16,48,256]{2,1,0:T(8,128)}), f32[16,48,256]{2,1,0:T(8,128)S(1)}, u32[]{:S(2)}, u32[]{:S(2)}) async-start(f32[16,48,256]{2,1,0:T(8,128)} %broadcast_in_dim.7), calls=%async_computation | async-start | bytes 1572864 | tf_op jit(solution)/shard_map/all_to_all | solution.py:21
  40.6 6.4 %collective-permute-start.6 = (f32[4,48,256]{2,1,0:T(8,128)S(1)}, f32[4,48,256]{2,1,0:T(8,128)S(1)}, u32[]{:S(2)}, u32[]{:S(2)}) collective-permute-start(f32[4,48,256]{2,1,0:T(8,128)S(1)} %pad_maximum_fusion.6), channel_id=1, source_target_pairs={{0,8},{8,0},{1,9},{9,1},{2,10},{10,2},{3,11},{11,3},{4,12},{12,4},... | collective-permute-start | bytes 589832 | tf_op jit(solution)/shard_map/ppermute | solution.py:30
  43.6 18.8 %collective-permute-start.2 = (f32[256,256]{1,0:T(8,128)S(1)}, f32[256,256]{1,0:T(8,128)S(1)}, u32[]{:S(2)}, u32[]{:S(2)}) collective-permute-start(f32[256,256]{1,0:T(8,128)S(1)} %pad_maximum_fusion.4), channel_id=1, source_target_pairs={{0,2},{2,0},{1,3},{3,1},{4,6},{6,4},{5,7},{7,5},{8,10},{10,8},{9,1... | collective-permute-start | bytes 786440 | tf_op jit(solution)/shard_map/ppermute | solution.py:30
  47.0 25.5 %collective-permute-start.7 = (f32[8,48,256]{2,1,0:T(8,128)S(1)}, f32[8,48,256]{2,1,0:T(8,128)}, u32[]{:S(2)}, u32[]{:S(2)}) collective-permute-start(f32[8,48,256]{2,1,0:T(8,128)S(1)} %pad_maximum_fusion.3), channel_id=1, source_target_pairs={{0,2},{2,0},{1,3},{3,1},{4,6},{6,4},{5,7},{7,5},{8,10},{10,8},{9,1... | collective-permute-start | bytes 1179656 | tf_op jit(solution)/shard_map/ppermute | solution.py:30
  62.5 17.6 %collective-permute-start.3 = (f32[256,512]{1,0:T(8,128)S(1)}, f32[256,512]{1,0:T(8,128)}, u32[]{:S(2)}, u32[]{:S(2)}) collective-permute-start(f32[256,512]{1,0:T(8,128)S(1)} %pad_maximum_fusion.2), channel_id=1, source_target_pairs={{0,1},{1,0},{2,3},{3,2},{4,5},{5,4},{6,7},{7,6},{8,9},{9,8},{10,11... | collective-permute-start | bytes 1572872 | tf_op jit(solution)/shard_map/ppermute | solution.py:30
  74.6 13.7 %collective-permute-start.8 = (f32[16,48,256]{2,1,0:T(8,128)}, f32[16,48,256]{2,1,0:T(8,128)}, u32[]{:S(2)}, u32[]{:S(2)}) collective-permute-start(f32[16,48,256]{2,1,0:T(8,128)} %pad_maximum_fusion.1), channel_id=1, source_target_pairs={{0,1},{1,0},{2,3},{3,2},{4,5},{5,4},{6,7},{7,6},{8,9},{9,8},{10,11... | collective-permute-start | bytes 2359304 | tf_op jit(solution)/shard_map/ppermute | solution.py:30
  84.9 9.4 %all-to-all-start.1 = ((f32[4,48,256]{2,1,0:T(8,128)}), f32[4,48,256]{2,1,0:T(8,128)S(1)}, u32[]{:S(2)}, u32[]{:S(2)}) async-start(f32[4,48,256]{2,1,0:T(8,128)} %fusion.5), calls=%async_computation.1 | async-start | bytes 393216 | tf_op jit(solution)/shard_map/all_to_all | solution.py:21
  100.0 27.8 %collective-permute-start.9 = (f32[3,16,128]{2,1,0:T(8,128)S(1)}, f32[3,16,128]{2,1,0:T(8,128)S(1)}, u32[]{:S(2)}, u32[]{:S(2)}) collective-permute-start(f32[3,16,128]{2,1,0:T(8,128)S(1)} %get-tuple-element.37), channel_id=1, source_target_pairs={{0,0},{1,1},{2,32},{3,33},{4,64},{5,65},{6,96},{7,97},{8,128},{9,1... | collective-permute-start | bytes 73736 | tf_op jit(solution)/shard_map/ppermute | solution.py:93
  100.6 27.1 %collective-permute-start.10 = (f32[3,16,128]{2,1,0:T(8,128)S(1)}, f32[3,16,128]{2,1,0:T(8,128)S(1)}, u32[]{:S(2)}, u32[]{:S(2)}) collective-permute-start(f32[3,16,128]{2,1,0:T(8,128)S(1)} %get-tuple-element.38), channel_id=1, source_target_pairs={{0,1},{1,0},{2,33},{3,32},{4,65},{5,64},{6,97},{7,96},{8,129},{9,1... | collective-permute-start | bytes 73736 | tf_op jit(solution)/shard_map/ppermute | solution.py:94
  104.0 42.0 %copy-start = (f32[3,32,512]{2,1,0:T(8,128)S(1)}, f32[3,32,512]{2,1,0:T(8,128)}, u32[]{:S(2)}) copy-start(f32[3,32,512]{2,1,0:T(8,128)} %param.7) | copy-start | bytes 589828
  104.9 34.8 %all-to-all-start.2 = ((f32[16,1,1536]{2,1,0:T(1,128)}), f32[16,1,1536]{2,1,0:T(1,128)S(1)}, u32[]{:S(2)}, u32[]{:S(2)}) async-start(f32[16,1,1536]{2,1,0:T(1,128)} %all_to_all.27), calls=%async_computation.2 | async-start | bytes 196608 | tf_op jit(solution)/shard_map/all_to_all | solution.py:21
  140.7 16.2 %all-to-all-start.3 = ((f32[32,1,1920]{2,1,0:T(1,128)}), f32[32,1,1920]{2,1,0:T(1,128)S(1)}, u32[]{:S(2)}, u32[]{:S(2)}) async-start(f32[32,1,1920]{2,1,0:T(1,128)} %all_to_all.24), calls=%async_computation.3 | async-start | bytes 491520 | tf_op jit(solution)/shard_map/all_to_all | solution.py:21

commit v4 on v3

v4 whole, which is shorter than its diff:
```python
import jax
import jax.numpy as jnp
from jax import lax
from jax.sharding import Mesh, PartitionSpec as P

TILE = 128
NCORE = 2
ROW = ("zh", "zl", "yh")
COL = ("xh", "xl", "ylh", "yll", "core")
HIGHEST = lax.Precision.HIGHEST


def tile_masks(row_blocks, list_len, ntiles):
    tiles = jnp.arange(ntiles, dtype=jnp.int32)
    valid = jnp.arange(row_blocks.shape[1], dtype=jnp.int32)[None, :] < list_len[:, None]
    hit = (row_blocks[:, :, None] == tiles[None, None, :]) & valid[:, :, None]
    return jnp.any(hit, axis=1).astype(jnp.float32)


def row_mask(tile_mask, row, rows):
    tiles = rows // TILE
    picked = lax.dynamic_slice_in_dim(tile_mask, row * tiles, tiles, 1)
    return jnp.repeat(picked, TILE, axis=1)[:, None, :]


def exchange(blocks, axes):
    return lax.all_to_all(blocks, axes, split_axis=0, concat_axis=0, tiled=True)


def doubled(block, axis, dim):
    other = lax.ppermute(block, axis, [(0, 1), (1, 0)])
    side = lax.axis_index(axis)
    first = jnp.where(side == 0, block, other)
    second = jnp.where(side == 0, other, block)
    return jnp.concatenate([first, second], dim)


def digit_swap():
    zh, zl, yh = (lax.axis_size(a) for a in ROW)
    x, rest = lax.axis_size(COL[:2]), lax.axis_size(COL[2:])
    pairs = []
    for a in range(zh):
        for b in range(zl * yh):
            for c in range(x):
                for d in range(rest):
                    source = ((a * zl * yh + b) * x + c) * rest + d
                    target = ((c * zl * yh + b) * x + a) * rest + d
                    pairs.append((source, target))
    return pairs


def transposed(nrows):
    return [
        ((r * nrows + q) * NCORE + h, (q * nrows + r) * NCORE + h)
        for r in range(nrows)
        for q in range(nrows)
        for h in range(NCORE)
    ]


def shards(ainv, lpanel, kk_inverse, row_blocks, list_len):
    nx = lax.axis_size(COL[:2])
    nrows, ncols = lax.axis_size(ROW), lax.axis_size(COL)
    nchips = ncols // NCORE
    rows, sibs, width = lpanel.shape
    cols = ainv.shape[1]
    wide = sibs * width
    core = lax.axis_index("core")

    panel = jnp.transpose(lpanel, (1, 2, 0)).reshape(wide, rows)
    swapped = lax.ppermute(panel, ROW + COL, digit_swap())

    tile_mask = tile_masks(row_blocks, list_len, rows * nrows // TILE)
    own_mask = row_mask(tile_mask, lax.axis_index(ROW), rows)
    factor_mask = row_mask(tile_mask, lax.axis_index(COL[:2] + ROW[1:]), rows)

    factor = (swapped.reshape(sibs, width, rows) * factor_mask).reshape(wide, rows)
    factor = jnp.broadcast_to(factor, (nrows, wide, rows))
    factor = exchange(factor, ROW).reshape(nx, 2, 2, wide, rows)

    ainv = ainv[None]
    for axis in ("ylh", "yll", "core"):
        ainv = doubled(ainv, axis, 2 if axis == "core" else 0)

    panel_all = panel[None]
    for axis in ("ylh", "yll", "xh", "xl"):
        panel_all = doubled(panel_all, axis, 0)
    panel_all = panel_all.reshape(2, 2, 2, 2, sibs, width, rows)

    product = 0.0
    for high in range(2):
        for low in range(2):
            part = factor[:, high, low].reshape(nx * wide, rows)
            block = ainv[2 * low + high]
            product += lax.dot_general(part, block, (((1,), (1,)), ((), ())), precision=HIGHEST)
    product = product.reshape(nx, 1, wide, rows)
    product = jnp.broadcast_to(product, (nx, NCORE, wide, rows)).reshape(nx * NCORE, wide, rows)
    product = exchange(product, COL[:2] + COL[4:])
    product = jnp.sum(product.reshape(nx, NCORE, wide, rows), axis=0)
    both = product.reshape(NCORE, sibs, width, rows) * -own_mask

    term = jnp.einsum("cebdsvi,kswi->ecdbsvkw", panel_all, both, precision=HIGHEST)
    term = exchange(term.reshape(nrows, -1), ROW)
    diag = jnp.sum(term, axis=0)

    half = lax.dynamic_slice_in_dim(both, core * cols, cols, 3)
    ainv_ki = lax.ppermute(half, ROW + COL, transposed(nrows))
    diag, ainv_ki = lax.optimization_barrier((diag, ainv_ki))
    ainv_ki = ainv_ki.transpose(1, 0, 2, 3).reshape(sibs, NCORE * width, cols)

    share = rows // ncols
    split = jnp.where(core == 0, both[0], both[1]).reshape(wide, ncols, share)
    split = split.transpose(1, 0, 2).reshape(ncols, wide * share)
    joined = jnp.concatenate([jnp.broadcast_to(diag, (ncols, diag.size)), split], 1)
    joined = exchange(joined, COL)
    diag = joined[:, : diag.size].reshape(nchips, NCORE, sibs, width, NCORE * width)
    ainv_kk = kk_inverse - diag.transpose(2, 1, 3, 0, 4).reshape(kk_inverse.shape)
    split = joined[:, diag.size // ncols :].reshape(ncols, sibs, width, share)
    ainv_ik = split.transpose(3, 1, 0, 2).reshape(share, sibs, -1)
    return ainv_ik, ainv_kk, ainv_ki


def solution(mesh):
    devices = mesh.devices.reshape(4, 2, 2, 2, 2, 2, 2, 2)
    fine = Mesh(devices, ROW + COL)
    placed = (P(ROW, COL), P(ROW, None, COL), P(None, ROW, None), P(), P())

    return jax.shard_map(
        shards,
        mesh=fine,
        in_specs=placed,
        out_specs=(P(ROW + COL, None, None), P(None, ROW, None), P(None, ROW, COL)),
        check_vma=False,
    )
```

time: 161 us -> 141 us (0.88); the launches traced: 160 us -> 138 us
  starting transfers between devices: 92.2 us -> 74.6 us
  other arithmetic: 7.95 us -> 3.28 us
  matrix products: 7.45 us -> 5.04 us
  waiting for transfers between devices: 42.1 us -> 44 us
    ppermute x8 -> x7, starting transfers between devices: 34.3 us -> 23 us  [doubled(): other = lax.ppermute(block, axis, [(0, 1), (1, 0)])]
    all_to_all x4, starting transfers between devices: 53.9 us -> 49.4 us  [exchange(): return lax.all_to_all(blocks, axes, split_axis=0, concat_axis=0, tiled=True)]
    ppermute x2 -> x1, starting transfers between devices: 3.43 us -> 0.66 us  [shards(): ainv_ki = lax.ppermute(half, ROW + COL, transposed(nrows))]
    select_n x8 -> x6, other arithmetic: 3.58 us -> 1.17 us  [doubled(): first = jnp.where(side == 0, block, other)]
    dot_general x2 -> x5, matrix products: 7.45 us -> 5.04 us  [the longest x1 3.34 us: shards(): jnp.einsum('cebdsvi,kswi->ecdbsvkw', panel_all, both, precision=HIGHEST)]
    ppermute x8 -> x7, waiting for transfers between devices: 15.5 us -> 16.8 us  [doubled(): other = lax.ppermute(block, axis, [(0, 1), (1, 0)])]
  transfers between devices with their start and end apart: 15 -> 13, of which waited for: 6 -> 5; matrix products, arithmetic and copies ran while one was open for 7% -> 5% of each run, Pallas kernels for 0% -> 0%
where the time goes in v4:
time: 141 us; the launch traced here: 138 us
  starting transfers between devices  74.6 us (53%)
  waiting for transfers between devices  44 us (31%)
  local copies, waits for them, and re-layouts  10.3 us (7%)
  matrix products  5.04 us (4%)
  other arithmetic  3.28 us (2%)
    all_to_all x4, starting transfers between devices, exchange(): return lax.all_to_all(blocks, axes, split_axis=0, concat_axis=0, tiled=True)  49.4 us
    all_to_all x4, waiting for transfers between devices, exchange(): return lax.all_to_all(blocks, axes, split_axis=0, concat_axis=0, tiled=True)  27.2 us
    ppermute x7, starting transfers between devices, doubled(): other = lax.ppermute(block, axis, [(0, 1), (1, 0)])  23 us
    ppermute x7, waiting for transfers between devices, doubled(): other = lax.ppermute(block, axis, [(0, 1), (1, 0)])  16.8 us
    dot_general x1, matrix products, shards(): jnp.einsum('cebdsvi,kswi->ecdbsvkw', panel_all, both, precision=HIGHEST)  3.34 us
    all_to_all x3, local copies, waits for them, and re-layouts, exchange(): return lax.all_to_all(blocks, axes, split_axis=0, concat_axis=0, tiled=True)  2.91 us
  transfers between devices with their start and end apart: 13, of which 5 were waited for; matrix products, arithmetic and copies ran while one was open for 5% of the time, Pallas kernels for 0%

profile of v4, /device:TPU:1, one launch (start us, length us, event | category | flops | bytes accessed | tf_op | source)
XLA Modules:
  0.0 138.3 jit_solution(3178721266824829567)
XLA Ops:
  0.6 1.5 %collective-permute-start = (f32[48,256]{1,0:T(8,128)}, f32[48,256]{1,0:T(8,128)S(1)}, u32[]{:S(2)}, u32[]{:S(2)}) collective-permute-start(f32[48,256]{1,0:T(8,128)} %bitcast.92), channel_id=1, source_target_pairs={{0,0},{1,1},{2,2},{3,3},{4,4},{5,5},{6,6},{7,7},{8,128},{9,129},{1... | collective-permute-start | bytes 147464 | tf_op jit(solution)/shard_map/ppermute | solution.py:71
  2.1 5.0 %collective-permute-start.1 = (f32[1,256,128]{2,1,0:T(8,128)}, f32[1,256,128]{2,1,0:T(8,128)S(1)}, u32[]{:S(2)}, u32[]{:S(2)}) collective-permute-start(f32[1,256,128]{2,1,0:T(8,128)} %bitcast.89), channel_id=1, source_target_pairs={{0,4},{4,0},{1,5},{5,1},{2,6},{6,2},{3,7},{7,3},{8,12},{12,8},{9,1... | collective-permute-start | bytes 393224 | tf_op jit(solution)/shard_map/ppermute | solution.py:31
  7.1 1.9 %collective-permute-start.4 = (f32[1,48,256]{2,1,0:T(8,128)}, f32[1,48,256]{2,1,0:T(8,128)S(1)}, u32[]{:S(2)}, u32[]{:S(2)}) collective-permute-start(f32[1,48,256]{2,1,0:T(8,128)} %bitcast.93), channel_id=1, source_target_pairs={{0,4},{4,0},{1,5},{5,1},{2,6},{6,2},{3,7},{7,3},{8,12},{12,8},{9,1... | collective-permute-start | bytes 147464 | tf_op jit(solution)/shard_map/ppermute | solution.py:31
  9.1 0.6 copy-done.4
  9.7 0.1 iota_compare_fusion.1
  9.8 0.1 fusion.16
  9.9 0.1 dynamic-slice_negate_fusion
  10.0 0.1 broadcast_bitcast_fusion.1
  10.1 0.0 collective-permute-done
  10.1 1.0 broadcast_in_dim.29
  11.1 18.2 %all-to-all-start = ((f32[16,48,256]{2,1,0:T(8,128)}), f32[16,48,256]{2,1,0:T(8,128)S(1)}, u32[]{:S(2)}, u32[]{:S(2)}) async-start(f32[16,48,256]{2,1,0:T(8,128)} %broadcast_in_dim.29), calls=%async_computation | async-start | bytes 1572864 | tf_op jit(solution)/shard_map/all_to_all | solution.py:27
  29.3 0.0 collective-permute-done.4
  29.3 0.0 copy-start.1
  29.4 2.4 %collective-permute-start.5 = (f32[2,48,256]{2,1,0:T(8,128)S(1)}, f32[2,48,256]{2,1,0:T(8,128)S(1)}, u32[]{:S(2)}, u32[]{:S(2)}) collective-permute-start(f32[2,48,256]{2,1,0:T(8,128)S(1)} %pad_maximum_fusion.7), channel_id=1, source_target_pairs={{0,2},{2,0},{1,3},{3,1},{4,6},{6,4},{5,7},{7,5},{8,10},{10,8},{9,1... | collective-permute-start | bytes 294920 | tf_op jit(solution)/shard_map/ppermute | solution.py:31
  31.8 0.0 collective-permute-done.1
  31.9 3.0 %collective-permute-start.2 = (f32[2,256,128]{2,1,0:T(8,128)S(1)}, f32[2,256,128]{2,1,0:T(8,128)S(1)}, u32[]{:S(2)}, u32[]{:S(2)}) collective-permute-start(f32[2,256,128]{2,1,0:T(8,128)S(1)} %pad_maximum_fusion.4), channel_id=1, source_target_pairs={{0,2},{2,0},{1,3},{3,1},{4,6},{6,4},{5,7},{7,5},{8,10},{10,8},{9,1... | collective-permute-start | bytes 786440 | tf_op jit(solution)/shard_map/ppermute | solution.py:31
  34.9 14.8 %collective-permute-done.5 = f32[2,48,256]{2,1,0:T(8,128)S(1)} collective-permute-done((f32[2,48,256]{2,1,0:T(8,128)S(1)}, f32[2,48,256]{2,1,0:T(8,128)S(1)}, u32[]{:S(2)}, u32[]{:S(2)}) %collective-permute-start.5) | collective-permute-done | bytes 98336 | tf_op jit(solution)/shard_map/ppermute | solution.py:31
  49.8 3.6 %collective-permute-start.6 = (f32[4,48,256]{2,1,0:T(8,128)S(1)}, f32[4,48,256]{2,1,0:T(8,128)S(1)}, u32[]{:S(2)}, u32[]{:S(2)}) collective-permute-start(f32[4,48,256]{2,1,0:T(8,128)S(1)} %pad_maximum_fusion.6), channel_id=1, source_target_pairs={{0,16},{16,0},{1,17},{17,1},{2,18},{18,2},{3,19},{19,3},{4,20},{20... | collective-permute-start | bytes 589832 | tf_op jit(solution)/shard_map/ppermute | solution.py:31
  53.4 2.0 %collective-permute-done.2 = f32[2,256,128]{2,1,0:T(8,128)S(1)} collective-permute-done((f32[2,256,128]{2,1,0:T(8,128)S(1)}, f32[2,256,128]{2,1,0:T(8,128)S(1)}, u32[]{:S(2)}, u32[]{:S(2)}) %collective-permute-start.2) | collective-permute-done | bytes 262176 | tf_op jit(solution)/shard_map/ppermute | solution.py:31
  55.4 2.6 %collective-permute-start.3 = (f32[4,256,128]{2,1,0:T(8,128)S(1)}, f32[4,256,128]{2,1,0:T(8,128)S(1)}, u32[]{:S(2)}, u32[]{:S(2)}) collective-permute-start(f32[4,256,128]{2,1,0:T(8,128)S(1)} %pad_maximum_fusion.1), channel_id=1, source_target_pairs={{0,1},{1,0},{2,3},{3,2},{4,5},{5,4},{6,7},{7,6},{8,9},{9,8},{10,11... | collective-permute-start | bytes 1572872 | tf_op jit(solution)/shard_map/ppermute | solution.py:31
  58.1 0.1 broadcast_bitcast_fusion
  58.1 0.0 collective-permute-done.6
  58.2 0.8 pad_maximum_fusion.2
  59.0 4.4 %collective-permute-start.7 = (f32[8,48,256]{2,1,0:T(8,128)}, f32[8,48,256]{2,1,0:T(8,128)}, u32[]{:S(2)}, u32[]{:S(2)}) collective-permute-start(f32[8,48,256]{2,1,0:T(8,128)} %pad_maximum_fusion.2), channel_id=1, source_target_pairs={{0,8},{8,0},{1,9},{9,1},{2,10},{10,2},{3,11},{11,3},{4,12},{12,4},... | collective-permute-start | bytes 1179656 | tf_op jit(solution)/shard_map/ppermute | solution.py:31
  63.4 0.1 broadcast_select_fusion
  63.5 0.0 all-to-all-done
  63.5 0.1 fusion.21
  63.6 0.4 fusion.9
  64.0 0.4 convolution_add_fusion.2
  64.4 0.4 convolution_add_fusion.1
  64.9 0.4 convolution_add_fusion
  65.3 0.8 broadcast_in_dim.32
  66.1 7.2 %all-to-all-start.1 = ((f32[8,48,256]{2,1,0:T(8,128)}), f32[8,48,256]{2,1,0:T(8,128)S(1)}, u32[]{:S(2)}, u32[]{:S(2)}) async-start(f32[8,48,256]{2,1,0:T(8,128)} %bitcast.14), calls=%async_computation.1 | async-start | bytes 786432 | tf_op jit(solution)/shard_map/all_to_all | solution.py:27
  73.3 0.0 collective-permute-done.7
  73.3 1.1 broadcast_select_fusion.3
  74.4 0.1 pad_maximum_fusion
  74.4 6.6 %all-to-all-done.1 = f32[8,48,256]{2,1,0:T(8,128)S(1)} async-done(((f32[8,48,256]{2,1,0:T(8,128)}), f32[8,48,256]{2,1,0:T(8,128)S(1)}, u32[]{:S(2)}, u32[]{:S(2)}) %all-to-all-start.1) | async-done | bytes 393248 | tf_op jit(solution)/shard_map/all_to_all | solution.py:27
  81.1 3.3 %convolution_bitcast_fusion = f32[2,2,2,2,3,16,2,16]{5,7,2,3,0,1,6,4:T(8,128)S(1)} fusion(f32[2,2,2,2,3,16,256,1]{6,5,4,3,2,1,0,7:T(8,128)S(1)} %bitcast.76, f32[2,3,16,256]{3,2,1,0:T(8,128)S(1)} %bitcast.80, f32[3,256]{1,0:T(4,128)S(1)} %bitcast.95), kind=kOutput, calls=%fused_computation.6 | convolution fusion | flops 75522048 | bytes 986112 | tf_op jit(solution)/shard_map/cebdsvi,kswi->ecdbsvkw/dot_general | solution.py:102
  84.4 0.5 copy.38
  84.9 1.7 %all_to_all.27 = f32[16,1,1536]{2,1,0:T(1,128)} reshape(f32[2,2,2,2,3,16,2,16]{7,6,5,4,3,2,1,0:T(2,128)S(1)} %copy.38) | data formatting | bytes 196608 | tf_op jit(solution)/shard_map/all_to_all | solution.py:27
  86.6 10.9 %all-to-all-start.2 = ((f32[16,1,1536]{2,1,0:T(1,128)}), f32[16,1,1536]{2,1,0:T(1,128)S(1)}, u32[]{:S(2)}, u32[]{:S(2)}) async-start(f32[16,1,1536]{2,1,0:T(1,128)} %all_to_all.27), calls=%async_computation.2 | async-start | bytes 196608 | tf_op jit(solution)/shard_map/all_to_all | solution.py:27
  97.6 0.7 collective-permute-start.8
  98.3 0.2 copy.40
  98.5 0.2 select_n.131
  98.7 0.1 copy.41
  98.9 0.1 copy.42
  99.0 10.3 %all-to-all-done.2 = f32[16,1,1536]{2,1,0:T(1,128)S(1)} async-done(((f32[16,1,1536]{2,1,0:T(1,128)}), f32[16,1,1536]{2,1,0:T(1,128)S(1)}, u32[]{:S(2)}, u32[]{:S(2)}) %all-to-all-start.2) | async-done | bytes 98336 | tf_op jit(solution)/shard_map/all_to_all | solution.py:27
  109.3 0.1 reduce_sum.19
  109.4 0.0 collective-permute-done.8
  109.4 0.9 all_to_all.24
  110.3 13.0 %all-to-all-start.3 = ((f32[32,1,1920]{2,1,0:T(1,128)}), f32[32,1,1920]{2,1,0:T(1,128)S(1)}, u32[]{:S(2)}, u32[]{:S(2)}) async-start(f32[32,1,1920]{2,1,0:T(1,128)} %all_to_all.24), calls=%async_computation.3 | async-start | bytes 491520 | tf_op jit(solution)/shard_map/all_to_all | solution.py:27
  123.3 0.6 copy.47
  123.9 10.3 %all-to-all-done.3 = f32[32,1,1920]{2,1,0:T(1,128)S(1)} async-done(((f32[32,1,1920]{2,1,0:T(1,128)}), f32[32,1,1920]{2,1,0:T(1,128)S(1)}, u32[]{:S(2)}, u32[]{:S(2)}) %all-to-all-start.3) | async-done | bytes 245792 | tf_op jit(solution)/shard_map/all_to_all | solution.py:27
  134.2 0.3 copy.43
  134.6 0.1 slice.61
  134.6 0.2 copy.44
  134.8 0.8 reshape.98
  135.7 0.2 copy.45
  135.9 0.2 reshape.99
  136.2 0.5 copy.46
  136.6 0.0 copy-start
  136.6 0.3 reshape.100
  137.0 0.6 copy-done
  137.5 0.7 sub.3
  (27 shorter events, 0.3 us)
Async XLA Ops:
  0.6 9.5 %collective-permute-start = (f32[48,256]{1,0:T(8,128)}, f32[48,256]{1,0:T(8,128)S(1)}, u32[]{:S(2)}, u32[]{:S(2)}) collective-permute-start(f32[48,256]{1,0:T(8,128)} %bitcast.92), channel_id=1, source_target_pairs={{0,0},{1,1},{2,2},{3,3},{4,4},{5,5},{6,6},{7,7},{8,128},{9,129},{1... | collective-permute-start | bytes 147464 | tf_op jit(solution)/shard_map/ppermute | solution.py:71
  2.1 29.7 %collective-permute-start.1 = (f32[1,256,128]{2,1,0:T(8,128)}, f32[1,256,128]{2,1,0:T(8,128)S(1)}, u32[]{:S(2)}, u32[]{:S(2)}) collective-permute-start(f32[1,256,128]{2,1,0:T(8,128)} %bitcast.89), channel_id=1, source_target_pairs={{0,4},{4,0},{1,5},{5,1},{2,6},{6,2},{3,7},{7,3},{8,12},{12,8},{9,1... | collective-permute-start | bytes 393224 | tf_op jit(solution)/shard_map/ppermute | solution.py:31
  7.1 22.2 %collective-permute-start.4 = (f32[1,48,256]{2,1,0:T(8,128)}, f32[1,48,256]{2,1,0:T(8,128)S(1)}, u32[]{:S(2)}, u32[]{:S(2)}) collective-permute-start(f32[1,48,256]{2,1,0:T(8,128)} %bitcast.93), channel_id=1, source_target_pairs={{0,4},{4,0},{1,5},{5,1},{2,6},{6,2},{3,7},{7,3},{8,12},{12,8},{9,1... | collective-permute-start | bytes 147464 | tf_op jit(solution)/shard_map/ppermute | solution.py:31
  9.1 0.7 copy-start.4
  9.1 0.7 copy-start.3
  11.1 18.3 %copy-start.2 = (f32[256,3,16]{0,2,1:T(8,128)S(1)}, f32[256,3,16]{0,2,1:T(8,128)}, u32[]{:S(2)}) copy-start(f32[256,3,16]{0,2,1:T(8,128)} %param.6) | copy-start | bytes 147460
  11.1 52.4 %all-to-all-start = ((f32[16,48,256]{2,1,0:T(8,128)}), f32[16,48,256]{2,1,0:T(8,128)S(1)}, u32[]{:S(2)}, u32[]{:S(2)}) async-start(f32[16,48,256]{2,1,0:T(8,128)} %broadcast_in_dim.29), calls=%async_computation | async-start | bytes 1572864 | tf_op jit(solution)/shard_map/all_to_all | solution.py:27
  29.3 2.5 %copy-start.1 = (f32[256,128]{1,0:T(8,128)S(1)}, f32[256,128]{1,0:T(8,128)}, u32[]{:S(2)}) copy-start(f32[256,128]{1,0:T(8,128)} %param.5) | copy-start | bytes 393220
  29.4 20.3 %collective-permute-start.5 = (f32[2,48,256]{2,1,0:T(8,128)S(1)}, f32[2,48,256]{2,1,0:T(8,128)S(1)}, u32[]{:S(2)}, u32[]{:S(2)}) collective-permute-start(f32[2,48,256]{2,1,0:T(8,128)S(1)} %pad_maximum_fusion.7), channel_id=1, source_target_pairs={{0,2},{2,0},{1,3},{3,1},{4,6},{6,4},{5,7},{7,5},{8,10},{10,8},{9,1... | collective-permute-start | bytes 294920 | tf_op jit(solution)/shard_map/ppermute | solution.py:31
  31.9 23.4 %collective-permute-start.2 = (f32[2,256,128]{2,1,0:T(8,128)S(1)}, f32[2,256,128]{2,1,0:T(8,128)S(1)}, u32[]{:S(2)}, u32[]{:S(2)}) collective-permute-start(f32[2,256,128]{2,1,0:T(8,128)S(1)} %pad_maximum_fusion.4), channel_id=1, source_target_pairs={{0,2},{2,0},{1,3},{3,1},{4,6},{6,4},{5,7},{7,5},{8,10},{10,8},{9,1... | collective-permute-start | bytes 786440 | tf_op jit(solution)/shard_map/ppermute | solution.py:31
  49.8 8.4 %collective-permute-start.6 = (f32[4,48,256]{2,1,0:T(8,128)S(1)}, f32[4,48,256]{2,1,0:T(8,128)S(1)}, u32[]{:S(2)}, u32[]{:S(2)}) collective-permute-start(f32[4,48,256]{2,1,0:T(8,128)S(1)} %pad_maximum_fusion.6), channel_id=1, source_target_pairs={{0,16},{16,0},{1,17},{17,1},{2,18},{18,2},{3,19},{19,3},{4,20},{20... | collective-permute-start | bytes 589832 | tf_op jit(solution)/shard_map/ppermute | solution.py:31
  55.4 8.0 %collective-permute-start.3 = (f32[4,256,128]{2,1,0:T(8,128)S(1)}, f32[4,256,128]{2,1,0:T(8,128)S(1)}, u32[]{:S(2)}, u32[]{:S(2)}) collective-permute-start(f32[4,256,128]{2,1,0:T(8,128)S(1)} %pad_maximum_fusion.1), channel_id=1, source_target_pairs={{0,1},{1,0},{2,3},{3,2},{4,5},{5,4},{6,7},{7,6},{8,9},{9,8},{10,11... | collective-permute-start | bytes 1572872 | tf_op jit(solution)/shard_map/ppermute | solution.py:31
  59.0 14.3 %collective-permute-start.7 = (f32[8,48,256]{2,1,0:T(8,128)}, f32[8,48,256]{2,1,0:T(8,128)}, u32[]{:S(2)}, u32[]{:S(2)}) collective-permute-start(f32[8,48,256]{2,1,0:T(8,128)} %pad_maximum_fusion.2), channel_id=1, source_target_pairs={{0,8},{8,0},{1,9},{9,1},{2,10},{10,2},{3,11},{11,3},{4,12},{12,4},... | collective-permute-start | bytes 1179656 | tf_op jit(solution)/shard_map/ppermute | solution.py:31
  66.1 14.9 %all-to-all-start.1 = ((f32[8,48,256]{2,1,0:T(8,128)}), f32[8,48,256]{2,1,0:T(8,128)S(1)}, u32[]{:S(2)}, u32[]{:S(2)}) async-start(f32[8,48,256]{2,1,0:T(8,128)} %bitcast.14), calls=%async_computation.1 | async-start | bytes 786432 | tf_op jit(solution)/shard_map/all_to_all | solution.py:27
  86.6 22.7 %all-to-all-start.2 = ((f32[16,1,1536]{2,1,0:T(1,128)}), f32[16,1,1536]{2,1,0:T(1,128)S(1)}, u32[]{:S(2)}, u32[]{:S(2)}) async-start(f32[16,1,1536]{2,1,0:T(1,128)} %all_to_all.27), calls=%async_computation.2 | async-start | bytes 196608 | tf_op jit(solution)/shard_map/all_to_all | solution.py:27
  97.6 11.8 %collective-permute-start.8 = (f32[2,3,16,128]{3,2,1,0:T(8,128)S(1)}, f32[2,3,16,128]{3,2,1,0:T(8,128)S(1)}, u32[]{:S(2)}, u32[]{:S(2)}) collective-permute-start(f32[2,3,16,128]{3,2,1,0:T(8,128)S(1)} %constant_dynamic-slice_fusion), channel_id=1, source_target_pairs={{0,0},{1,1},{2,32},{3,33},{4,64},{5,65},{6,96},{7,97},{8,128},{9,1... | collective-permute-start | bytes 147464 | tf_op jit(solution)/shard_map/ppermute | solution.py:107
  110.3 23.9 %all-to-all-start.3 = ((f32[32,1,1920]{2,1,0:T(1,128)}), f32[32,1,1920]{2,1,0:T(1,128)S(1)}, u32[]{:S(2)}, u32[]{:S(2)}) async-start(f32[32,1,1920]{2,1,0:T(1,128)} %all_to_all.24), calls=%async_computation.3 | async-start | bytes 491520 | tf_op jit(solution)/shard_map/all_to_all | solution.py:27
  136.6 0.9 copy-start

commit v5 on v4

--- a/solution.py
+++ b/solution.py
@@ -35,7 +35,7 @@
     return jnp.concatenate([first, second], dim)
 
 
-def digit_swap():
+def digit_swap(flip):
     zh, zl, yh = (lax.axis_size(a) for a in ROW)
     x, rest = lax.axis_size(COL[:2]), lax.axis_size(COL[2:])
     pairs = []
@@ -44,7 +44,7 @@
             for c in range(x):
                 for d in range(rest):
                     source = ((a * zl * yh + b) * x + c) * rest + d
-                    target = ((c * zl * yh + b) * x + a) * rest + d
+                    target = ((c * zl * yh + (b ^ flip)) * x + a) * rest + d
                     pairs.append((source, target))
     return pairs
 
@@ -68,29 +68,32 @@
     core = lax.axis_index("core")
 
     panel = jnp.transpose(lpanel, (1, 2, 0)).reshape(wide, rows)
-    swapped = lax.ppermute(panel, ROW + COL, digit_swap())
+    yh = lax.axis_index("yh")
+    same = lax.ppermute(panel, ROW + COL, digit_swap(0))
+    flip = lax.ppermute(panel, ROW + COL, digit_swap(1))
 
     tile_mask = tile_masks(row_blocks, list_len, rows * nrows // TILE)
     own_mask = row_mask(tile_mask, lax.axis_index(ROW), rows)
-    factor_mask = row_mask(tile_mask, lax.axis_index(COL[:2] + ROW[1:]), rows)
-
-    factor = (swapped.reshape(sibs, width, rows) * factor_mask).reshape(wide, rows)
-    factor = jnp.broadcast_to(factor, (nrows, wide, rows))
-    factor = exchange(factor, ROW).reshape(nx, 2, 2, wide, rows)
+    pair_mask = row_mask(tile_mask, lax.axis_index(COL[:2] + ROW[1:2]), 2 * rows)
+    pair = [jnp.where(yh == 0, same, flip), jnp.where(yh == 0, flip, same)]
+    pair = jnp.concatenate(pair, 1).reshape(sibs, width, 2 * rows) * pair_mask
+    pair = pair.reshape(wide, 2 * rows)
+    pair = jnp.broadcast_to(pair, (nrows // 2, wide, 2 * rows))
+    factor = exchange(pair, ROW[:2]).reshape(nx, 2, wide, 2 * rows)
 
     ainv = ainv[None]
     for axis in ("ylh", "yll", "core"):
         ainv = doubled(ainv, axis, 2 if axis == "core" else 0)
 
     panel_all = panel[None]
-    for axis in ("ylh", "yll", "xh", "xl"):
+    for axis in ("ylh", "yll", "xh"):
         panel_all = doubled(panel_all, axis, 0)
-    panel_all = panel_all.reshape(2, 2, 2, 2, sibs, width, rows)
+    panel_far = lax.ppermute(panel_all, "xl", [(0, 1), (1, 0)])
 
     product = 0.0
     for high in range(2):
         for low in range(2):
-            part = factor[:, high, low].reshape(nx * wide, rows)
+            part = factor[:, high, :, low * rows : (low + 1) * rows].reshape(nx * wide, rows)
             block = ainv[2 * low + high]
             product += lax.dot_general(part, block, (((1,), (1,)), ((), ())), precision=HIGHEST)
     product = product.reshape(nx, 1, wide, rows)
@@ -98,15 +101,18 @@
     product = exchange(product, COL[:2] + COL[4:])
     product = jnp.sum(product.reshape(nx, NCORE, wide, rows), axis=0)
     both = product.reshape(NCORE, sibs, width, rows) * -own_mask
+    pair = both.transpose(1, 0, 2, 3).reshape(sibs, NCORE * width, rows)
 
-    term = jnp.einsum("cebdsvi,kswi->ecdbsvkw", panel_all, both, precision=HIGHEST)
+    terms = []
+    for source in (panel_all, panel_far):
+        source = source.reshape(2, 2, 2, sibs, width, rows)
+        terms.append(jnp.einsum("ebdsvi,swi->edbsvw", source, pair, precision=HIGHEST))
+    xl = lax.axis_index("xl")
+    first = jnp.where(xl == 0, terms[0], terms[1])
+    second = jnp.where(xl == 0, terms[1], terms[0])
+    term = jnp.stack([first, second], 1)
     term = exchange(term.reshape(nrows, -1), ROW)
     diag = jnp.sum(term, axis=0)
-
-    half = lax.dynamic_slice_in_dim(both, core * cols, cols, 3)
-    ainv_ki = lax.ppermute(half, ROW + COL, transposed(nrows))
-    diag, ainv_ki = lax.optimization_barrier((diag, ainv_ki))
-    ainv_ki = ainv_ki.transpose(1, 0, 2, 3).reshape(sibs, NCORE * width, cols)
 
     share = rows // ncols
     split = jnp.where(core == 0, both[0], both[1]).reshape(wide, ncols, share)
@@ -117,6 +123,8 @@
     ainv_kk = kk_inverse - diag.transpose(2, 1, 3, 0, 4).reshape(kk_inverse.shape)
     split = joined[:, diag.size // ncols :].reshape(ncols, sibs, width, share)
     ainv_ik = split.transpose(3, 1, 0, 2).reshape(share, sibs, -1)
+    half = lax.dynamic_slice_in_dim(pair, core * cols, cols, 2)
+    ainv_ki = lax.ppermute(half, ROW + COL, transposed(nrows))
     return ainv_ik, ainv_kk, ainv_ki
 
 

time: 141 us -> 130 us (0.922)
  the two profiles are of different devices: /device:TPU:1 before, /device:TPU:12 now
where the time goes in v5:
time: 130 us; the launch traced here: 129 us
  starting transfers between devices  64.1 us (49%)
  waiting for transfers between devices  50.5 us (39%)
  local copies, waits for them, and re-layouts  9.06 us (7%)
  matrix products  2.62 us (2%)
  other arithmetic  1.46 us (1%)
    all_to_all x4, starting transfers between devices, exchange(): return lax.all_to_all(blocks, axes, split_axis=0, concat_axis=0, tiled=True)  22.5 us
    all_to_all x4, waiting for transfers between devices, exchange(): return lax.all_to_all(blocks, axes, split_axis=0, concat_axis=0, tiled=True)  20 us
    ppermute x6, starting transfers between devices, doubled(): other = lax.ppermute(block, axis, [(0, 1), (1, 0)])  19.4 us
    ppermute x1, waiting for transfers between devices, shards(): ainv_ki = lax.ppermute(half, ROW + COL, transposed(nrows))  14.3 us
    ppermute x1, starting transfers between devices, shards(): same = lax.ppermute(panel, ROW + COL, digit_swap(0))  10.9 us
    ppermute x1, waiting for transfers between devices, shards(): panel_far = lax.ppermute(panel_all, 'xl', [(0, 1), (1, 0)])  8.92 us
    ppermute x1, starting transfers between devices, shards(): flip = lax.ppermute(panel, ROW + COL, digit_swap(1))  6.28 us
    ppermute x6, waiting for transfers between devices, doubled(): other = lax.ppermute(block, axis, [(0, 1), (1, 0)])  4.05 us
  transfers between devices with their start and end apart: 14, of which 7 were waited for; matrix products, arithmetic and copies ran while one was open for 4% of the time, Pallas kernels for 0%

profile of v5, /device:TPU:12, one launch (start us, length us, event | category | flops | bytes accessed | tf_op | source)
XLA Modules:
  0.0 128.8 jit_solution(1651279467737821580)
XLA Ops:
  0.6 10.9 %collective-permute-start = (f32[48,256]{1,0:T(8,128)}, f32[48,256]{1,0:T(8,128)S(1)}, u32[]{:S(2)}, u32[]{:S(2)}) collective-permute-start(f32[48,256]{1,0:T(8,128)} %bitcast.104), channel_id=1, source_target_pairs={{0,0},{1,1},{2,2},{3,3},{4,4},{5,5},{6,6},{7,7},{8,128},{9,129},{1... | collective-permute-start | bytes 147464 | tf_op jit(solution)/shard_map/ppermute | solution.py:72
  11.5 6.3 %collective-permute-start.1 = (f32[48,256]{1,0:T(8,128)}, f32[48,256]{1,0:T(8,128)S(1)}, u32[]{:S(2)}, u32[]{:S(2)}) collective-permute-start(f32[48,256]{1,0:T(8,128)} %bitcast.105), channel_id=1, source_target_pairs={{0,32},{1,33},{2,34},{3,35},{4,36},{5,37},{6,38},{7,39},{8,160},{9... | collective-permute-start | bytes 147464 | tf_op jit(solution)/shard_map/ppermute | solution.py:73
  17.8 2.7 %collective-permute-start.2 = (f32[1,256,128]{2,1,0:T(8,128)}, f32[1,256,128]{2,1,0:T(8,128)S(1)}, u32[]{:S(2)}, u32[]{:S(2)}) collective-permute-start(f32[1,256,128]{2,1,0:T(8,128)} %bitcast.103), channel_id=1, source_target_pairs={{0,4},{4,0},{1,5},{5,1},{2,6},{6,2},{3,7},{7,3},{8,12},{12,8},{9,1... | collective-permute-start | bytes 393224 | tf_op jit(solution)/shard_map/ppermute | solution.py:31
  20.5 4.0 %collective-permute-start.5 = (f32[1,48,256]{2,1,0:T(8,128)}, f32[1,48,256]{2,1,0:T(8,128)S(1)}, u32[]{:S(2)}, u32[]{:S(2)}) collective-permute-start(f32[1,48,256]{2,1,0:T(8,128)} %bitcast.106), channel_id=1, source_target_pairs={{0,4},{4,0},{1,5},{5,1},{2,6},{6,2},{3,7},{7,3},{8,12},{12,8},{9,1... | collective-permute-start | bytes 147464 | tf_op jit(solution)/shard_map/ppermute | solution.py:31
  24.6 0.6 copy-done.4
  25.2 0.1 iota_compare_fusion.1
  25.3 0.1 fusion.18
  25.4 0.1 constant_dynamic-slice_fusion.1
  25.5 0.1 broadcast_bitcast_fusion
  25.6 0.1 dynamic-slice_negate_fusion
  25.6 0.0 collective-permute-done
  25.7 3.3 %collective-permute-done.1 = f32[48,256]{1,0:T(8,128)S(1)} collective-permute-done((f32[48,256]{1,0:T(8,128)}, f32[48,256]{1,0:T(8,128)S(1)}, u32[]{:S(2)}, u32[]{:S(2)}) %collective-permute-start.1) | collective-permute-done | bytes 49184 | tf_op jit(solution)/shard_map/ppermute | solution.py:73
  28.9 1.0 broadcast_in_dim.29
  29.9 3.7 %all-to-all-start = ((f32[8,48,512]{2,1,0:T(8,128)}), f32[8,48,512]{2,1,0:T(8,128)S(1)}, u32[]{:S(2)}, u32[]{:S(2)}) async-start(f32[8,48,512]{2,1,0:T(8,128)} %broadcast_in_dim.29), calls=%async_computation | async-start | bytes 1572864 | tf_op jit(solution)/shard_map/all_to_all | solution.py:27
  33.6 0.0 collective-permute-done.2
  33.7 0.0 copy-start.2
  33.7 2.3 %collective-permute-start.3 = (f32[2,256,128]{2,1,0:T(8,128)S(1)}, f32[2,256,128]{2,1,0:T(8,128)S(1)}, u32[]{:S(2)}, u32[]{:S(2)}) collective-permute-start(f32[2,256,128]{2,1,0:T(8,128)S(1)} %pad_maximum_fusion.4), channel_id=1, source_target_pairs={{0,2},{2,0},{1,3},{3,1},{4,6},{6,4},{5,7},{7,5},{8,10},{10,8},{9,1... | collective-permute-start | bytes 786440 | tf_op jit(solution)/shard_map/ppermute | solution.py:31
  36.1 3.6 %collective-permute-start.6 = (f32[2,48,256]{2,1,0:T(8,128)S(1)}, f32[2,48,256]{2,1,0:T(8,128)S(1)}, u32[]{:S(2)}, u32[]{:S(2)}) collective-permute-start(f32[2,48,256]{2,1,0:T(8,128)S(1)} %pad_maximum_fusion.7), channel_id=1, source_target_pairs={{0,2},{2,0},{1,3},{3,1},{4,6},{6,4},{5,7},{7,5},{8,10},{10,8},{9,1... | collective-permute-start | bytes 294920 | tf_op jit(solution)/shard_map/ppermute | solution.py:31
  39.6 4.0 %collective-permute-done.3 = f32[2,256,128]{2,1,0:T(8,128)S(1)} collective-permute-done((f32[2,256,128]{2,1,0:T(8,128)S(1)}, f32[2,256,128]{2,1,0:T(8,128)S(1)}, u32[]{:S(2)}, u32[]{:S(2)}) %collective-permute-start.3) | collective-permute-done | bytes 262176 | tf_op jit(solution)/shard_map/ppermute | solution.py:31
  43.7 1.9 %collective-permute-start.4 = (f32[4,256,128]{2,1,0:T(8,128)S(1)}, f32[4,256,128]{2,1,0:T(8,128)S(1)}, u32[]{:S(2)}, u32[]{:S(2)}) collective-permute-start(f32[4,256,128]{2,1,0:T(8,128)S(1)} %pad_maximum_fusion), channel_id=1, source_target_pairs={{0,1},{1,0},{2,3},{3,2},{4,5},{5,4},{6,7},{7,6},{8,9},{9,8},{10,11... | collective-permute-start | bytes 1572872 | tf_op jit(solution)/shard_map/ppermute | solution.py:31
  45.7 0.1 broadcast_bitcast_fusion.1
  45.7 0.0 collective-permute-done.6
  45.8 4.9 %collective-permute-start.7 = (f32[4,48,256]{2,1,0:T(8,128)S(1)}, f32[4,48,256]{2,1,0:T(8,128)S(1)}, u32[]{:S(2)}, u32[]{:S(2)}) collective-permute-start(f32[4,48,256]{2,1,0:T(8,128)S(1)} %pad_maximum_fusion.6), channel_id=1, source_target_pairs={{0,16},{16,0},{1,17},{17,1},{2,18},{18,2},{3,19},{19,3},{4,20},{20... | collective-permute-start | bytes 589832 | tf_op jit(solution)/shard_map/ppermute | solution.py:31
  50.7 0.0 collective-permute-done.4
  50.7 0.1 broadcast_select_fusion
  50.8 5.1 %all-to-all-done = f32[8,48,512]{2,1,0:T(8,128)S(1)} async-done(((f32[8,48,512]{2,1,0:T(8,128)}), f32[8,48,512]{2,1,0:T(8,128)S(1)}, u32[]{:S(2)}, u32[]{:S(2)}) %all-to-all-start) | async-done | bytes 786464 | tf_op jit(solution)/shard_map/all_to_all | solution.py:27
  55.9 0.1 fusion.23
  55.9 0.4 fusion.12
  56.4 0.4 convolution_add_fusion.2
  56.8 0.4 convolution_add_fusion.1
  57.2 0.4 convolution_add_fusion
  57.7 0.8 broadcast_in_dim.32
  58.5 6.5 %all-to-all-start.1 = ((f32[8,48,256]{2,1,0:T(8,128)}), f32[8,48,256]{2,1,0:T(8,128)S(1)}, u32[]{:S(2)}, u32[]{:S(2)}) async-start(f32[8,48,256]{2,1,0:T(8,128)} %bitcast.15), calls=%async_computation.1 | async-start | bytes 786432 | tf_op jit(solution)/shard_map/all_to_all | solution.py:27
  64.9 0.0 collective-permute-done.7
  65.0 3.1 %collective-permute-start.8 = (f32[8,48,256]{2,1,0:T(8,128)S(1)}, f32[8,48,256]{2,1,0:T(8,128)S(1)}, u32[]{:S(2)}, u32[]{:S(2)}) collective-permute-start(f32[8,48,256]{2,1,0:T(8,128)S(1)} %pad_maximum_fusion.1), channel_id=1, source_target_pairs={{0,8},{8,0},{1,9},{9,1},{2,10},{10,2},{3,11},{11,3},{4,12},{12,4},... | collective-permute-start | bytes 1179656 | tf_op jit(solution)/shard_map/ppermute | solution.py:91
  68.1 2.8 %all-to-all-done.1 = f32[8,48,256]{2,1,0:T(8,128)S(1)} async-done(((f32[8,48,256]{2,1,0:T(8,128)}), f32[8,48,256]{2,1,0:T(8,128)S(1)}, u32[]{:S(2)}, u32[]{:S(2)}) %all-to-all-start.1) | async-done | bytes 393248 | tf_op jit(solution)/shard_map/all_to_all | solution.py:27
  71.0 8.9 %collective-permute-done.8 = f32[8,48,256]{2,1,0:T(8,128)S(1)} collective-permute-done((f32[8,48,256]{2,1,0:T(8,128)S(1)}, f32[8,48,256]{2,1,0:T(8,128)S(1)}, u32[]{:S(2)}, u32[]{:S(2)}) %collective-permute-start.8) | collective-permute-done | bytes 393248 | tf_op jit(solution)/shard_map/ppermute | solution.py:91
  79.9 0.5 fusion
  80.4 0.5 select_bitcast_fusion.1
  80.9 0.9 all_to_all.27
  81.8 6.0 %all-to-all-start.2 = ((f32[16,1,1536]{2,1,0:T(1,128)}), f32[16,1,1536]{2,1,0:T(1,128)S(1)}, u32[]{:S(2)}, u32[]{:S(2)}) async-start(f32[16,1,1536]{2,1,0:T(1,128)} %all_to_all.27), calls=%async_computation.2 | async-start | bytes 196608 | tf_op jit(solution)/shard_map/all_to_all | solution.py:27
  87.8 0.2 copy.41
  88.0 0.2 select_n.153
  88.2 0.1 copy.42
  88.4 0.1 copy.43
  88.5 12.1 %all-to-all-done.2 = f32[16,1,1536]{2,1,0:T(1,128)S(1)} async-done(((f32[16,1,1536]{2,1,0:T(1,128)}), f32[16,1,1536]{2,1,0:T(1,128)S(1)}, u32[]{:S(2)}, u32[]{:S(2)}) %all-to-all-start.2) | async-done | bytes 98336 | tf_op jit(solution)/shard_map/all_to_all | solution.py:27
  100.6 0.1 reduce_sum.19
  100.7 0.9 all_to_all.24
  101.6 6.4 %all-to-all-start.3 = ((f32[32,1,1920]{2,1,0:T(1,128)}), f32[32,1,1920]{2,1,0:T(1,128)S(1)}, u32[]{:S(2)}, u32[]{:S(2)}) async-start(f32[32,1,1920]{2,1,0:T(1,128)} %all_to_all.24), calls=%async_computation.3 | async-start | bytes 491520 | tf_op jit(solution)/shard_map/all_to_all | solution.py:27
  108.0 1.9 %collective-permute-start.9 = (f32[3,32,128]{2,1,0:T(8,128)S(1)}, f32[3,32,128]{2,1,0:T(8,128)S(1)}, u32[]{:S(2)}, u32[]{:S(2)}) collective-permute-start(f32[3,32,128]{2,1,0:T(8,128)S(1)} %constant_dynamic-slice_fusion), channel_id=1, source_target_pairs={{0,0},{1,1},{2,32},{3,33},{4,64},{5,65},{6,96},{7,97},{8,128},{9,1... | collective-permute-start | bytes 147464 | tf_op jit(solution)/shard_map/ppermute | solution.py:127
  109.9 14.3 %collective-permute-done.9 = f32[3,32,128]{2,1,0:T(8,128)S(1)} collective-permute-done((f32[3,32,128]{2,1,0:T(8,128)S(1)}, f32[3,32,128]{2,1,0:T(8,128)S(1)}, u32[]{:S(2)}, u32[]{:S(2)}) %collective-permute-start.9) | collective-permute-done | bytes 49184 | tf_op jit(solution)/shard_map/ppermute | solution.py:127
  124.2 0.0 all-to-all-done.3
  124.2 0.3 copy.44
  124.5 0.1 slice.61
  124.6 0.2 copy.45
  124.8 0.8 reshape.103
  125.6 0.2 copy.46
  125.9 0.2 reshape.104
  126.1 0.5 copy.47
  126.6 0.0 copy-start
  126.6 0.3 reshape.105
  126.9 0.6 copy-done
  127.5 0.7 sub.3
  128.2 0.6 copy.62
  (33 shorter events, 0.5 us)
Async XLA Ops:
  0.6 25.0 %collective-permute-start = (f32[48,256]{1,0:T(8,128)}, f32[48,256]{1,0:T(8,128)S(1)}, u32[]{:S(2)}, u32[]{:S(2)}) collective-permute-start(f32[48,256]{1,0:T(8,128)} %bitcast.104), channel_id=1, source_target_pairs={{0,0},{1,1},{2,2},{3,3},{4,4},{5,5},{6,6},{7,7},{8,128},{9,129},{1... | collective-permute-start | bytes 147464 | tf_op jit(solution)/shard_map/ppermute | solution.py:72
  11.5 17.4 %collective-permute-start.1 = (f32[48,256]{1,0:T(8,128)}, f32[48,256]{1,0:T(8,128)S(1)}, u32[]{:S(2)}, u32[]{:S(2)}) collective-permute-start(f32[48,256]{1,0:T(8,128)} %bitcast.105), channel_id=1, source_target_pairs={{0,32},{1,33},{2,34},{3,35},{4,36},{5,37},{6,38},{7,39},{8,160},{9... | collective-permute-start | bytes 147464 | tf_op jit(solution)/shard_map/ppermute | solution.py:73
  17.8 15.8 %collective-permute-start.2 = (f32[1,256,128]{2,1,0:T(8,128)}, f32[1,256,128]{2,1,0:T(8,128)S(1)}, u32[]{:S(2)}, u32[]{:S(2)}) collective-permute-start(f32[1,256,128]{2,1,0:T(8,128)} %bitcast.103), channel_id=1, source_target_pairs={{0,4},{4,0},{1,5},{5,1},{2,6},{6,2},{3,7},{7,3},{8,12},{12,8},{9,1... | collective-permute-start | bytes 393224 | tf_op jit(solution)/shard_map/ppermute | solution.py:31
  20.5 15.5 %collective-permute-start.5 = (f32[1,48,256]{2,1,0:T(8,128)}, f32[1,48,256]{2,1,0:T(8,128)S(1)}, u32[]{:S(2)}, u32[]{:S(2)}) collective-permute-start(f32[1,48,256]{2,1,0:T(8,128)} %bitcast.106), channel_id=1, source_target_pairs={{0,4},{4,0},{1,5},{5,1},{2,6},{6,2},{3,7},{7,3},{8,12},{12,8},{9,1... | collective-permute-start | bytes 147464 | tf_op jit(solution)/shard_map/ppermute | solution.py:31
  24.6 0.7 copy-start.4
  24.6 0.7 copy-start.3
  29.9 3.7 %copy-start.1 = (f32[256,128]{1,0:T(8,128)S(1)}, f32[256,128]{1,0:T(8,128)}, u32[]{:S(2)}) copy-start(f32[256,128]{1,0:T(8,128)} %param.5) | copy-start | bytes 393220
  29.9 25.9 %all-to-all-start = ((f32[8,48,512]{2,1,0:T(8,128)}), f32[8,48,512]{2,1,0:T(8,128)S(1)}, u32[]{:S(2)}, u32[]{:S(2)}) async-start(f32[8,48,512]{2,1,0:T(8,128)} %broadcast_in_dim.29), calls=%async_computation | async-start | bytes 1572864 | tf_op jit(solution)/shard_map/all_to_all | solution.py:27
  33.7 2.3 %copy-start.2 = (f32[256,3,16]{0,2,1:T(8,128)S(1)}, f32[256,3,16]{0,2,1:T(8,128)}, u32[]{:S(2)}) copy-start(f32[256,3,16]{0,2,1:T(8,128)} %param.6) | copy-start | bytes 147460
  33.7 9.9 %collective-permute-start.3 = (f32[2,256,128]{2,1,0:T(8,128)S(1)}, f32[2,256,128]{2,1,0:T(8,128)S(1)}, u32[]{:S(2)}, u32[]{:S(2)}) collective-permute-start(f32[2,256,128]{2,1,0:T(8,128)S(1)} %pad_maximum_fusion.4), channel_id=1, source_target_pairs={{0,2},{2,0},{1,3},{3,1},{4,6},{6,4},{5,7},{7,5},{8,10},{10,8},{9,1... | collective-permute-start | bytes 786440 | tf_op jit(solution)/shard_map/ppermute | solution.py:31
  36.1 9.7 %collective-permute-start.6 = (f32[2,48,256]{2,1,0:T(8,128)S(1)}, f32[2,48,256]{2,1,0:T(8,128)S(1)}, u32[]{:S(2)}, u32[]{:S(2)}) collective-permute-start(f32[2,48,256]{2,1,0:T(8,128)S(1)} %pad_maximum_fusion.7), channel_id=1, source_target_pairs={{0,2},{2,0},{1,3},{3,1},{4,6},{6,4},{5,7},{7,5},{8,10},{10,8},{9,1... | collective-permute-start | bytes 294920 | tf_op jit(solution)/shard_map/ppermute | solution.py:31
  43.7 7.0 %collective-permute-start.4 = (f32[4,256,128]{2,1,0:T(8,128)S(1)}, f32[4,256,128]{2,1,0:T(8,128)S(1)}, u32[]{:S(2)}, u32[]{:S(2)}) collective-permute-start(f32[4,256,128]{2,1,0:T(8,128)S(1)} %pad_maximum_fusion), channel_id=1, source_target_pairs={{0,1},{1,0},{2,3},{3,2},{4,5},{5,4},{6,7},{7,6},{8,9},{9,8},{10,11... | collective-permute-start | bytes 1572872 | tf_op jit(solution)/shard_map/ppermute | solution.py:31
  45.8 19.1 %collective-permute-start.7 = (f32[4,48,256]{2,1,0:T(8,128)S(1)}, f32[4,48,256]{2,1,0:T(8,128)S(1)}, u32[]{:S(2)}, u32[]{:S(2)}) collective-permute-start(f32[4,48,256]{2,1,0:T(8,128)S(1)} %pad_maximum_fusion.6), channel_id=1, source_target_pairs={{0,16},{16,0},{1,17},{17,1},{2,18},{18,2},{3,19},{19,3},{4,20},{20... | collective-permute-start | bytes 589832 | tf_op jit(solution)/shard_map/ppermute | solution.py:31
  58.5 12.5 %all-to-all-start.1 = ((f32[8,48,256]{2,1,0:T(8,128)}), f32[8,48,256]{2,1,0:T(8,128)S(1)}, u32[]{:S(2)}, u32[]{:S(2)}) async-start(f32[8,48,256]{2,1,0:T(8,128)} %bitcast.15), calls=%async_computation.1 | async-start | bytes 786432 | tf_op jit(solution)/shard_map/all_to_all | solution.py:27
  65.0 14.9 %collective-permute-start.8 = (f32[8,48,256]{2,1,0:T(8,128)S(1)}, f32[8,48,256]{2,1,0:T(8,128)S(1)}, u32[]{:S(2)}, u32[]{:S(2)}) collective-permute-start(f32[8,48,256]{2,1,0:T(8,128)S(1)} %pad_maximum_fusion.1), channel_id=1, source_target_pairs={{0,8},{8,0},{1,9},{9,1},{2,10},{10,2},{3,11},{11,3},{4,12},{12,4},... | collective-permute-start | bytes 1179656 | tf_op jit(solution)/shard_map/ppermute | solution.py:91
  81.8 18.8 %all-to-all-start.2 = ((f32[16,1,1536]{2,1,0:T(1,128)}), f32[16,1,1536]{2,1,0:T(1,128)S(1)}, u32[]{:S(2)}, u32[]{:S(2)}) async-start(f32[16,1,1536]{2,1,0:T(1,128)} %all_to_all.27), calls=%async_computation.2 | async-start | bytes 196608 | tf_op jit(solution)/shard_map/all_to_all | solution.py:27
  101.6 22.6 %all-to-all-start.3 = ((f32[32,1,1920]{2,1,0:T(1,128)}), f32[32,1,1920]{2,1,0:T(1,128)S(1)}, u32[]{:S(2)}, u32[]{:S(2)}) async-start(f32[32,1,1920]{2,1,0:T(1,128)} %all_to_all.24), calls=%async_computation.3 | async-start | bytes 491520 | tf_op jit(solution)/shard_map/all_to_all | solution.py:27
  108.0 16.2 %collective-permute-start.9 = (f32[3,32,128]{2,1,0:T(8,128)S(1)}, f32[3,32,128]{2,1,0:T(8,128)S(1)}, u32[]{:S(2)}, u32[]{:S(2)}) collective-permute-start(f32[3,32,128]{2,1,0:T(8,128)S(1)} %constant_dynamic-slice_fusion), channel_id=1, source_target_pairs={{0,0},{1,1},{2,32},{3,33},{4,64},{5,65},{6,96},{7,97},{8,128},{9,1... | collective-permute-start | bytes 147464 | tf_op jit(solution)/shard_map/ppermute | solution.py:127
  126.6 0.9 copy-start

commit v6 on v5

--- a/solution.py
+++ b/solution.py
@@ -81,13 +81,12 @@
     pair = jnp.broadcast_to(pair, (nrows // 2, wide, 2 * rows))
     factor = exchange(pair, ROW[:2]).reshape(nx, 2, wide, 2 * rows)
 
-    ainv = ainv[None]
-    for axis in ("ylh", "yll", "core"):
-        ainv = doubled(ainv, axis, 2 if axis == "core" else 0)
-
-    panel_all = panel[None]
-    for axis in ("ylh", "yll", "xh"):
-        panel_all = doubled(panel_all, axis, 0)
+    load = jnp.concatenate([ainv, panel[:, :cols], panel[:, cols:]], 0)[None]
+    for axis in ("ylh", "yll"):
+        load = doubled(load, axis, 0)
+    ainv = doubled(load[:, :rows], "core", 2)
+    panel_all = jnp.concatenate([load[:, rows : rows + wide], load[:, rows + wide :]], 2)
+    panel_all = doubled(panel_all, "xh", 0)
     panel_far = lax.ppermute(panel_all, "xl", [(0, 1), (1, 0)])
 
     product = 0.0
@@ -112,19 +111,22 @@
     second = jnp.where(xl == 0, terms[1], terms[0])
     term = jnp.stack([first, second], 1)
     term = exchange(term.reshape(nrows, -1), ROW)
-    diag = jnp.sum(term, axis=0)
+    own = lax.dynamic_slice_in_dim(kk_inverse, core * width, width, 1)
+    own = lax.dynamic_slice_in_dim(own, lax.axis_index(COL[:4]) * NCORE * width, NCORE * width, 2)
+    diag = own.reshape(-1) - jnp.sum(term, axis=0)
+
+    half = lax.dynamic_slice_in_dim(pair, core * cols, cols, 2)
+    ainv_ki = lax.ppermute(half, ROW + COL, transposed(nrows))
 
     share = rows // ncols
     split = jnp.where(core == 0, both[0], both[1]).reshape(wide, ncols, share)
     split = split.transpose(1, 0, 2).reshape(ncols, wide * share)
     joined = jnp.concatenate([jnp.broadcast_to(diag, (ncols, diag.size)), split], 1)
     joined = exchange(joined, COL)
-    diag = joined[:, : diag.size].reshape(nchips, NCORE, sibs, width, NCORE * width)
-    ainv_kk = kk_inverse - diag.transpose(2, 1, 3, 0, 4).reshape(kk_inverse.shape)
-    split = joined[:, diag.size // ncols :].reshape(ncols, sibs, width, share)
+    diag = joined[:, : own.size].reshape(nchips, NCORE, sibs, width, NCORE * width)
+    ainv_kk = diag.transpose(2, 1, 3, 0, 4).reshape(kk_inverse.shape)
+    split = joined[:, own.size :].reshape(ncols, sibs, width, share)
     ainv_ik = split.transpose(3, 1, 0, 2).reshape(share, sibs, -1)
-    half = lax.dynamic_slice_in_dim(pair, core * cols, cols, 2)
-    ainv_ki = lax.ppermute(half, ROW + COL, transposed(nrows))
     return ainv_ik, ainv_kk, ainv_ki
 
 

time: 130 us -> 137 us (1.054)
  waiting for transfers between devices: 50.5 us -> 60.8 us
  starting transfers between devices: 64.1 us -> 59.8 us
    all_to_all x4, waiting for transfers between devices: 20 us -> 28.9 us  [exchange(): return lax.all_to_all(blocks, axes, split_axis=0, concat_axis=0, tiled=True)]
    ppermute x6 -> x4, waiting for transfers between devices: 4.05 us -> 8.8 us  [doubled(): other = lax.ppermute(block, axis, [(0, 1), (1, 0)])]
    ppermute x6 -> x4, starting transfers between devices: 19.4 us -> 14.9 us  [doubled(): other = lax.ppermute(block, axis, [(0, 1), (1, 0)])]
    ppermute x1, waiting for transfers between devices: 3.26 us -> 0.01 us  [shards(): flip = lax.ppermute(panel, ROW + COL, digit_swap(1))]
  transfers between devices with their start and end apart: 14 -> 12, of which waited for: 7 -> 7; matrix products, arithmetic and copies ran while one was open for 4% -> 5% of each run, Pallas kernels for 0% -> 0%
where the time goes in v6:
time: 137 us; the launch traced here: 136 us
  waiting for transfers between devices  60.8 us (44%)
  starting transfers between devices  59.8 us (44%)
  local copies, waits for them, and re-layouts  10.1 us (7%)
  matrix products  2.62 us (2%)
  other arithmetic  1.74 us (1%)
    all_to_all x4, waiting for transfers between devices, exchange(): return lax.all_to_all(blocks, axes, split_axis=0, concat_axis=0, tiled=True)  28.9 us
    all_to_all x4, starting transfers between devices, exchange(): return lax.all_to_all(blocks, axes, split_axis=0, concat_axis=0, tiled=True)  22.6 us
    ppermute x4, starting transfers between devices, doubled(): other = lax.ppermute(block, axis, [(0, 1), (1, 0)])  14.9 us
    ppermute x1, waiting for transfers between devices, shards(): ainv_ki = lax.ppermute(half, ROW + COL, transposed(nrows))  14.3 us
    ppermute x1, starting transfers between devices, shards(): same = lax.ppermute(panel, ROW + COL, digit_swap(0))  11 us
    ppermute x1, waiting for transfers between devices, shards(): panel_far = lax.ppermute(panel_all, 'xl', [(0, 1), (1, 0)])  8.92 us
    ppermute x4, waiting for transfers between devices, doubled(): other = lax.ppermute(block, axis, [(0, 1), (1, 0)])  8.8 us
    ppermute x1, starting transfers between devices, shards(): flip = lax.ppermute(panel, ROW + COL, digit_swap(1))  6.28 us
  transfers between devices with their start and end apart: 12, of which 7 were waited for; matrix products, arithmetic and copies ran while one was open for 5% of the time, Pallas kernels for 0%

profile of v6, /device:TPU:12, one launch (start us, length us, event | category | flops | bytes accessed | tf_op | source)
XLA Modules:
  0.0 136.2 jit_solution(804913910909538748)
XLA Ops:
  0.6 0.0 copy-start
  0.6 11.0 %collective-permute-start = (f32[48,256]{1,0:T(8,128)}, f32[48,256]{1,0:T(8,128)S(1)}, u32[]{:S(2)}, u32[]{:S(2)}) collective-permute-start(f32[48,256]{1,0:T(8,128)} %bitcast.102), channel_id=1, source_target_pairs={{0,0},{1,1},{2,2},{3,3},{4,4},{5,5},{6,6},{7,7},{8,128},{9,129},{1... | collective-permute-start | bytes 147464 | tf_op jit(solution)/shard_map/ppermute | solution.py:72
  11.6 6.3 %collective-permute-start.1 = (f32[48,256]{1,0:T(8,128)}, f32[48,256]{1,0:T(8,128)S(1)}, u32[]{:S(2)}, u32[]{:S(2)}) collective-permute-start(f32[48,256]{1,0:T(8,128)} %bitcast.103), channel_id=1, source_target_pairs={{0,32},{1,33},{2,34},{3,35},{4,36},{5,37},{6,38},{7,39},{8,160},{9... | collective-permute-start | bytes 147464 | tf_op jit(solution)/shard_map/ppermute | solution.py:73
  17.9 0.8 fusion.27
  18.7 1.0 maximum_bitcast_fusion
  19.7 2.7 %collective-permute-start.2 = (f32[1,352,128]{2,1,0:T(8,128)S(1)}, f32[1,352,128]{2,1,0:T(8,128)S(1)}, u32[]{:S(2)}, u32[]{:S(2)}) collective-permute-start(f32[1,352,128]{2,1,0:T(8,128)S(1)} %maximum_bitcast_fusion), channel_id=1, source_target_pairs={{0,4},{4,0},{1,5},{5,1},{2,6},{6,2},{3,7},{7,3},{8,12},{12,8},{9,1... | collective-permute-start | bytes 540680 | tf_op jit(solution)/shard_map/ppermute | solution.py:31
  22.4 0.0 copy-start.3
  22.4 0.0 copy-start.2
  22.5 0.6 copy-done.3
  23.1 0.1 iota_compare_fusion.1
  23.2 0.1 fusion.21
  23.3 0.1 constant_dynamic-slice_fusion.1
  23.4 0.1 broadcast_bitcast_fusion
  23.4 6.3 %collective-permute-done.2 = f32[1,352,128]{2,1,0:T(8,128)S(1)} collective-permute-done((f32[1,352,128]{2,1,0:T(8,128)S(1)}, f32[1,352,128]{2,1,0:T(8,128)S(1)}, u32[]{:S(2)}, u32[]{:S(2)}) %collective-permute-start.2) | collective-permute-done | bytes 180256 | tf_op jit(solution)/shard_map/ppermute | solution.py:31
  29.9 5.8 %collective-permute-start.3 = (f32[2,352,128]{2,1,0:T(8,128)S(1)}, f32[2,352,128]{2,1,0:T(8,128)S(1)}, u32[]{:S(2)}, u32[]{:S(2)}) collective-permute-start(f32[2,352,128]{2,1,0:T(8,128)S(1)} %pad_maximum_fusion.2), channel_id=1, source_target_pairs={{0,2},{2,0},{1,3},{3,1},{4,6},{6,4},{5,7},{7,5},{8,10},{10,8},{9,1... | collective-permute-start | bytes 1081352 | tf_op jit(solution)/shard_map/ppermute | solution.py:31
  35.7 0.0 collective-permute-done
  35.7 0.0 collective-permute-done.1
  35.8 1.0 broadcast_in_dim.29
  36.8 4.9 %all-to-all-start = ((f32[8,48,512]{2,1,0:T(8,128)}), f32[8,48,512]{2,1,0:T(8,128)S(1)}, u32[]{:S(2)}, u32[]{:S(2)}) async-start(f32[8,48,512]{2,1,0:T(8,128)} %broadcast_in_dim.29), calls=%async_computation | async-start | bytes 1572864 | tf_op jit(solution)/shard_map/all_to_all | solution.py:27
  41.7 0.1 dynamic-slice_negate_fusion
  41.7 2.5 %collective-permute-done.3 = f32[2,352,128]{2,1,0:T(8,128)S(1)} collective-permute-done((f32[2,352,128]{2,1,0:T(8,128)S(1)}, f32[2,352,128]{2,1,0:T(8,128)S(1)}, u32[]{:S(2)}, u32[]{:S(2)}) %collective-permute-start.3) | collective-permute-done | bytes 360480 | tf_op jit(solution)/shard_map/ppermute | solution.py:31
  44.3 1.9 %collective-permute-start.4 = (f32[4,256,128]{2,1,0:T(8,128)S(1)}, f32[4,256,128]{2,1,0:T(8,128)S(1)}, u32[]{:S(2)}, u32[]{:S(2)}) collective-permute-start(f32[4,256,128]{2,1,0:T(8,128)S(1)} %fusion), channel_id=1, source_target_pairs={{0,1},{1,0},{2,3},{3,2},{4,5},{5,4},{6,7},{7,6},{8,9},{9,8},{10,11... | collective-permute-start | bytes 1572872 | tf_op jit(solution)/shard_map/ppermute | solution.py:31
  46.2 0.1 broadcast_bitcast_fusion.1
  46.3 0.1 constant_dynamic-slice_fusion.2
  46.4 0.1 reshape.96
  46.5 4.5 %collective-permute-start.5 = (f32[4,48,256]{2,1,0:T(8,128)S(1)}, f32[4,48,256]{2,1,0:T(8,128)S(1)}, u32[]{:S(2)}, u32[]{:S(2)}) collective-permute-start(f32[4,48,256]{2,1,0:T(8,128)S(1)} %fusion.18), channel_id=1, source_target_pairs={{0,16},{16,0},{1,17},{17,1},{2,18},{18,2},{3,19},{19,3},{4,20},{20... | collective-permute-start | bytes 589832 | tf_op jit(solution)/shard_map/ppermute | solution.py:31
  50.9 0.0 collective-permute-done.4
  51.0 0.1 broadcast_select_fusion
  51.0 13.5 %all-to-all-done = f32[8,48,512]{2,1,0:T(8,128)S(1)} async-done(((f32[8,48,512]{2,1,0:T(8,128)}), f32[8,48,512]{2,1,0:T(8,128)S(1)}, u32[]{:S(2)}, u32[]{:S(2)}) %all-to-all-start) | async-done | bytes 786464 | tf_op jit(solution)/shard_map/all_to_all | solution.py:27
  64.6 0.1 fusion.26
  64.6 0.4 fusion.13
  65.1 0.4 convolution_add_fusion.2
  65.5 0.4 convolution_add_fusion.1
  65.9 0.4 convolution_add_fusion
  66.4 0.8 broadcast_in_dim.32
  67.1 8.4 %all-to-all-start.1 = ((f32[8,48,256]{2,1,0:T(8,128)}), f32[8,48,256]{2,1,0:T(8,128)S(1)}, u32[]{:S(2)}, u32[]{:S(2)}) async-start(f32[8,48,256]{2,1,0:T(8,128)} %bitcast.15), calls=%async_computation.1 | async-start | bytes 786432 | tf_op jit(solution)/shard_map/all_to_all | solution.py:27
  75.5 0.0 collective-permute-done.5
  75.6 3.1 %collective-permute-start.6 = (f32[8,48,256]{2,1,0:T(8,128)S(1)}, f32[8,48,256]{2,1,0:T(8,128)S(1)}, u32[]{:S(2)}, u32[]{:S(2)}) collective-permute-start(f32[8,48,256]{2,1,0:T(8,128)S(1)} %pad_maximum_fusion), channel_id=1, source_target_pairs={{0,8},{8,0},{1,9},{9,1},{2,10},{10,2},{3,11},{11,3},{4,12},{12,4},... | collective-permute-start | bytes 1179656 | tf_op jit(solution)/shard_map/ppermute | solution.py:90
  78.7 2.8 %all-to-all-done.1 = f32[8,48,256]{2,1,0:T(8,128)S(1)} async-done(((f32[8,48,256]{2,1,0:T(8,128)}), f32[8,48,256]{2,1,0:T(8,128)S(1)}, u32[]{:S(2)}, u32[]{:S(2)}) %all-to-all-start.1) | async-done | bytes 393248 | tf_op jit(solution)/shard_map/all_to_all | solution.py:27
  81.6 8.9 %collective-permute-done.6 = f32[8,48,256]{2,1,0:T(8,128)S(1)} collective-permute-done((f32[8,48,256]{2,1,0:T(8,128)S(1)}, f32[8,48,256]{2,1,0:T(8,128)S(1)}, u32[]{:S(2)}, u32[]{:S(2)}) %collective-permute-start.6) | collective-permute-done | bytes 393248 | tf_op jit(solution)/shard_map/ppermute | solution.py:90
  90.5 0.5 fusion.1
  91.0 0.5 select_bitcast_fusion.1
  91.5 0.9 all_to_all.27
  92.4 3.5 %all-to-all-start.2 = ((f32[16,1,1536]{2,1,0:T(1,128)}), f32[16,1,1536]{2,1,0:T(1,128)S(1)}, u32[]{:S(2)}, u32[]{:S(2)}) async-start(f32[16,1,1536]{2,1,0:T(1,128)} %all_to_all.27), calls=%async_computation.2 | async-start | bytes 196608 | tf_op jit(solution)/shard_map/all_to_all | solution.py:27
  95.9 0.2 copy.41
  96.1 0.2 select_n.137
  96.4 0.1 copy.42
  96.5 0.1 copy.43
  96.6 12.5 %all-to-all-done.2 = f32[16,1,1536]{2,1,0:T(1,128)S(1)} async-done(((f32[16,1,1536]{2,1,0:T(1,128)}), f32[16,1,1536]{2,1,0:T(1,128)S(1)}, u32[]{:S(2)}, u32[]{:S(2)}) %all-to-all-start.2) | async-done | bytes 98336 | tf_op jit(solution)/shard_map/all_to_all | solution.py:27
  109.1 0.1 reduce_sum.19
  109.2 0.9 all_to_all.24
  110.1 5.9 %all-to-all-start.3 = ((f32[32,1,1920]{2,1,0:T(1,128)}), f32[32,1,1920]{2,1,0:T(1,128)S(1)}, u32[]{:S(2)}, u32[]{:S(2)}) async-start(f32[32,1,1920]{2,1,0:T(1,128)} %all_to_all.24), calls=%async_computation.3 | async-start | bytes 491520 | tf_op jit(solution)/shard_map/all_to_all | solution.py:27
  116.0 1.9 %collective-permute-start.7 = (f32[3,32,128]{2,1,0:T(8,128)S(1)}, f32[3,32,128]{2,1,0:T(8,128)S(1)}, u32[]{:S(2)}, u32[]{:S(2)}) collective-permute-start(f32[3,32,128]{2,1,0:T(8,128)S(1)} %constant_dynamic-slice_fusion), channel_id=1, source_target_pairs={{0,0},{1,1},{2,32},{3,33},{4,64},{5,65},{6,96},{7,97},{8,128},{9,1... | collective-permute-start | bytes 147464 | tf_op jit(solution)/shard_map/ppermute | solution.py:119
  117.9 14.3 %collective-permute-done.7 = f32[3,32,128]{2,1,0:T(8,128)S(1)} collective-permute-done((f32[3,32,128]{2,1,0:T(8,128)S(1)}, f32[3,32,128]{2,1,0:T(8,128)S(1)}, u32[]{:S(2)}, u32[]{:S(2)}) %collective-permute-start.7) | collective-permute-done | bytes 49184 | tf_op jit(solution)/shard_map/ppermute | solution.py:119
  132.2 0.0 all-to-all-done.3
  132.2 0.3 copy.44
  132.6 0.1 slice.87
  132.6 0.2 copy.45
  132.8 0.8 reshape.107
  133.7 0.2 copy.46
  133.9 0.2 reshape.108
  134.1 0.5 copy.47
  134.6 1.0 reshape.109
  135.6 0.6 copy.62
  (29 shorter events, 0.5 us)
Async XLA Ops:
  0.6 45.7 %copy-start = (f32[3,32,512]{2,1,0:T(8,128)S(1)}, f32[3,32,512]{2,1,0:T(8,128)}, u32[]{:S(2)}) copy-start(f32[3,32,512]{2,1,0:T(8,128)} %param.7) | copy-start | bytes 589828
  0.6 35.1 %collective-permute-start = (f32[48,256]{1,0:T(8,128)}, f32[48,256]{1,0:T(8,128)S(1)}, u32[]{:S(2)}, u32[]{:S(2)}) collective-permute-start(f32[48,256]{1,0:T(8,128)} %bitcast.102), channel_id=1, source_target_pairs={{0,0},{1,1},{2,2},{3,3},{4,4},{5,5},{6,6},{7,7},{8,128},{9,129},{1... | collective-permute-start | bytes 147464 | tf_op jit(solution)/shard_map/ppermute | solution.py:72
  11.6 24.1 %collective-permute-start.1 = (f32[48,256]{1,0:T(8,128)}, f32[48,256]{1,0:T(8,128)S(1)}, u32[]{:S(2)}, u32[]{:S(2)}) collective-permute-start(f32[48,256]{1,0:T(8,128)} %bitcast.103), channel_id=1, source_target_pairs={{0,32},{1,33},{2,34},{3,35},{4,36},{5,37},{6,38},{7,39},{8,160},{9... | collective-permute-start | bytes 147464 | tf_op jit(solution)/shard_map/ppermute | solution.py:73
  18.7 11.1 %copy-start.1 = (f32[256,128]{1,0:T(8,128)S(1)}, f32[256,128]{1,0:T(8,128)}, u32[]{:S(2)}) copy-start(f32[256,128]{1,0:T(8,128)} %param.5) | copy-start | bytes 393220
  19.7 10.1 %collective-permute-start.2 = (f32[1,352,128]{2,1,0:T(8,128)S(1)}, f32[1,352,128]{2,1,0:T(8,128)S(1)}, u32[]{:S(2)}, u32[]{:S(2)}) collective-permute-start(f32[1,352,128]{2,1,0:T(8,128)S(1)} %maximum_bitcast_fusion), channel_id=1, source_target_pairs={{0,4},{4,0},{1,5},{5,1},{2,6},{6,2},{3,7},{7,3},{8,12},{12,8},{9,1... | collective-permute-start | bytes 540680 | tf_op jit(solution)/shard_map/ppermute | solution.py:31
  22.4 0.7 copy-start.3
  22.4 0.7 copy-start.2
  29.9 14.3 %collective-permute-start.3 = (f32[2,352,128]{2,1,0:T(8,128)S(1)}, f32[2,352,128]{2,1,0:T(8,128)S(1)}, u32[]{:S(2)}, u32[]{:S(2)}) collective-permute-start(f32[2,352,128]{2,1,0:T(8,128)S(1)} %pad_maximum_fusion.2), channel_id=1, source_target_pairs={{0,2},{2,0},{1,3},{3,1},{4,6},{6,4},{5,7},{7,5},{8,10},{10,8},{9,1... | collective-permute-start | bytes 1081352 | tf_op jit(solution)/shard_map/ppermute | solution.py:31
  36.8 27.8 %all-to-all-start = ((f32[8,48,512]{2,1,0:T(8,128)}), f32[8,48,512]{2,1,0:T(8,128)S(1)}, u32[]{:S(2)}, u32[]{:S(2)}) async-start(f32[8,48,512]{2,1,0:T(8,128)} %broadcast_in_dim.29), calls=%async_computation | async-start | bytes 1572864 | tf_op jit(solution)/shard_map/all_to_all | solution.py:27
  44.3 6.7 %collective-permute-start.4 = (f32[4,256,128]{2,1,0:T(8,128)S(1)}, f32[4,256,128]{2,1,0:T(8,128)S(1)}, u32[]{:S(2)}, u32[]{:S(2)}) collective-permute-start(f32[4,256,128]{2,1,0:T(8,128)S(1)} %fusion), channel_id=1, source_target_pairs={{0,1},{1,0},{2,3},{3,2},{4,5},{5,4},{6,7},{7,6},{8,9},{9,8},{10,11... | collective-permute-start | bytes 1572872 | tf_op jit(solution)/shard_map/ppermute | solution.py:31
  46.5 29.0 %collective-permute-start.5 = (f32[4,48,256]{2,1,0:T(8,128)S(1)}, f32[4,48,256]{2,1,0:T(8,128)S(1)}, u32[]{:S(2)}, u32[]{:S(2)}) collective-permute-start(f32[4,48,256]{2,1,0:T(8,128)S(1)} %fusion.18), channel_id=1, source_target_pairs={{0,16},{16,0},{1,17},{17,1},{2,18},{18,2},{3,19},{19,3},{4,20},{20... | collective-permute-start | bytes 589832 | tf_op jit(solution)/shard_map/ppermute | solution.py:31
  67.1 14.4 %all-to-all-start.1 = ((f32[8,48,256]{2,1,0:T(8,128)}), f32[8,48,256]{2,1,0:T(8,128)S(1)}, u32[]{:S(2)}, u32[]{:S(2)}) async-start(f32[8,48,256]{2,1,0:T(8,128)} %bitcast.15), calls=%async_computation.1 | async-start | bytes 786432 | tf_op jit(solution)/shard_map/all_to_all | solution.py:27
  75.6 14.9 %collective-permute-start.6 = (f32[8,48,256]{2,1,0:T(8,128)S(1)}, f32[8,48,256]{2,1,0:T(8,128)S(1)}, u32[]{:S(2)}, u32[]{:S(2)}) collective-permute-start(f32[8,48,256]{2,1,0:T(8,128)S(1)} %pad_maximum_fusion), channel_id=1, source_target_pairs={{0,8},{8,0},{1,9},{9,1},{2,10},{10,2},{3,11},{11,3},{4,12},{12,4},... | collective-permute-start | bytes 1179656 | tf_op jit(solution)/shard_map/ppermute | solution.py:90
  92.4 16.7 %all-to-all-start.2 = ((f32[16,1,1536]{2,1,0:T(1,128)}), f32[16,1,1536]{2,1,0:T(1,128)S(1)}, u32[]{:S(2)}, u32[]{:S(2)}) async-start(f32[16,1,1536]{2,1,0:T(1,128)} %all_to_all.27), calls=%async_computation.2 | async-start | bytes 196608 | tf_op jit(solution)/shard_map/all_to_all | solution.py:27
  110.1 22.1 %all-to-all-start.3 = ((f32[32,1,1920]{2,1,0:T(1,128)}), f32[32,1,1920]{2,1,0:T(1,128)S(1)}, u32[]{:S(2)}, u32[]{:S(2)}) async-start(f32[32,1,1920]{2,1,0:T(1,128)} %all_to_all.24), calls=%async_computation.3 | async-start | bytes 491520 | tf_op jit(solution)/shard_map/all_to_all | solution.py:27
  116.0 16.2 %collective-permute-start.7 = (f32[3,32,128]{2,1,0:T(8,128)S(1)}, f32[3,32,128]{2,1,0:T(8,128)S(1)}, u32[]{:S(2)}, u32[]{:S(2)}) collective-permute-start(f32[3,32,128]{2,1,0:T(8,128)S(1)} %constant_dynamic-slice_fusion), channel_id=1, source_target_pairs={{0,0},{1,1},{2,32},{3,33},{4,64},{5,65},{6,96},{7,97},{8,128},{9,1... | collective-permute-start | bytes 147464 | tf_op jit(solution)/shard_map/ppermute | solution.py:119

commit v7 on v6

--- a/solution.py
+++ b/solution.py
@@ -35,17 +35,18 @@
     return jnp.concatenate([first, second], dim)
 
 
-def digit_swap(flip):
+def digit_swap():
     zh, zl, yh = (lax.axis_size(a) for a in ROW)
-    x, rest = lax.axis_size(COL[:2]), lax.axis_size(COL[2:])
+    x, yl = lax.axis_size(COL[:2]), lax.axis_size(COL[2:4])
     pairs = []
     for a in range(zh):
         for b in range(zl * yh):
             for c in range(x):
-                for d in range(rest):
-                    source = ((a * zl * yh + b) * x + c) * rest + d
-                    target = ((c * zl * yh + (b ^ flip)) * x + a) * rest + d
-                    pairs.append((source, target))
+                for d in range(yl):
+                    for h in range(NCORE):
+                        source = (((a * zl * yh + b) * x + c) * yl + d) * NCORE + h
+                        target = (((a * yl + d) * x + c) * zl * yh + b) * NCORE + h
+                        pairs.append((source, target))
     return pairs
 
 
@@ -59,7 +60,7 @@
 
 
 def shards(ainv, lpanel, kk_inverse, row_blocks, list_len):
-    nx = lax.axis_size(COL[:2])
+    nyl = lax.axis_size(COL[2:4])
     nrows, ncols = lax.axis_size(ROW), lax.axis_size(COL)
     nchips = ncols // NCORE
     rows, sibs, width = lpanel.shape
@@ -68,37 +69,34 @@
     core = lax.axis_index("core")
 
     panel = jnp.transpose(lpanel, (1, 2, 0)).reshape(wide, rows)
-    yh = lax.axis_index("yh")
-    same = lax.ppermute(panel, ROW + COL, digit_swap(0))
-    flip = lax.ppermute(panel, ROW + COL, digit_swap(1))
+    swapped = lax.ppermute(panel, ROW + COL, digit_swap())
 
     tile_mask = tile_masks(row_blocks, list_len, rows * nrows // TILE)
     own_mask = row_mask(tile_mask, lax.axis_index(ROW), rows)
-    pair_mask = row_mask(tile_mask, lax.axis_index(COL[:2] + ROW[1:2]), 2 * rows)
-    pair = [jnp.where(yh == 0, same, flip), jnp.where(yh == 0, flip, same)]
-    pair = jnp.concatenate(pair, 1).reshape(sibs, width, 2 * rows) * pair_mask
-    pair = pair.reshape(wide, 2 * rows)
-    pair = jnp.broadcast_to(pair, (nrows // 2, wide, 2 * rows))
-    factor = exchange(pair, ROW[:2]).reshape(nx, 2, wide, 2 * rows)
+    factor_mask = row_mask(tile_mask, lax.axis_index(ROW[:1] + COL[2:4]), rows)
+    factor = (swapped.reshape(sibs, width, rows) * factor_mask).reshape(wide, rows)
+    factor = jnp.broadcast_to(factor, (nrows, wide, rows))
+    factor = exchange(factor, ROW).reshape(2, 2, nyl * wide, rows)
 
-    load = jnp.concatenate([ainv, panel[:, :cols], panel[:, cols:]], 0)[None]
-    for axis in ("ylh", "yll"):
-        load = doubled(load, axis, 0)
-    ainv = doubled(load[:, :rows], "core", 2)
-    panel_all = jnp.concatenate([load[:, rows : rows + wide], load[:, rows + wide :]], 2)
-    panel_all = doubled(panel_all, "xh", 0)
+    ainv = ainv[None]
+    for axis in ("xh", "xl", "core"):
+        ainv = doubled(ainv, axis, 2 if axis == "core" else 0)
+    panel_all = panel[None]
+    for axis in ("ylh", "yll", "xh"):
+        panel_all = doubled(panel_all, axis, 0)
     panel_far = lax.ppermute(panel_all, "xl", [(0, 1), (1, 0)])
 
     product = 0.0
     for high in range(2):
         for low in range(2):
-            part = factor[:, high, :, low * rows : (low + 1) * rows].reshape(nx * wide, rows)
             block = ainv[2 * low + high]
-            product += lax.dot_general(part, block, (((1,), (1,)), ((), ())), precision=HIGHEST)
-    product = product.reshape(nx, 1, wide, rows)
-    product = jnp.broadcast_to(product, (nx, NCORE, wide, rows)).reshape(nx * NCORE, wide, rows)
-    product = exchange(product, COL[:2] + COL[4:])
-    product = jnp.sum(product.reshape(nx, NCORE, wide, rows), axis=0)
+            product += lax.dot_general(
+                factor[high, low], block, (((1,), (1,)), ((), ())), precision=HIGHEST
+            )
+    product = product.reshape(nyl, 1, wide, rows)
+    product = jnp.broadcast_to(product, (nyl, NCORE, wide, rows)).reshape(-1, wide, rows)
+    product = exchange(product, COL[2:])
+    product = jnp.sum(product.reshape(nyl, NCORE, wide, rows), axis=0)
     both = product.reshape(NCORE, sibs, width, rows) * -own_mask
     pair = both.transpose(1, 0, 2, 3).reshape(sibs, NCORE * width, rows)
 

time: 137 us -> 132 us (0.964)
  waiting for transfers between devices: 60.8 us -> 52.5 us
  starting transfers between devices: 59.8 us -> 63.6 us
    ppermute x2 -> x1, starting transfers between devices: 17.3 us -> 6.72 us  [shards(): swapped = lax.ppermute(panel, ROW + COL, digit_swap())]
    all_to_all x4, waiting for transfers between devices: 28.9 us -> 18.8 us  [exchange(): return lax.all_to_all(blocks, axes, split_axis=0, concat_axis=0, tiled=True)]
    all_to_all x4, starting transfers between devices: 22.6 us -> 30.1 us  [exchange(): return lax.all_to_all(blocks, axes, split_axis=0, concat_axis=0, tiled=True)]
    ppermute x4 -> x6, waiting for transfers between devices: 8.8 us -> 14.9 us  [doubled(): other = lax.ppermute(block, axis, [(0, 1), (1, 0)])]
    ppermute x4 -> x6, starting transfers between devices: 14.9 us -> 20.9 us  [doubled(): other = lax.ppermute(block, axis, [(0, 1), (1, 0)])]
    ppermute x1, waiting for transfers between devices: 8.92 us -> 4.55 us  [shards(): panel_far = lax.ppermute(panel_all, 'xl', [(0, 1), (1, 0)])]
  transfers between devices with their start and end apart: 12 -> 13, of which waited for: 7 -> 7; matrix products, arithmetic and copies ran while one was open for 5% -> 5% of each run, Pallas kernels for 0% -> 0%
where the time goes in v7:
time: 132 us; the launch traced here: 131 us
  starting transfers between devices  63.6 us (48%)
  waiting for transfers between devices  52.5 us (40%)
  local copies, waits for them, and re-layouts  9.12 us (7%)
  matrix products  2.61 us (2%)
  other arithmetic  1.68 us (1%)
    all_to_all x4, starting transfers between devices, exchange(): return lax.all_to_all(blocks, axes, split_axis=0, concat_axis=0, tiled=True)  30.1 us
    ppermute x6, starting transfers between devices, doubled(): other = lax.ppermute(block, axis, [(0, 1), (1, 0)])  20.9 us
    all_to_all x4, waiting for transfers between devices, exchange(): return lax.all_to_all(blocks, axes, split_axis=0, concat_axis=0, tiled=True)  18.8 us
    ppermute x6, waiting for transfers between devices, doubled(): other = lax.ppermute(block, axis, [(0, 1), (1, 0)])  14.9 us
    ppermute x1, waiting for transfers between devices, shards(): ainv_ki = lax.ppermute(half, ROW + COL, transposed(nrows))  14.3 us
    ppermute x1, starting transfers between devices, shards(): swapped = lax.ppermute(panel, ROW + COL, digit_swap())  6.72 us
    ppermute x1, waiting for transfers between devices, shards(): panel_far = lax.ppermute(panel_all, 'xl', [(0, 1), (1, 0)])  4.55 us
    ppermute x1, starting transfers between devices, shards(): panel_far = lax.ppermute(panel_all, 'xl', [(0, 1), (1, 0)])  4.01 us
  transfers between devices with their start and end apart: 13, of which 7 were waited for; matrix products, arithmetic and copies ran while one was open for 5% of the time, Pallas kernels for 0%

profile of v7, /device:TPU:12, one launch (start us, length us, event | category | flops | bytes accessed | tf_op | source)
XLA Modules:
  0.0 130.7 jit_solution(1997427524801567750)
XLA Ops:
  0.6 0.0 copy-start
  0.6 2.5 %collective-permute-start.1 = (f32[1,256,128]{2,1,0:T(8,128)}, f32[1,256,128]{2,1,0:T(8,128)S(1)}, u32[]{:S(2)}, u32[]{:S(2)}) collective-permute-start(f32[1,256,128]{2,1,0:T(8,128)} %bitcast.106), channel_id=1, source_target_pairs={{0,16},{16,0},{1,17},{17,1},{2,18},{18,2},{3,19},{19,3},{4,20},{20... | collective-permute-start | bytes 393224 | tf_op jit(solution)/shard_map/ppermute | solution.py:31
  3.2 6.7 %collective-permute-start = (f32[48,256]{1,0:T(8,128)}, f32[48,256]{1,0:T(8,128)S(1)}, u32[]{:S(2)}, u32[]{:S(2)}) collective-permute-start(f32[48,256]{1,0:T(8,128)} %bitcast.107), channel_id=1, source_target_pairs={{0,0},{1,1},{2,32},{3,33},{4,64},{5,65},{6,96},{7,97},{8,8},{9,9},... | collective-permute-start | bytes 147464 | tf_op jit(solution)/shard_map/ppermute | solution.py:72
  9.9 4.3 %collective-permute-start.4 = (f32[1,48,256]{2,1,0:T(8,128)}, f32[1,48,256]{2,1,0:T(8,128)S(1)}, u32[]{:S(2)}, u32[]{:S(2)}) collective-permute-start(f32[1,48,256]{2,1,0:T(8,128)} %bitcast.108), channel_id=1, source_target_pairs={{0,4},{4,0},{1,5},{5,1},{2,6},{6,2},{3,7},{7,3},{8,12},{12,8},{9,1... | collective-permute-start | bytes 147464 | tf_op jit(solution)/shard_map/ppermute | solution.py:31
  14.3 0.6 copy-done.4
  14.9 0.1 iota_compare_fusion.1
  15.0 0.1 fusion.18
  15.1 0.1 dynamic-slice_negate_fusion
  15.2 0.1 broadcast_bitcast_fusion.1
  15.2 0.0 collective-permute-done
  15.3 1.0 broadcast_in_dim.29
  16.2 11.6 %all-to-all-start = ((f32[16,48,256]{2,1,0:T(8,128)}), f32[16,48,256]{2,1,0:T(8,128)S(1)}, u32[]{:S(2)}, u32[]{:S(2)}) async-start(f32[16,48,256]{2,1,0:T(8,128)} %broadcast_in_dim.29), calls=%async_computation | async-start | bytes 1572864 | tf_op jit(solution)/shard_map/all_to_all | solution.py:27
  27.8 0.0 collective-permute-done.1
  27.8 0.0 copy-done.1
  27.8 0.0 copy-start.2
  27.9 4.0 %collective-permute-start.2 = (f32[2,256,128]{2,1,0:T(8,128)S(1)}, f32[2,256,128]{2,1,0:T(8,128)S(1)}, u32[]{:S(2)}, u32[]{:S(2)}) collective-permute-start(f32[2,256,128]{2,1,0:T(8,128)S(1)} %pad_maximum_fusion.4), channel_id=1, source_target_pairs={{0,8},{8,0},{1,9},{9,1},{2,10},{10,2},{3,11},{11,3},{4,12},{12,4},... | collective-permute-start | bytes 786440 | tf_op jit(solution)/shard_map/ppermute | solution.py:31
  31.9 0.0 collective-permute-done.4
  31.9 0.0 copy-done.2
  31.9 5.1 %collective-permute-done.2 = f32[2,256,128]{2,1,0:T(8,128)S(1)} collective-permute-done((f32[2,256,128]{2,1,0:T(8,128)S(1)}, f32[2,256,128]{2,1,0:T(8,128)S(1)}, u32[]{:S(2)}, u32[]{:S(2)}) %collective-permute-start.2) | collective-permute-done | bytes 262176 | tf_op jit(solution)/shard_map/ppermute | solution.py:31
  37.1 1.9 %collective-permute-start.3 = (f32[4,256,128]{2,1,0:T(8,128)S(1)}, f32[4,256,128]{2,1,0:T(8,128)S(1)}, u32[]{:S(2)}, u32[]{:S(2)}) collective-permute-start(f32[4,256,128]{2,1,0:T(8,128)S(1)} %pad_maximum_fusion), channel_id=1, source_target_pairs={{0,1},{1,0},{2,3},{3,2},{4,5},{5,4},{6,7},{7,6},{8,9},{9,8},{10,11... | collective-permute-start | bytes 1572872 | tf_op jit(solution)/shard_map/ppermute | solution.py:31
  39.1 3.2 %collective-permute-start.5 = (f32[2,48,256]{2,1,0:T(8,128)S(1)}, f32[2,48,256]{2,1,0:T(8,128)S(1)}, u32[]{:S(2)}, u32[]{:S(2)}) collective-permute-start(f32[2,48,256]{2,1,0:T(8,128)S(1)} %pad_maximum_fusion.7), channel_id=1, source_target_pairs={{0,2},{2,0},{1,3},{3,1},{4,6},{6,4},{5,7},{7,5},{8,10},{10,8},{9,1... | collective-permute-start | bytes 294920 | tf_op jit(solution)/shard_map/ppermute | solution.py:31
  42.3 9.8 %collective-permute-done.5 = f32[2,48,256]{2,1,0:T(8,128)S(1)} collective-permute-done((f32[2,48,256]{2,1,0:T(8,128)S(1)}, f32[2,48,256]{2,1,0:T(8,128)S(1)}, u32[]{:S(2)}, u32[]{:S(2)}) %collective-permute-start.5) | collective-permute-done | bytes 98336 | tf_op jit(solution)/shard_map/ppermute | solution.py:31
  52.1 4.9 %collective-permute-start.6 = (f32[4,48,256]{2,1,0:T(8,128)S(1)}, f32[4,48,256]{2,1,0:T(8,128)}, u32[]{:S(2)}, u32[]{:S(2)}) collective-permute-start(f32[4,48,256]{2,1,0:T(8,128)S(1)} %pad_maximum_fusion.6), channel_id=1, source_target_pairs={{0,16},{16,0},{1,17},{17,1},{2,18},{18,2},{3,19},{19,3},{4,20},{20... | collective-permute-start | bytes 589832 | tf_op jit(solution)/shard_map/ppermute | solution.py:31
  57.0 0.0 collective-permute-done.3
  57.0 0.1 broadcast_select_fusion
  57.1 1.7 %all-to-all-done = f32[16,48,256]{2,1,0:T(8,128)S(1)} async-done(((f32[16,48,256]{2,1,0:T(8,128)}), f32[16,48,256]{2,1,0:T(8,128)S(1)}, u32[]{:S(2)}, u32[]{:S(2)}) %all-to-all-start) | async-done | bytes 786464 | tf_op jit(solution)/shard_map/all_to_all | solution.py:27
  58.8 0.4 fusion.12
  59.2 0.4 convolution_add_fusion.2
  59.7 0.4 convolution_add_fusion.1
  60.1 0.4 convolution_add_fusion
  60.5 0.8 broadcast_in_dim.32
  61.3 3.4 %all-to-all-start.1 = ((f32[8,48,256]{2,1,0:T(8,128)}), f32[8,48,256]{2,1,0:T(8,128)S(1)}, u32[]{:S(2)}, u32[]{:S(2)}) async-start(f32[8,48,256]{2,1,0:T(8,128)} %bitcast.14), calls=%async_computation.1 | async-start | bytes 786432 | tf_op jit(solution)/shard_map/all_to_all | solution.py:27
  64.7 0.1 broadcast_bitcast_fusion
  64.8 0.1 constant_dynamic-slice_fusion.2
  64.9 0.1 reshape.96
  65.0 0.0 collective-permute-done.6
  65.0 1.0 broadcast_select_fusion.5
  66.0 4.0 %collective-permute-start.7 = (f32[8,48,256]{2,1,0:T(8,128)S(1)}, f32[8,48,256]{2,1,0:T(8,128)S(1)}, u32[]{:S(2)}, u32[]{:S(2)}) collective-permute-start(f32[8,48,256]{2,1,0:T(8,128)S(1)} %pad_maximum_fusion.1), channel_id=1, source_target_pairs={{0,8},{8,0},{1,9},{9,1},{2,10},{10,2},{3,11},{11,3},{4,12},{12,4},... | collective-permute-start | bytes 1179656 | tf_op jit(solution)/shard_map/ppermute | solution.py:87
  70.0 4.6 %all-to-all-done.1 = f32[8,48,256]{2,1,0:T(8,128)S(1)} async-done(((f32[8,48,256]{2,1,0:T(8,128)}), f32[8,48,256]{2,1,0:T(8,128)S(1)}, u32[]{:S(2)}, u32[]{:S(2)}) %all-to-all-start.1) | async-done | bytes 393248 | tf_op jit(solution)/shard_map/all_to_all | solution.py:27
  74.7 4.6 %collective-permute-done.7 = f32[8,48,256]{2,1,0:T(8,128)S(1)} collective-permute-done((f32[8,48,256]{2,1,0:T(8,128)S(1)}, f32[8,48,256]{2,1,0:T(8,128)S(1)}, u32[]{:S(2)}, u32[]{:S(2)}) %collective-permute-start.7) | collective-permute-done | bytes 393248 | tf_op jit(solution)/shard_map/ppermute | solution.py:87
  79.3 0.5 fusion
  79.7 0.5 select_bitcast_fusion.1
  80.3 0.9 all_to_all.27
  81.1 7.8 %all-to-all-start.2 = ((f32[16,1,1536]{2,1,0:T(1,128)}), f32[16,1,1536]{2,1,0:T(1,128)S(1)}, u32[]{:S(2)}, u32[]{:S(2)}) async-start(f32[16,1,1536]{2,1,0:T(1,128)} %all_to_all.27), calls=%async_computation.2 | async-start | bytes 196608 | tf_op jit(solution)/shard_map/all_to_all | solution.py:27
  89.0 0.2 copy.41
  89.2 0.2 select_n.152
  89.4 0.1 copy.42
  89.6 0.1 copy.43
  89.7 12.5 %all-to-all-done.2 = f32[16,1,1536]{2,1,0:T(1,128)S(1)} async-done(((f32[16,1,1536]{2,1,0:T(1,128)}), f32[16,1,1536]{2,1,0:T(1,128)S(1)}, u32[]{:S(2)}, u32[]{:S(2)}) %all-to-all-start.2) | async-done | bytes 98336 | tf_op jit(solution)/shard_map/all_to_all | solution.py:27
  102.2 0.1 reduce_sum.19
  102.3 0.9 all_to_all.24
  103.2 7.3 %all-to-all-start.3 = ((f32[32,1,1920]{2,1,0:T(1,128)}), f32[32,1,1920]{2,1,0:T(1,128)S(1)}, u32[]{:S(2)}, u32[]{:S(2)}) async-start(f32[32,1,1920]{2,1,0:T(1,128)} %all_to_all.24), calls=%async_computation.3 | async-start | bytes 491520 | tf_op jit(solution)/shard_map/all_to_all | solution.py:27
  110.5 1.9 %collective-permute-start.8 = (f32[3,32,128]{2,1,0:T(8,128)S(1)}, f32[3,32,128]{2,1,0:T(8,128)S(1)}, u32[]{:S(2)}, u32[]{:S(2)}) collective-permute-start(f32[3,32,128]{2,1,0:T(8,128)S(1)} %constant_dynamic-slice_fusion), channel_id=1, source_target_pairs={{0,0},{1,1},{2,32},{3,33},{4,64},{5,65},{6,96},{7,97},{8,128},{9,1... | collective-permute-start | bytes 147464 | tf_op jit(solution)/shard_map/ppermute | solution.py:117
  112.4 14.3 %collective-permute-done.8 = f32[3,32,128]{2,1,0:T(8,128)S(1)} collective-permute-done((f32[3,32,128]{2,1,0:T(8,128)S(1)}, f32[3,32,128]{2,1,0:T(8,128)S(1)}, u32[]{:S(2)}, u32[]{:S(2)}) %collective-permute-start.8) | collective-permute-done | bytes 49184 | tf_op jit(solution)/shard_map/ppermute | solution.py:117
  126.7 0.0 all-to-all-done.3
  126.7 0.3 copy.44
  127.1 0.1 slice.61
  127.2 0.2 copy.45
  127.3 0.8 reshape.107
  128.2 0.2 copy.46
  128.4 0.2 reshape.108
  128.7 0.5 copy.47
  129.1 1.0 reshape.109
  130.1 0.6 copy.62
  (30 shorter events, 0.4 us)
Async XLA Ops:
  0.6 64.2 %copy-start = (f32[3,32,512]{2,1,0:T(8,128)S(1)}, f32[3,32,512]{2,1,0:T(8,128)}, u32[]{:S(2)}) copy-start(f32[3,32,512]{2,1,0:T(8,128)} %param.7) | copy-start | bytes 589828
  0.6 27.1 %collective-permute-start.1 = (f32[1,256,128]{2,1,0:T(8,128)}, f32[1,256,128]{2,1,0:T(8,128)S(1)}, u32[]{:S(2)}, u32[]{:S(2)}) collective-permute-start(f32[1,256,128]{2,1,0:T(8,128)} %bitcast.106), channel_id=1, source_target_pairs={{0,16},{16,0},{1,17},{17,1},{2,18},{18,2},{3,19},{19,3},{4,20},{20... | collective-permute-start | bytes 393224 | tf_op jit(solution)/shard_map/ppermute | solution.py:31
  3.2 12.1 %collective-permute-start = (f32[48,256]{1,0:T(8,128)}, f32[48,256]{1,0:T(8,128)S(1)}, u32[]{:S(2)}, u32[]{:S(2)}) collective-permute-start(f32[48,256]{1,0:T(8,128)} %bitcast.107), channel_id=1, source_target_pairs={{0,0},{1,1},{2,32},{3,33},{4,64},{5,65},{6,96},{7,97},{8,8},{9,9},... | collective-permute-start | bytes 147464 | tf_op jit(solution)/shard_map/ppermute | solution.py:72
  9.9 22.0 %collective-permute-start.4 = (f32[1,48,256]{2,1,0:T(8,128)}, f32[1,48,256]{2,1,0:T(8,128)S(1)}, u32[]{:S(2)}, u32[]{:S(2)}) collective-permute-start(f32[1,48,256]{2,1,0:T(8,128)} %bitcast.108), channel_id=1, source_target_pairs={{0,4},{4,0},{1,5},{5,1},{2,6},{6,2},{3,7},{7,3},{8,12},{12,8},{9,1... | collective-permute-start | bytes 147464 | tf_op jit(solution)/shard_map/ppermute | solution.py:31
  14.2 0.7 copy-start.4
  14.3 0.7 copy-start.3
  16.2 11.6 %copy-start.1 = (f32[256,128]{1,0:T(8,128)S(1)}, f32[256,128]{1,0:T(8,128)}, u32[]{:S(2)}) copy-start(f32[256,128]{1,0:T(8,128)} %param.5) | copy-start | bytes 393220
  16.2 42.6 %all-to-all-start = ((f32[16,48,256]{2,1,0:T(8,128)}), f32[16,48,256]{2,1,0:T(8,128)S(1)}, u32[]{:S(2)}, u32[]{:S(2)}) async-start(f32[16,48,256]{2,1,0:T(8,128)} %broadcast_in_dim.29), calls=%async_computation | async-start | bytes 1572864 | tf_op jit(solution)/shard_map/all_to_all | solution.py:27
  27.8 4.1 %copy-start.2 = (f32[256,3,16]{0,2,1:T(8,128)S(1)}, f32[256,3,16]{0,2,1:T(8,128)}, u32[]{:S(2)}) copy-start(f32[256,3,16]{0,2,1:T(8,128)} %param.6) | copy-start | bytes 147460
  27.9 9.2 %collective-permute-start.2 = (f32[2,256,128]{2,1,0:T(8,128)S(1)}, f32[2,256,128]{2,1,0:T(8,128)S(1)}, u32[]{:S(2)}, u32[]{:S(2)}) collective-permute-start(f32[2,256,128]{2,1,0:T(8,128)S(1)} %pad_maximum_fusion.4), channel_id=1, source_target_pairs={{0,8},{8,0},{1,9},{9,1},{2,10},{10,2},{3,11},{11,3},{4,12},{12,4},... | collective-permute-start | bytes 786440 | tf_op jit(solution)/shard_map/ppermute | solution.py:31
  37.1 19.9 %collective-permute-start.3 = (f32[4,256,128]{2,1,0:T(8,128)S(1)}, f32[4,256,128]{2,1,0:T(8,128)S(1)}, u32[]{:S(2)}, u32[]{:S(2)}) collective-permute-start(f32[4,256,128]{2,1,0:T(8,128)S(1)} %pad_maximum_fusion), channel_id=1, source_target_pairs={{0,1},{1,0},{2,3},{3,2},{4,5},{5,4},{6,7},{7,6},{8,9},{9,8},{10,11... | collective-permute-start | bytes 1572872 | tf_op jit(solution)/shard_map/ppermute | solution.py:31
  39.1 13.0 %collective-permute-start.5 = (f32[2,48,256]{2,1,0:T(8,128)S(1)}, f32[2,48,256]{2,1,0:T(8,128)S(1)}, u32[]{:S(2)}, u32[]{:S(2)}) collective-permute-start(f32[2,48,256]{2,1,0:T(8,128)S(1)} %pad_maximum_fusion.7), channel_id=1, source_target_pairs={{0,2},{2,0},{1,3},{3,1},{4,6},{6,4},{5,7},{7,5},{8,10},{10,8},{9,1... | collective-permute-start | bytes 294920 | tf_op jit(solution)/shard_map/ppermute | solution.py:31
  52.1 12.9 %collective-permute-start.6 = (f32[4,48,256]{2,1,0:T(8,128)S(1)}, f32[4,48,256]{2,1,0:T(8,128)}, u32[]{:S(2)}, u32[]{:S(2)}) collective-permute-start(f32[4,48,256]{2,1,0:T(8,128)S(1)} %pad_maximum_fusion.6), channel_id=1, source_target_pairs={{0,16},{16,0},{1,17},{17,1},{2,18},{18,2},{3,19},{19,3},{4,20},{20... | collective-permute-start | bytes 589832 | tf_op jit(solution)/shard_map/ppermute | solution.py:31
  61.3 13.3 %all-to-all-start.1 = ((f32[8,48,256]{2,1,0:T(8,128)}), f32[8,48,256]{2,1,0:T(8,128)S(1)}, u32[]{:S(2)}, u32[]{:S(2)}) async-start(f32[8,48,256]{2,1,0:T(8,128)} %bitcast.14), calls=%async_computation.1 | async-start | bytes 786432 | tf_op jit(solution)/shard_map/all_to_all | solution.py:27
  66.0 13.3 %collective-permute-start.7 = (f32[8,48,256]{2,1,0:T(8,128)S(1)}, f32[8,48,256]{2,1,0:T(8,128)S(1)}, u32[]{:S(2)}, u32[]{:S(2)}) collective-permute-start(f32[8,48,256]{2,1,0:T(8,128)S(1)} %pad_maximum_fusion.1), channel_id=1, source_target_pairs={{0,8},{8,0},{1,9},{9,1},{2,10},{10,2},{3,11},{11,3},{4,12},{12,4},... | collective-permute-start | bytes 1179656 | tf_op jit(solution)/shard_map/ppermute | solution.py:87
  81.1 21.1 %all-to-all-start.2 = ((f32[16,1,1536]{2,1,0:T(1,128)}), f32[16,1,1536]{2,1,0:T(1,128)S(1)}, u32[]{:S(2)}, u32[]{:S(2)}) async-start(f32[16,1,1536]{2,1,0:T(1,128)} %all_to_all.27), calls=%async_computation.2 | async-start | bytes 196608 | tf_op jit(solution)/shard_map/all_to_all | solution.py:27
  103.2 23.6 %all-to-all-start.3 = ((f32[32,1,1920]{2,1,0:T(1,128)}), f32[32,1,1920]{2,1,0:T(1,128)S(1)}, u32[]{:S(2)}, u32[]{:S(2)}) async-start(f32[32,1,1920]{2,1,0:T(1,128)} %all_to_all.24), calls=%async_computation.3 | async-start | bytes 491520 | tf_op jit(solution)/shard_map/all_to_all | solution.py:27
  110.5 16.2 %collective-permute-start.8 = (f32[3,32,128]{2,1,0:T(8,128)S(1)}, f32[3,32,128]{2,1,0:T(8,128)S(1)}, u32[]{:S(2)}, u32[]{:S(2)}) collective-permute-start(f32[3,32,128]{2,1,0:T(8,128)S(1)} %constant_dynamic-slice_fusion), channel_id=1, source_target_pairs={{0,0},{1,1},{2,32},{3,33},{4,64},{5,65},{6,96},{7,97},{8,128},{9,1... | collective-permute-start | bytes 147464 | tf_op jit(solution)/shard_map/ppermute | solution.py:117

commit v8 on v4

--- a/solution.py
+++ b/solution.py
@@ -73,7 +73,6 @@
     tile_mask = tile_masks(row_blocks, list_len, rows * nrows // TILE)
     own_mask = row_mask(tile_mask, lax.axis_index(ROW), rows)
     factor_mask = row_mask(tile_mask, lax.axis_index(COL[:2] + ROW[1:]), rows)
-
     factor = (swapped.reshape(sibs, width, rows) * factor_mask).reshape(wide, rows)
     factor = jnp.broadcast_to(factor, (nrows, wide, rows))
     factor = exchange(factor, ROW).reshape(nx, 2, 2, wide, rows)
@@ -81,41 +80,48 @@
     ainv = ainv[None]
     for axis in ("ylh", "yll", "core"):
         ainv = doubled(ainv, axis, 2 if axis == "core" else 0)
-
     panel_all = panel[None]
-    for axis in ("ylh", "yll", "xh", "xl"):
+    for axis in ("ylh", "xh", "xl"):
         panel_all = doubled(panel_all, axis, 0)
-    panel_all = panel_all.reshape(2, 2, 2, 2, sibs, width, rows)
+    panel_far = lax.ppermute(panel_all, "yll", [(0, 1), (1, 0)])
 
     product = 0.0
     for high in range(2):
         for low in range(2):
+            block = ainv[2 * low + high]
             part = factor[:, high, low].reshape(nx * wide, rows)
-            block = ainv[2 * low + high]
             product += lax.dot_general(part, block, (((1,), (1,)), ((), ())), precision=HIGHEST)
     product = product.reshape(nx, 1, wide, rows)
-    product = jnp.broadcast_to(product, (nx, NCORE, wide, rows)).reshape(nx * NCORE, wide, rows)
+    product = jnp.broadcast_to(product, (nx, NCORE, wide, rows)).reshape(-1, wide, rows)
     product = exchange(product, COL[:2] + COL[4:])
     product = jnp.sum(product.reshape(nx, NCORE, wide, rows), axis=0)
     both = product.reshape(NCORE, sibs, width, rows) * -own_mask
+    pair = both.transpose(1, 0, 2, 3).reshape(sibs, NCORE * width, rows)
 
-    term = jnp.einsum("cebdsvi,kswi->ecdbsvkw", panel_all, both, precision=HIGHEST)
+    terms = []
+    for source in (panel_all, panel_far):
+        source = source.reshape(2, 2, 2, sibs, width, rows)
+        terms.append(jnp.einsum("cedsvi,swi->ecdsvw", source, pair, precision=HIGHEST))
+    yll = lax.axis_index("yll")
+    first = jnp.where(yll == 0, terms[0], terms[1])
+    second = jnp.where(yll == 0, terms[1], terms[0])
+    term = jnp.stack([first, second], 3)
     term = exchange(term.reshape(nrows, -1), ROW)
-    diag = jnp.sum(term, axis=0)
+    own = lax.dynamic_slice_in_dim(kk_inverse, core * width, width, 1)
+    own = lax.dynamic_slice_in_dim(own, lax.axis_index(COL[:4]) * NCORE * width, NCORE * width, 2)
+    diag = own.reshape(-1) - jnp.sum(term, axis=0)
 
-    half = lax.dynamic_slice_in_dim(both, core * cols, cols, 3)
+    half = lax.dynamic_slice_in_dim(pair, core * cols, cols, 2)
     ainv_ki = lax.ppermute(half, ROW + COL, transposed(nrows))
-    diag, ainv_ki = lax.optimization_barrier((diag, ainv_ki))
-    ainv_ki = ainv_ki.transpose(1, 0, 2, 3).reshape(sibs, NCORE * width, cols)
 
     share = rows // ncols
     split = jnp.where(core == 0, both[0], both[1]).reshape(wide, ncols, share)
     split = split.transpose(1, 0, 2).reshape(ncols, wide * share)
     joined = jnp.concatenate([jnp.broadcast_to(diag, (ncols, diag.size)), split], 1)
     joined = exchange(joined, COL)
-    diag = joined[:, : diag.size].reshape(nchips, NCORE, sibs, width, NCORE * width)
-    ainv_kk = kk_inverse - diag.transpose(2, 1, 3, 0, 4).reshape(kk_inverse.shape)
-    split = joined[:, diag.size // ncols :].reshape(ncols, sibs, width, share)
+    diag = joined[:, : own.size].reshape(nchips, NCORE, sibs, width, NCORE * width)
+    ainv_kk = diag.transpose(2, 1, 3, 0, 4).reshape(kk_inverse.shape)
+    split = joined[:, own.size :].reshape(ncols, sibs, width, share)
     ainv_ik = split.transpose(3, 1, 0, 2).reshape(share, sibs, -1)
     return ainv_ik, ainv_kk, ainv_ki
 

time: 141 us -> 149 us (1.057)
  the two profiles are of different devices: /device:TPU:1 before, /device:TPU:12 now
where the time goes in v8:
time: 149 us; the launch traced here: 148 us
  starting transfers between devices  71.1 us (48%)
  waiting for transfers between devices  62.6 us (42%)
  local copies, waits for them, and re-layouts  9.19 us (6%)
  matrix products  2.62 us (2%)
  other arithmetic  1.67 us (1%)
    all_to_all x4, starting transfers between devices, exchange(): return lax.all_to_all(blocks, axes, split_axis=0, concat_axis=0, tiled=True)  34.6 us
    ppermute x6, waiting for transfers between devices, doubled(): other = lax.ppermute(block, axis, [(0, 1), (1, 0)])  25.3 us
    ppermute x6, starting transfers between devices, doubled(): other = lax.ppermute(block, axis, [(0, 1), (1, 0)])  21.5 us
    all_to_all x4, waiting for transfers between devices, exchange(): return lax.all_to_all(blocks, axes, split_axis=0, concat_axis=0, tiled=True)  14.9 us
    ppermute x1, waiting for transfers between devices, shards(): ainv_ki = lax.ppermute(half, ROW + COL, transposed(nrows))  14.3 us
    ppermute x1, starting transfers between devices, shards(): swapped = lax.ppermute(panel, ROW + COL, digit_swap())  11 us
    ppermute x1, waiting for transfers between devices, shards(): panel_far = lax.ppermute(panel_all, 'yll', [(0, 1), (1, 0)])  8.17 us
  transfers between devices with their start and end apart: 13, of which 6 were waited for; matrix products, arithmetic and copies ran while one was open for 4% of the time, Pallas kernels for 0%

profile of v8, /device:TPU:12, one launch (start us, length us, event | category | flops | bytes accessed | tf_op | source)
XLA Modules:
  0.0 148.3 jit_solution(17217799290048424746)
XLA Ops:
  0.6 0.0 copy-start
  0.6 11.0 %collective-permute-start = (f32[48,256]{1,0:T(8,128)}, f32[48,256]{1,0:T(8,128)S(1)}, u32[]{:S(2)}, u32[]{:S(2)}) collective-permute-start(f32[48,256]{1,0:T(8,128)} %bitcast.104), channel_id=1, source_target_pairs={{0,0},{1,1},{2,2},{3,3},{4,4},{5,5},{6,6},{7,7},{8,128},{9,129},{1... | collective-permute-start | bytes 147464 | tf_op jit(solution)/shard_map/ppermute | solution.py:71
  11.6 4.5 %collective-permute-start.1 = (f32[1,256,128]{2,1,0:T(8,128)}, f32[1,256,128]{2,1,0:T(8,128)S(1)}, u32[]{:S(2)}, u32[]{:S(2)}) collective-permute-start(f32[1,256,128]{2,1,0:T(8,128)} %bitcast.103), channel_id=1, source_target_pairs={{0,4},{4,0},{1,5},{5,1},{2,6},{6,2},{3,7},{7,3},{8,12},{12,8},{9,1... | collective-permute-start | bytes 393224 | tf_op jit(solution)/shard_map/ppermute | solution.py:31
  16.2 2.2 %collective-permute-start.4 = (f32[1,48,256]{2,1,0:T(8,128)}, f32[1,48,256]{2,1,0:T(8,128)S(1)}, u32[]{:S(2)}, u32[]{:S(2)}) collective-permute-start(f32[1,48,256]{2,1,0:T(8,128)} %bitcast.105), channel_id=1, source_target_pairs={{0,4},{4,0},{1,5},{5,1},{2,6},{6,2},{3,7},{7,3},{8,12},{12,8},{9,1... | collective-permute-start | bytes 147464 | tf_op jit(solution)/shard_map/ppermute | solution.py:31
  18.4 0.6 copy-done.4
  19.1 0.1 iota_compare_fusion.1
  19.2 0.1 fusion.18
  19.3 0.1 dynamic-slice_negate_fusion
  19.4 0.1 broadcast_bitcast_fusion.1
  19.4 0.0 collective-permute-done
  19.4 1.0 broadcast_in_dim.29
  20.4 7.4 %all-to-all-start = ((f32[16,48,256]{2,1,0:T(8,128)}), f32[16,48,256]{2,1,0:T(8,128)S(1)}, u32[]{:S(2)}, u32[]{:S(2)}) async-start(f32[16,48,256]{2,1,0:T(8,128)} %broadcast_in_dim.29), calls=%async_computation | async-start | bytes 1572864 | tf_op jit(solution)/shard_map/all_to_all | solution.py:27
  27.8 0.0 collective-permute-done.1
  27.8 0.0 copy-done.1
  27.9 0.0 copy-start.2
  27.9 3.4 %collective-permute-start.2 = (f32[2,256,128]{2,1,0:T(8,128)S(1)}, f32[2,256,128]{2,1,0:T(8,128)S(1)}, u32[]{:S(2)}, u32[]{:S(2)}) collective-permute-start(f32[2,256,128]{2,1,0:T(8,128)S(1)} %pad_maximum_fusion.4), channel_id=1, source_target_pairs={{0,2},{2,0},{1,3},{3,1},{4,6},{6,4},{5,7},{7,5},{8,10},{10,8},{9,1... | collective-permute-start | bytes 786440 | tf_op jit(solution)/shard_map/ppermute | solution.py:31
  31.3 0.1 broadcast_bitcast_fusion
  31.4 0.0 collective-permute-done.4
  31.4 20.5 %collective-permute-done.2 = f32[2,256,128]{2,1,0:T(8,128)S(1)} collective-permute-done((f32[2,256,128]{2,1,0:T(8,128)S(1)}, f32[2,256,128]{2,1,0:T(8,128)S(1)}, u32[]{:S(2)}, u32[]{:S(2)}) %collective-permute-start.2) | collective-permute-done | bytes 262176 | tf_op jit(solution)/shard_map/ppermute | solution.py:31
  52.0 1.9 %collective-permute-start.3 = (f32[4,256,128]{2,1,0:T(8,128)S(1)}, f32[4,256,128]{2,1,0:T(8,128)S(1)}, u32[]{:S(2)}, u32[]{:S(2)}) collective-permute-start(f32[4,256,128]{2,1,0:T(8,128)S(1)} %pad_maximum_fusion), channel_id=1, source_target_pairs={{0,1},{1,0},{2,3},{3,2},{4,5},{5,4},{6,7},{7,6},{8,9},{9,8},{10,11... | collective-permute-start | bytes 1572872 | tf_op jit(solution)/shard_map/ppermute | solution.py:31
  54.0 3.7 %collective-permute-start.5 = (f32[2,48,256]{2,1,0:T(8,128)S(1)}, f32[2,48,256]{2,1,0:T(8,128)S(1)}, u32[]{:S(2)}, u32[]{:S(2)}) collective-permute-start(f32[2,48,256]{2,1,0:T(8,128)S(1)} %pad_maximum_fusion.7), channel_id=1, source_target_pairs={{0,16},{16,0},{1,17},{17,1},{2,18},{18,2},{3,19},{19,3},{4,20},{20... | collective-permute-start | bytes 294920 | tf_op jit(solution)/shard_map/ppermute | solution.py:31
  57.7 0.1 constant_dynamic-slice_fusion.2
  57.7 0.1 reshape.96
  57.8 4.7 %collective-permute-done.5 = f32[2,48,256]{2,1,0:T(8,128)S(1)} collective-permute-done((f32[2,48,256]{2,1,0:T(8,128)S(1)}, f32[2,48,256]{2,1,0:T(8,128)S(1)}, u32[]{:S(2)}, u32[]{:S(2)}) %collective-permute-start.5) | collective-permute-done | bytes 98336 | tf_op jit(solution)/shard_map/ppermute | solution.py:31
  62.6 5.8 %collective-permute-start.6 = (f32[4,48,256]{2,1,0:T(8,128)S(1)}, f32[4,48,256]{2,1,0:T(8,128)}, u32[]{:S(2)}, u32[]{:S(2)}) collective-permute-start(f32[4,48,256]{2,1,0:T(8,128)S(1)} %pad_maximum_fusion.6), channel_id=1, source_target_pairs={{0,8},{8,0},{1,9},{9,1},{2,10},{10,2},{3,11},{11,3},{4,12},{12,4},... | collective-permute-start | bytes 589832 | tf_op jit(solution)/shard_map/ppermute | solution.py:31
  68.4 0.0 collective-permute-done.3
  68.4 0.1 broadcast_select_fusion
  68.5 0.0 all-to-all-done
  68.5 0.1 fusion.23
  68.6 0.4 fusion.12
  69.0 0.4 convolution_add_fusion.2
  69.4 0.4 convolution_add_fusion.1
  69.9 0.4 convolution_add_fusion
  70.3 0.8 broadcast_in_dim.32
  71.1 4.8 %all-to-all-start.1 = ((f32[8,48,256]{2,1,0:T(8,128)}), f32[8,48,256]{2,1,0:T(8,128)S(1)}, u32[]{:S(2)}, u32[]{:S(2)}) async-start(f32[8,48,256]{2,1,0:T(8,128)} %bitcast.14), calls=%async_computation.1 | async-start | bytes 786432 | tf_op jit(solution)/shard_map/all_to_all | solution.py:27
  75.9 0.0 collective-permute-done.6
  75.9 1.0 broadcast_select_fusion.5
  76.9 2.0 %collective-permute-start.7 = (f32[8,48,256]{2,1,0:T(8,128)S(1)}, f32[8,48,256]{2,1,0:T(8,128)S(1)}, u32[]{:S(2)}, u32[]{:S(2)}) collective-permute-start(f32[8,48,256]{2,1,0:T(8,128)S(1)} %pad_maximum_fusion.1), channel_id=1, source_target_pairs={{0,2},{2,0},{1,3},{3,1},{4,6},{6,4},{5,7},{7,5},{8,10},{10,8},{9,1... | collective-permute-start | bytes 1179656 | tf_op jit(solution)/shard_map/ppermute | solution.py:86
  78.9 2.8 %all-to-all-done.1 = f32[8,48,256]{2,1,0:T(8,128)S(1)} async-done(((f32[8,48,256]{2,1,0:T(8,128)}), f32[8,48,256]{2,1,0:T(8,128)S(1)}, u32[]{:S(2)}, u32[]{:S(2)}) %all-to-all-start.1) | async-done | bytes 393248 | tf_op jit(solution)/shard_map/all_to_all | solution.py:27
  81.7 8.2 %collective-permute-done.7 = f32[8,48,256]{2,1,0:T(8,128)S(1)} collective-permute-done((f32[8,48,256]{2,1,0:T(8,128)S(1)}, f32[8,48,256]{2,1,0:T(8,128)S(1)}, u32[]{:S(2)}, u32[]{:S(2)}) %collective-permute-start.7) | collective-permute-done | bytes 393248 | tf_op jit(solution)/shard_map/ppermute | solution.py:86
  89.9 0.5 fusion
  90.4 0.5 select_bitcast_fusion.1
  90.9 0.9 all_to_all.27
  91.8 10.9 %all-to-all-start.2 = ((f32[16,1,1536]{2,1,0:T(1,128)}), f32[16,1,1536]{2,1,0:T(1,128)S(1)}, u32[]{:S(2)}, u32[]{:S(2)}) async-start(f32[16,1,1536]{2,1,0:T(1,128)} %all_to_all.27), calls=%async_computation.2 | async-start | bytes 196608 | tf_op jit(solution)/shard_map/all_to_all | solution.py:27
  102.7 0.2 copy.41
  102.9 0.2 select_n.152
  103.2 0.1 copy.42
  103.3 0.1 copy.43
  103.4 12.1 %all-to-all-done.2 = f32[16,1,1536]{2,1,0:T(1,128)S(1)} async-done(((f32[16,1,1536]{2,1,0:T(1,128)}), f32[16,1,1536]{2,1,0:T(1,128)S(1)}, u32[]{:S(2)}, u32[]{:S(2)}) %all-to-all-start.2) | async-done | bytes 98336 | tf_op jit(solution)/shard_map/all_to_all | solution.py:27
  115.5 0.1 reduce_sum.19
  115.6 0.9 all_to_all.24
  116.5 11.6 %all-to-all-start.3 = ((f32[32,1,1920]{2,1,0:T(1,128)}), f32[32,1,1920]{2,1,0:T(1,128)S(1)}, u32[]{:S(2)}, u32[]{:S(2)}) async-start(f32[32,1,1920]{2,1,0:T(1,128)} %all_to_all.24), calls=%async_computation.3 | async-start | bytes 491520 | tf_op jit(solution)/shard_map/all_to_all | solution.py:27
  128.1 1.9 %collective-permute-start.8 = (f32[3,32,128]{2,1,0:T(8,128)S(1)}, f32[3,32,128]{2,1,0:T(8,128)S(1)}, u32[]{:S(2)}, u32[]{:S(2)}) collective-permute-start(f32[3,32,128]{2,1,0:T(8,128)S(1)} %constant_dynamic-slice_fusion), channel_id=1, source_target_pairs={{0,0},{1,1},{2,32},{3,33},{4,64},{5,65},{6,96},{7,97},{8,128},{9,1... | collective-permute-start | bytes 147464 | tf_op jit(solution)/shard_map/ppermute | solution.py:115
  130.0 14.3 %collective-permute-done.8 = f32[3,32,128]{2,1,0:T(8,128)S(1)} collective-permute-done((f32[3,32,128]{2,1,0:T(8,128)S(1)}, f32[3,32,128]{2,1,0:T(8,128)S(1)}, u32[]{:S(2)}, u32[]{:S(2)}) %collective-permute-start.8) | collective-permute-done | bytes 49184 | tf_op jit(solution)/shard_map/ppermute | solution.py:115
  144.3 0.0 all-to-all-done.3
  144.3 0.3 copy.44
  144.7 0.1 slice.61
  144.7 0.2 copy.45
  144.9 0.8 reshape.107
  145.8 0.2 copy.46
  146.0 0.2 reshape.108
  146.2 0.5 copy.47
  146.7 1.0 reshape.109
  147.7 0.6 copy.62
  (31 shorter events, 0.4 us)
Async XLA Ops:
  0.6 57.0 %copy-start = (f32[3,32,512]{2,1,0:T(8,128)S(1)}, f32[3,32,512]{2,1,0:T(8,128)}, u32[]{:S(2)}) copy-start(f32[3,32,512]{2,1,0:T(8,128)} %param.7) | copy-start | bytes 589828
  0.6 18.8 %collective-permute-start = (f32[48,256]{1,0:T(8,128)}, f32[48,256]{1,0:T(8,128)S(1)}, u32[]{:S(2)}, u32[]{:S(2)}) collective-permute-start(f32[48,256]{1,0:T(8,128)} %bitcast.104), channel_id=1, source_target_pairs={{0,0},{1,1},{2,2},{3,3},{4,4},{5,5},{6,6},{7,7},{8,128},{9,129},{1... | collective-permute-start | bytes 147464 | tf_op jit(solution)/shard_map/ppermute | solution.py:71
  11.6 16.2 %collective-permute-start.1 = (f32[1,256,128]{2,1,0:T(8,128)}, f32[1,256,128]{2,1,0:T(8,128)S(1)}, u32[]{:S(2)}, u32[]{:S(2)}) collective-permute-start(f32[1,256,128]{2,1,0:T(8,128)} %bitcast.103), channel_id=1, source_target_pairs={{0,4},{4,0},{1,5},{5,1},{2,6},{6,2},{3,7},{7,3},{8,12},{12,8},{9,1... | collective-permute-start | bytes 393224 | tf_op jit(solution)/shard_map/ppermute | solution.py:31
  16.2 15.2 %collective-permute-start.4 = (f32[1,48,256]{2,1,0:T(8,128)}, f32[1,48,256]{2,1,0:T(8,128)S(1)}, u32[]{:S(2)}, u32[]{:S(2)}) collective-permute-start(f32[1,48,256]{2,1,0:T(8,128)} %bitcast.105), channel_id=1, source_target_pairs={{0,4},{4,0},{1,5},{5,1},{2,6},{6,2},{3,7},{7,3},{8,12},{12,8},{9,1... | collective-permute-start | bytes 147464 | tf_op jit(solution)/shard_map/ppermute | solution.py:31
  18.4 0.7 copy-start.4
  18.4 0.7 copy-start.3
  20.4 7.4 %copy-start.1 = (f32[256,128]{1,0:T(8,128)S(1)}, f32[256,128]{1,0:T(8,128)}, u32[]{:S(2)}) copy-start(f32[256,128]{1,0:T(8,128)} %param.5) | copy-start | bytes 393220
  20.4 48.1 %all-to-all-start = ((f32[16,48,256]{2,1,0:T(8,128)}), f32[16,48,256]{2,1,0:T(8,128)S(1)}, u32[]{:S(2)}, u32[]{:S(2)}) async-start(f32[16,48,256]{2,1,0:T(8,128)} %broadcast_in_dim.29), calls=%async_computation | async-start | bytes 1572864 | tf_op jit(solution)/shard_map/all_to_all | solution.py:27
  27.9 3.5 %copy-start.2 = (f32[256,3,16]{0,2,1:T(8,128)S(1)}, f32[256,3,16]{0,2,1:T(8,128)}, u32[]{:S(2)}) copy-start(f32[256,3,16]{0,2,1:T(8,128)} %param.6) | copy-start | bytes 147460
  27.9 24.0 %collective-permute-start.2 = (f32[2,256,128]{2,1,0:T(8,128)S(1)}, f32[2,256,128]{2,1,0:T(8,128)S(1)}, u32[]{:S(2)}, u32[]{:S(2)}) collective-permute-start(f32[2,256,128]{2,1,0:T(8,128)S(1)} %pad_maximum_fusion.4), channel_id=1, source_target_pairs={{0,2},{2,0},{1,3},{3,1},{4,6},{6,4},{5,7},{7,5},{8,10},{10,8},{9,1... | collective-permute-start | bytes 786440 | tf_op jit(solution)/shard_map/ppermute | solution.py:31
  52.0 16.4 %collective-permute-start.3 = (f32[4,256,128]{2,1,0:T(8,128)S(1)}, f32[4,256,128]{2,1,0:T(8,128)S(1)}, u32[]{:S(2)}, u32[]{:S(2)}) collective-permute-start(f32[4,256,128]{2,1,0:T(8,128)S(1)} %pad_maximum_fusion), channel_id=1, source_target_pairs={{0,1},{1,0},{2,3},{3,2},{4,5},{5,4},{6,7},{7,6},{8,9},{9,8},{10,11... | collective-permute-start | bytes 1572872 | tf_op jit(solution)/shard_map/ppermute | solution.py:31
  54.0 8.6 %collective-permute-start.5 = (f32[2,48,256]{2,1,0:T(8,128)S(1)}, f32[2,48,256]{2,1,0:T(8,128)S(1)}, u32[]{:S(2)}, u32[]{:S(2)}) collective-permute-start(f32[2,48,256]{2,1,0:T(8,128)S(1)} %pad_maximum_fusion.7), channel_id=1, source_target_pairs={{0,16},{16,0},{1,17},{17,1},{2,18},{18,2},{3,19},{19,3},{4,20},{20... | collective-permute-start | bytes 294920 | tf_op jit(solution)/shard_map/ppermute | solution.py:31
  62.6 13.3 %collective-permute-start.6 = (f32[4,48,256]{2,1,0:T(8,128)S(1)}, f32[4,48,256]{2,1,0:T(8,128)}, u32[]{:S(2)}, u32[]{:S(2)}) collective-permute-start(f32[4,48,256]{2,1,0:T(8,128)S(1)} %pad_maximum_fusion.6), channel_id=1, source_target_pairs={{0,8},{8,0},{1,9},{9,1},{2,10},{10,2},{3,11},{11,3},{4,12},{12,4},... | collective-permute-start | bytes 589832 | tf_op jit(solution)/shard_map/ppermute | solution.py:31
  71.1 10.6 %all-to-all-start.1 = ((f32[8,48,256]{2,1,0:T(8,128)}), f32[8,48,256]{2,1,0:T(8,128)S(1)}, u32[]{:S(2)}, u32[]{:S(2)}) async-start(f32[8,48,256]{2,1,0:T(8,128)} %bitcast.14), calls=%async_computation.1 | async-start | bytes 786432 | tf_op jit(solution)/shard_map/all_to_all | solution.py:27
  76.9 13.0 %collective-permute-start.7 = (f32[8,48,256]{2,1,0:T(8,128)S(1)}, f32[8,48,256]{2,1,0:T(8,128)S(1)}, u32[]{:S(2)}, u32[]{:S(2)}) collective-permute-start(f32[8,48,256]{2,1,0:T(8,128)S(1)} %pad_maximum_fusion.1), channel_id=1, source_target_pairs={{0,2},{2,0},{1,3},{3,1},{4,6},{6,4},{5,7},{7,5},{8,10},{10,8},{9,1... | collective-permute-start | bytes 1179656 | tf_op jit(solution)/shard_map/ppermute | solution.py:86
  91.8 23.7 %all-to-all-start.2 = ((f32[16,1,1536]{2,1,0:T(1,128)}), f32[16,1,1536]{2,1,0:T(1,128)S(1)}, u32[]{:S(2)}, u32[]{:S(2)}) async-start(f32[16,1,1536]{2,1,0:T(1,128)} %all_to_all.27), calls=%async_computation.2 | async-start | bytes 196608 | tf_op jit(solution)/shard_map/all_to_all | solution.py:27
  116.5 27.8 %all-to-all-start.3 = ((f32[32,1,1920]{2,1,0:T(1,128)}), f32[32,1,1920]{2,1,0:T(1,128)S(1)}, u32[]{:S(2)}, u32[]{:S(2)}) async-start(f32[32,1,1920]{2,1,0:T(1,128)} %all_to_all.24), calls=%async_computation.3 | async-start | bytes 491520 | tf_op jit(solution)/shard_map/all_to_all | solution.py:27
  128.1 16.2 %collective-permute-start.8 = (f32[3,32,128]{2,1,0:T(8,128)S(1)}, f32[3,32,128]{2,1,0:T(8,128)S(1)}, u32[]{:S(2)}, u32[]{:S(2)}) collective-permute-start(f32[3,32,128]{2,1,0:T(8,128)S(1)} %constant_dynamic-slice_fusion), channel_id=1, source_target_pairs={{0,0},{1,1},{2,32},{3,33},{4,64},{5,65},{6,96},{7,97},{8,128},{9,1... | collective-permute-start | bytes 147464 | tf_op jit(solution)/shard_map/ppermute | solution.py:115

commit v9 on v7

--- a/solution.py
+++ b/solution.py
@@ -93,12 +93,14 @@
             product += lax.dot_general(
                 factor[high, low], block, (((1,), (1,)), ((), ())), precision=HIGHEST
             )
-    product = product.reshape(nyl, 1, wide, rows)
-    product = jnp.broadcast_to(product, (nyl, NCORE, wide, rows)).reshape(-1, wide, rows)
-    product = exchange(product, COL[2:])
-    product = jnp.sum(product.reshape(nyl, NCORE, wide, rows), axis=0)
-    both = product.reshape(NCORE, sibs, width, rows) * -own_mask
-    pair = both.transpose(1, 0, 2, 3).reshape(sibs, NCORE * width, rows)
+    product = exchange(product.reshape(nyl, wide, rows), COL[2:4])
+    plain = jnp.sum(product, axis=0)
+    other = lax.ppermute(plain, "core", [(0, 1), (1, 0)])
+    pair = [jnp.where(core == 0, plain, other), jnp.where(core == 0, other, plain)]
+    pair = [block.reshape(sibs, width, rows) for block in pair]
+    pair = -jnp.concatenate(pair, 1)
+    half = lax.dynamic_slice_in_dim(pair, core * cols, cols, 2)
+    pair = pair * own_mask
 
     terms = []
     for source in (panel_all, panel_far):
@@ -113,12 +115,13 @@
     own = lax.dynamic_slice_in_dim(own, lax.axis_index(COL[:4]) * NCORE * width, NCORE * width, 2)
     diag = own.reshape(-1) - jnp.sum(term, axis=0)
 
-    half = lax.dynamic_slice_in_dim(pair, core * cols, cols, 2)
     ainv_ki = lax.ppermute(half, ROW + COL, transposed(nrows))
+    tile = lax.dynamic_slice_in_dim(tile_mask, lax.axis_index(COL), 1, 1)
+    ainv_ki = ainv_ki * tile[:, :, None]
 
     share = rows // ncols
-    split = jnp.where(core == 0, both[0], both[1]).reshape(wide, ncols, share)
-    split = split.transpose(1, 0, 2).reshape(ncols, wide * share)
+    split = -plain.reshape(sibs, width, rows) * own_mask
+    split = split.reshape(wide, ncols, share).transpose(1, 0, 2).reshape(ncols, wide * share)
     joined = jnp.concatenate([jnp.broadcast_to(diag, (ncols, diag.size)), split], 1)
     joined = exchange(joined, COL)
     diag = joined[:, : own.size].reshape(nchips, NCORE, sibs, width, NCORE * width)

time: 132 us -> 147 us (1.11)
  starting transfers between devices: 63.6 us -> 82.5 us
  waiting for transfers between devices: 52.5 us -> 48.5 us
    all_to_all x4, starting transfers between devices: 30.1 us -> 46 us  [exchange(): return lax.all_to_all(blocks, axes, split_axis=0, concat_axis=0, tiled=True)]
    all_to_all x4, waiting for transfers between devices: 18.8 us -> 14.5 us  [exchange(): return lax.all_to_all(blocks, axes, split_axis=0, concat_axis=0, tiled=True)]
    ppermute x0 -> x1, starting transfers between devices: none -> 1.92 us  [shards(): other = lax.ppermute(plain, 'core', [(0, 1), (1, 0)])]
    ppermute x6, waiting for transfers between devices: 14.9 us -> 16.4 us  [doubled(): other = lax.ppermute(block, axis, [(0, 1), (1, 0)])]
  transfers between devices with their start and end apart: 13 -> 14, of which waited for: 7 -> 7; matrix products, arithmetic and copies ran while one was open for 5% -> 3% of each run, Pallas kernels for 0% -> 0%
where the time goes in v9:
time: 147 us; the launch traced here: 146 us
  starting transfers between devices  82.5 us (56%)
  waiting for transfers between devices  48.5 us (33%)
  local copies, waits for them, and re-layouts  8.3 us (6%)
  matrix products  3.32 us (2%)
  other arithmetic  2.28 us (2%)
    all_to_all x4, starting transfers between devices, exchange(): return lax.all_to_all(blocks, axes, split_axis=0, concat_axis=0, tiled=True)  46 us
    ppermute x6, starting transfers between devices, doubled(): other = lax.ppermute(block, axis, [(0, 1), (1, 0)])  21.8 us
    ppermute x6, waiting for transfers between devices, doubled(): other = lax.ppermute(block, axis, [(0, 1), (1, 0)])  16.4 us
    all_to_all x4, waiting for transfers between devices, exchange(): return lax.all_to_all(blocks, axes, split_axis=0, concat_axis=0, tiled=True)  14.5 us
    ppermute x1, waiting for transfers between devices, shards(): ainv_ki = lax.ppermute(half, ROW + COL, transposed(nrows))  13.9 us
    ppermute x1, starting transfers between devices, shards(): swapped = lax.ppermute(panel, ROW + COL, digit_swap())  6.72 us
    ppermute x1, starting transfers between devices, shards(): panel_far = lax.ppermute(panel_all, 'xl', [(0, 1), (1, 0)])  4 us
    ppermute x1, waiting for transfers between devices, shards(): panel_far = lax.ppermute(panel_all, 'xl', [(0, 1), (1, 0)])  3.37 us
  transfers between devices with their start and end apart: 14, of which 7 were waited for; matrix products, arithmetic and copies ran while one was open for 3% of the time, Pallas kernels for 0%

profile of v9, /device:TPU:12, one launch (start us, length us, event | category | flops | bytes accessed | tf_op | source)
XLA Modules:
  0.0 146.1 jit_solution(8924341691411879819)
XLA Ops:
  0.6 0.0 copy-start
  0.6 2.5 %collective-permute-start.1 = (f32[1,256,128]{2,1,0:T(8,128)}, f32[1,256,128]{2,1,0:T(8,128)S(1)}, u32[]{:S(2)}, u32[]{:S(2)}) collective-permute-start(f32[1,256,128]{2,1,0:T(8,128)} %bitcast.108), channel_id=1, source_target_pairs={{0,16},{16,0},{1,17},{17,1},{2,18},{18,2},{3,19},{19,3},{4,20},{20... | collective-permute-start | bytes 393224 | tf_op jit(solution)/shard_map/ppermute | solution.py:31
  3.2 6.7 %collective-permute-start = (f32[48,256]{1,0:T(8,128)}, f32[48,256]{1,0:T(8,128)S(1)}, u32[]{:S(2)}, u32[]{:S(2)}) collective-permute-start(f32[48,256]{1,0:T(8,128)} %bitcast.112), channel_id=1, source_target_pairs={{0,0},{1,1},{2,32},{3,33},{4,64},{5,65},{6,96},{7,97},{8,8},{9,9},... | collective-permute-start | bytes 147464 | tf_op jit(solution)/shard_map/ppermute | solution.py:72
  9.9 4.3 %collective-permute-start.5 = (f32[1,48,256]{2,1,0:T(8,128)}, f32[1,48,256]{2,1,0:T(8,128)S(1)}, u32[]{:S(2)}, u32[]{:S(2)}) collective-permute-start(f32[1,48,256]{2,1,0:T(8,128)} %bitcast.113), channel_id=1, source_target_pairs={{0,4},{4,0},{1,5},{5,1},{2,6},{6,2},{3,7},{7,3},{8,12},{12,8},{9,1... | collective-permute-start | bytes 147464 | tf_op jit(solution)/shard_map/ppermute | solution.py:31
  14.3 0.6 copy-done.4
  14.9 0.1 iota_compare_fusion.1
  15.0 0.1 fusion.25
  15.1 0.1 constant_dynamic-slice_fusion.2
  15.2 0.1 broadcast_bitcast_fusion.1
  15.2 0.0 collective-permute-done
  15.3 1.0 broadcast_in_dim.22
  16.2 11.6 %all-to-all-start = ((f32[16,48,256]{2,1,0:T(8,128)}), f32[16,48,256]{2,1,0:T(8,128)S(1)}, u32[]{:S(2)}, u32[]{:S(2)}) async-start(f32[16,48,256]{2,1,0:T(8,128)} %broadcast_in_dim.22), calls=%async_computation | async-start | bytes 1572864 | tf_op jit(solution)/shard_map/all_to_all | solution.py:27
  27.8 0.0 collective-permute-done.5
  27.8 0.0 copy-start.1
  27.9 4.1 %collective-permute-start.6 = (f32[2,48,256]{2,1,0:T(8,128)S(1)}, f32[2,48,256]{2,1,0:T(8,128)S(1)}, u32[]{:S(2)}, u32[]{:S(2)}) collective-permute-start(f32[2,48,256]{2,1,0:T(8,128)S(1)} %pad_maximum_fusion.7), channel_id=1, source_target_pairs={{0,2},{2,0},{1,3},{3,1},{4,6},{6,4},{5,7},{7,5},{8,10},{10,8},{9,1... | collective-permute-start | bytes 294920 | tf_op jit(solution)/shard_map/ppermute | solution.py:31
  31.9 0.0 collective-permute-done.1
  32.0 4.0 %collective-permute-start.2 = (f32[2,256,128]{2,1,0:T(8,128)S(1)}, f32[2,256,128]{2,1,0:T(8,128)S(1)}, u32[]{:S(2)}, u32[]{:S(2)}) collective-permute-start(f32[2,256,128]{2,1,0:T(8,128)S(1)} %pad_maximum_fusion.4), channel_id=1, source_target_pairs={{0,8},{8,0},{1,9},{9,1},{2,10},{10,2},{3,11},{11,3},{4,12},{12,4},... | collective-permute-start | bytes 786440 | tf_op jit(solution)/shard_map/ppermute | solution.py:31
  36.0 10.6 %collective-permute-done.6 = f32[2,48,256]{2,1,0:T(8,128)S(1)} collective-permute-done((f32[2,48,256]{2,1,0:T(8,128)S(1)}, f32[2,48,256]{2,1,0:T(8,128)S(1)}, u32[]{:S(2)}, u32[]{:S(2)}) %collective-permute-start.6) | collective-permute-done | bytes 98336 | tf_op jit(solution)/shard_map/ppermute | solution.py:31
  46.6 0.0 collective-permute-done.2
  46.7 1.9 %collective-permute-start.3 = (f32[4,256,128]{2,1,0:T(8,128)S(1)}, f32[4,256,128]{2,1,0:T(8,128)S(1)}, u32[]{:S(2)}, u32[]{:S(2)}) collective-permute-start(f32[4,256,128]{2,1,0:T(8,128)S(1)} %pad_maximum_fusion), channel_id=1, source_target_pairs={{0,1},{1,0},{2,3},{3,2},{4,5},{5,4},{6,7},{7,6},{8,9},{9,8},{10,11... | collective-permute-start | bytes 1572872 | tf_op jit(solution)/shard_map/ppermute | solution.py:31
  48.7 4.9 %collective-permute-start.7 = (f32[4,48,256]{2,1,0:T(8,128)S(1)}, f32[4,48,256]{2,1,0:T(8,128)}, u32[]{:S(2)}, u32[]{:S(2)}) collective-permute-start(f32[4,48,256]{2,1,0:T(8,128)S(1)} %pad_maximum_fusion.6), channel_id=1, source_target_pairs={{0,16},{16,0},{1,17},{17,1},{2,18},{18,2},{3,19},{19,3},{4,20},{20... | collective-permute-start | bytes 589832 | tf_op jit(solution)/shard_map/ppermute | solution.py:31
  53.6 5.9 %collective-permute-done.7 = f32[4,48,256]{2,1,0:T(8,128)} collective-permute-done((f32[4,48,256]{2,1,0:T(8,128)S(1)}, f32[4,48,256]{2,1,0:T(8,128)}, u32[]{:S(2)}, u32[]{:S(2)}) %collective-permute-start.7) | collective-permute-done | bytes 196640 | tf_op jit(solution)/shard_map/ppermute | solution.py:31
  59.5 1.0 broadcast_select_fusion.5
  60.5 0.1 broadcast_select_fusion
  60.5 0.0 all-to-all-done
  60.6 0.4 fusion.12
  61.0 0.4 convolution_add_fusion.2
  61.4 0.4 convolution_add_fusion.1
  61.8 1.1 convolution_add_fusion
  63.0 5.8 %all-to-all-start.1 = ((f32[4,48,256]{2,1,0:T(8,128)}), f32[4,48,256]{2,1,0:T(8,128)S(1)}, u32[]{:S(2)}, u32[]{:S(2)}) async-start(f32[4,48,256]{2,1,0:T(8,128)} %bitcast.13), calls=%async_computation.1 | async-start | bytes 393216 | tf_op jit(solution)/shard_map/all_to_all | solution.py:27
  68.8 4.0 %collective-permute-start.8 = (f32[8,48,256]{2,1,0:T(8,128)S(1)}, f32[8,48,256]{2,1,0:T(8,128)S(1)}, u32[]{:S(2)}, u32[]{:S(2)}) collective-permute-start(f32[8,48,256]{2,1,0:T(8,128)S(1)} %pad_maximum_fusion.1), channel_id=1, source_target_pairs={{0,8},{8,0},{1,9},{9,1},{2,10},{10,2},{3,11},{11,3},{4,12},{12,4},... | collective-permute-start | bytes 1179656 | tf_op jit(solution)/shard_map/ppermute | solution.py:87
  72.8 0.1 broadcast_bitcast_fusion
  72.9 1.9 %all-to-all-done.1 = f32[4,48,256]{2,1,0:T(8,128)S(1)} async-done(((f32[4,48,256]{2,1,0:T(8,128)}), f32[4,48,256]{2,1,0:T(8,128)S(1)}, u32[]{:S(2)}, u32[]{:S(2)}) %all-to-all-start.1) | async-done | bytes 196640 | tf_op jit(solution)/shard_map/all_to_all | solution.py:27
  74.8 1.9 %collective-permute-start.4 = (f32[48,256]{1,0:T(8,128)S(1)}, f32[48,256]{1,0:T(8,128)S(1)}, u32[]{:S(2)}, u32[]{:S(2)}) collective-permute-start(f32[48,256]{1,0:T(8,128)S(1)} %reduce_sum.18), channel_id=1, source_target_pairs={{0,1},{1,0},{2,3},{3,2},{4,5},{5,4},{6,7},{7,6},{8,9},{9,8},{10,11... | collective-permute-start | bytes 147464 | tf_op jit(solution)/shard_map/ppermute | solution.py:98
  76.8 0.1 constant_dynamic-slice_fusion.3
  76.9 0.1 copy.63
  77.0 0.3 mul.105
  77.3 0.2 mul.106
  77.6 0.1 reshape.84
  77.6 0.3 collective-permute-done.4
  78.0 0.1 copy.62
  78.1 3.4 %collective-permute-done.8 = f32[8,48,256]{2,1,0:T(8,128)S(1)} collective-permute-done((f32[8,48,256]{2,1,0:T(8,128)S(1)}, f32[8,48,256]{2,1,0:T(8,128)S(1)}, u32[]{:S(2)}, u32[]{:S(2)}) %collective-permute-start.8) | collective-permute-done | bytes 393248 | tf_op jit(solution)/shard_map/ppermute | solution.py:87
  81.4 0.5 fusion
  81.9 0.5 select_bitcast_fusion.1
  82.5 0.9 all_to_all.27
  83.3 20.7 %all-to-all-start.2 = ((f32[16,1,1536]{2,1,0:T(1,128)}), f32[16,1,1536]{2,1,0:T(1,128)S(1)}, u32[]{:S(2)}, u32[]{:S(2)}) async-start(f32[16,1,1536]{2,1,0:T(1,128)} %all_to_all.27), calls=%async_computation.2 | async-start | bytes 196608 | tf_op jit(solution)/shard_map/all_to_all | solution.py:27
  104.1 0.1 copy.64
  104.2 0.1 copy.65
  104.3 12.6 %all-to-all-done.2 = f32[16,1,1536]{2,1,0:T(1,128)S(1)} async-done(((f32[16,1,1536]{2,1,0:T(1,128)}), f32[16,1,1536]{2,1,0:T(1,128)S(1)}, u32[]{:S(2)}, u32[]{:S(2)}) %all-to-all-start.2) | async-done | bytes 98336 | tf_op jit(solution)/shard_map/all_to_all | solution.py:27
  116.9 0.1 reduce_sum.19
  117.0 0.9 all_to_all.24
  117.9 7.9 %all-to-all-start.3 = ((f32[32,1,1920]{2,1,0:T(1,128)}), f32[32,1,1920]{2,1,0:T(1,128)S(1)}, u32[]{:S(2)}, u32[]{:S(2)}) async-start(f32[32,1,1920]{2,1,0:T(1,128)} %all_to_all.24), calls=%async_computation.3 | async-start | bytes 491520 | tf_op jit(solution)/shard_map/all_to_all | solution.py:27
  125.9 2.1 %collective-permute-start.9 = (f32[3,32,128]{2,1,0:T(8,128)S(1)}, f32[3,32,128]{2,1,0:T(8,128)S(1)}, u32[]{:S(2)}, u32[]{:S(2)}) collective-permute-start(f32[3,32,128]{2,1,0:T(8,128)S(1)} %constant_dynamic-slice_fusion), channel_id=1, source_target_pairs={{0,0},{1,1},{2,32},{3,33},{4,64},{5,65},{6,96},{7,97},{8,128},{9,1... | collective-permute-start | bytes 147464 | tf_op jit(solution)/shard_map/ppermute | solution.py:118
  128.0 0.2 dynamic-slice_reduce_fusion
  128.1 13.9 %collective-permute-done.9 = f32[3,32,128]{2,1,0:T(8,128)S(1)} collective-permute-done((f32[3,32,128]{2,1,0:T(8,128)S(1)}, f32[3,32,128]{2,1,0:T(8,128)S(1)}, u32[]{:S(2)}, u32[]{:S(2)}) %collective-permute-start.9) | collective-permute-done | bytes 49184 | tf_op jit(solution)/shard_map/ppermute | solution.py:118
  142.1 0.7 broadcast_multiply_fusion
  142.8 0.3 copy.66
  143.1 0.1 slice.51
  143.2 0.2 copy.67
  143.4 0.8 reshape.94
  144.2 0.2 copy.68
  144.4 0.2 reshape.95
  144.7 0.5 copy.69
  145.2 1.0 reshape.96
  (33 shorter events, 0.4 us)
Async XLA Ops:
  0.6 76.1 %copy-start = (f32[3,32,512]{2,1,0:T(8,128)S(1)}, f32[3,32,512]{2,1,0:T(8,128)}, u32[]{:S(2)}) copy-start(f32[3,32,512]{2,1,0:T(8,128)} %param.7) | copy-start | bytes 589828
  0.6 31.3 %collective-permute-start.1 = (f32[1,256,128]{2,1,0:T(8,128)}, f32[1,256,128]{2,1,0:T(8,128)S(1)}, u32[]{:S(2)}, u32[]{:S(2)}) collective-permute-start(f32[1,256,128]{2,1,0:T(8,128)} %bitcast.108), channel_id=1, source_target_pairs={{0,16},{16,0},{1,17},{17,1},{2,18},{18,2},{3,19},{19,3},{4,20},{20... | collective-permute-start | bytes 393224 | tf_op jit(solution)/shard_map/ppermute | solution.py:31
  3.2 12.0 %collective-permute-start = (f32[48,256]{1,0:T(8,128)}, f32[48,256]{1,0:T(8,128)S(1)}, u32[]{:S(2)}, u32[]{:S(2)}) collective-permute-start(f32[48,256]{1,0:T(8,128)} %bitcast.112), channel_id=1, source_target_pairs={{0,0},{1,1},{2,32},{3,33},{4,64},{5,65},{6,96},{7,97},{8,8},{9,9},... | collective-permute-start | bytes 147464 | tf_op jit(solution)/shard_map/ppermute | solution.py:72
  9.9 17.9 %collective-permute-start.5 = (f32[1,48,256]{2,1,0:T(8,128)}, f32[1,48,256]{2,1,0:T(8,128)S(1)}, u32[]{:S(2)}, u32[]{:S(2)}) collective-permute-start(f32[1,48,256]{2,1,0:T(8,128)} %bitcast.113), channel_id=1, source_target_pairs={{0,4},{4,0},{1,5},{5,1},{2,6},{6,2},{3,7},{7,3},{8,12},{12,8},{9,1... | collective-permute-start | bytes 147464 | tf_op jit(solution)/shard_map/ppermute | solution.py:31
  14.2 0.7 copy-start.4
  14.3 0.7 copy-start.3
  16.2 11.6 %copy-start.2 = (f32[256,3,16]{0,2,1:T(8,128)S(1)}, f32[256,3,16]{0,2,1:T(8,128)}, u32[]{:S(2)}) copy-start(f32[256,3,16]{0,2,1:T(8,128)} %param.6) | copy-start | bytes 147460
  16.2 44.3 %all-to-all-start = ((f32[16,48,256]{2,1,0:T(8,128)}), f32[16,48,256]{2,1,0:T(8,128)S(1)}, u32[]{:S(2)}, u32[]{:S(2)}) async-start(f32[16,48,256]{2,1,0:T(8,128)} %broadcast_in_dim.22), calls=%async_computation | async-start | bytes 1572864 | tf_op jit(solution)/shard_map/all_to_all | solution.py:27
  27.8 4.1 %copy-start.1 = (f32[256,128]{1,0:T(8,128)S(1)}, f32[256,128]{1,0:T(8,128)}, u32[]{:S(2)}) copy-start(f32[256,128]{1,0:T(8,128)} %param.5) | copy-start | bytes 393220
  27.9 18.8 %collective-permute-start.6 = (f32[2,48,256]{2,1,0:T(8,128)S(1)}, f32[2,48,256]{2,1,0:T(8,128)S(1)}, u32[]{:S(2)}, u32[]{:S(2)}) collective-permute-start(f32[2,48,256]{2,1,0:T(8,128)S(1)} %pad_maximum_fusion.7), channel_id=1, source_target_pairs={{0,2},{2,0},{1,3},{3,1},{4,6},{6,4},{5,7},{7,5},{8,10},{10,8},{9,1... | collective-permute-start | bytes 294920 | tf_op jit(solution)/shard_map/ppermute | solution.py:31
  32.0 14.6 %collective-permute-start.2 = (f32[2,256,128]{2,1,0:T(8,128)S(1)}, f32[2,256,128]{2,1,0:T(8,128)S(1)}, u32[]{:S(2)}, u32[]{:S(2)}) collective-permute-start(f32[2,256,128]{2,1,0:T(8,128)S(1)} %pad_maximum_fusion.4), channel_id=1, source_target_pairs={{0,8},{8,0},{1,9},{9,1},{2,10},{10,2},{3,11},{11,3},{4,12},{12,4},... | collective-permute-start | bytes 786440 | tf_op jit(solution)/shard_map/ppermute | solution.py:31
  46.7 13.7 %collective-permute-start.3 = (f32[4,256,128]{2,1,0:T(8,128)S(1)}, f32[4,256,128]{2,1,0:T(8,128)S(1)}, u32[]{:S(2)}, u32[]{:S(2)}) collective-permute-start(f32[4,256,128]{2,1,0:T(8,128)S(1)} %pad_maximum_fusion), channel_id=1, source_target_pairs={{0,1},{1,0},{2,3},{3,2},{4,5},{5,4},{6,7},{7,6},{8,9},{9,8},{10,11... | collective-permute-start | bytes 1572872 | tf_op jit(solution)/shard_map/ppermute | solution.py:31
  48.7 10.8 %collective-permute-start.7 = (f32[4,48,256]{2,1,0:T(8,128)S(1)}, f32[4,48,256]{2,1,0:T(8,128)}, u32[]{:S(2)}, u32[]{:S(2)}) collective-permute-start(f32[4,48,256]{2,1,0:T(8,128)S(1)} %pad_maximum_fusion.6), channel_id=1, source_target_pairs={{0,16},{16,0},{1,17},{17,1},{2,18},{18,2},{3,19},{19,3},{4,20},{20... | collective-permute-start | bytes 589832 | tf_op jit(solution)/shard_map/ppermute | solution.py:31
  63.0 11.9 %all-to-all-start.1 = ((f32[4,48,256]{2,1,0:T(8,128)}), f32[4,48,256]{2,1,0:T(8,128)S(1)}, u32[]{:S(2)}, u32[]{:S(2)}) async-start(f32[4,48,256]{2,1,0:T(8,128)} %bitcast.13), calls=%async_computation.1 | async-start | bytes 393216 | tf_op jit(solution)/shard_map/all_to_all | solution.py:27
  68.8 12.6 %collective-permute-start.8 = (f32[8,48,256]{2,1,0:T(8,128)S(1)}, f32[8,48,256]{2,1,0:T(8,128)S(1)}, u32[]{:S(2)}, u32[]{:S(2)}) collective-permute-start(f32[8,48,256]{2,1,0:T(8,128)S(1)} %pad_maximum_fusion.1), channel_id=1, source_target_pairs={{0,8},{8,0},{1,9},{9,1},{2,10},{10,2},{3,11},{11,3},{4,12},{12,4},... | collective-permute-start | bytes 1179656 | tf_op jit(solution)/shard_map/ppermute | solution.py:87
  74.8 3.1 %collective-permute-start.4 = (f32[48,256]{1,0:T(8,128)S(1)}, f32[48,256]{1,0:T(8,128)S(1)}, u32[]{:S(2)}, u32[]{:S(2)}) collective-permute-start(f32[48,256]{1,0:T(8,128)S(1)} %reduce_sum.18), channel_id=1, source_target_pairs={{0,1},{1,0},{2,3},{3,2},{4,5},{5,4},{6,7},{7,6},{8,9},{9,8},{10,11... | collective-permute-start | bytes 147464 | tf_op jit(solution)/shard_map/ppermute | solution.py:98
  83.3 33.6 %all-to-all-start.2 = ((f32[16,1,1536]{2,1,0:T(1,128)}), f32[16,1,1536]{2,1,0:T(1,128)S(1)}, u32[]{:S(2)}, u32[]{:S(2)}) async-start(f32[16,1,1536]{2,1,0:T(1,128)} %all_to_all.27), calls=%async_computation.2 | async-start | bytes 196608 | tf_op jit(solution)/shard_map/all_to_all | solution.py:27
  117.9 24.9 %all-to-all-start.3 = ((f32[32,1,1920]{2,1,0:T(1,128)}), f32[32,1,1920]{2,1,0:T(1,128)S(1)}, u32[]{:S(2)}, u32[]{:S(2)}) async-start(f32[32,1,1920]{2,1,0:T(1,128)} %all_to_all.24), calls=%async_computation.3 | async-start | bytes 491520 | tf_op jit(solution)/shard_map/all_to_all | solution.py:27
  125.9 16.2 %collective-permute-start.9 = (f32[3,32,128]{2,1,0:T(8,128)S(1)}, f32[3,32,128]{2,1,0:T(8,128)S(1)}, u32[]{:S(2)}, u32[]{:S(2)}) collective-permute-start(f32[3,32,128]{2,1,0:T(8,128)S(1)} %constant_dynamic-slice_fusion), channel_id=1, source_target_pairs={{0,0},{1,1},{2,32},{3,33},{4,64},{5,65},{6,96},{7,97},{8,128},{9,1... | collective-permute-start | bytes 147464 | tf_op jit(solution)/shard_map/ppermute | solution.py:118

commit v10 on v9

--- a/solution.py
+++ b/solution.py
@@ -35,7 +35,7 @@
     return jnp.concatenate([first, second], dim)
 
 
-def digit_swap():
+def digit_swap(flip):
     zh, zl, yh = (lax.axis_size(a) for a in ROW)
     x, yl = lax.axis_size(COL[:2]), lax.axis_size(COL[2:4])
     pairs = []
@@ -45,7 +45,7 @@
                 for d in range(yl):
                     for h in range(NCORE):
                         source = (((a * zl * yh + b) * x + c) * yl + d) * NCORE + h
-                        target = (((a * yl + d) * x + c) * zl * yh + b) * NCORE + h
+                        target = (((a * yl + (d ^ flip)) * x + c) * zl * yh + b) * NCORE + h
                         pairs.append((source, target))
     return pairs
 
@@ -69,14 +69,17 @@
     core = lax.axis_index("core")
 
     panel = jnp.transpose(lpanel, (1, 2, 0)).reshape(wide, rows)
-    swapped = lax.ppermute(panel, ROW + COL, digit_swap())
+    yh = lax.axis_index("yh")
+    same = lax.ppermute(panel, ROW + COL, digit_swap(0))
+    flip = lax.ppermute(panel, ROW + COL, digit_swap(1))
 
     tile_mask = tile_masks(row_blocks, list_len, rows * nrows // TILE)
     own_mask = row_mask(tile_mask, lax.axis_index(ROW), rows)
     factor_mask = row_mask(tile_mask, lax.axis_index(ROW[:1] + COL[2:4]), rows)
-    factor = (swapped.reshape(sibs, width, rows) * factor_mask).reshape(wide, rows)
-    factor = jnp.broadcast_to(factor, (nrows, wide, rows))
-    factor = exchange(factor, ROW).reshape(2, 2, nyl * wide, rows)
+    factor = jnp.stack([jnp.where(yh == 0, same, flip), jnp.where(yh == 0, flip, same)])
+    factor = factor.reshape(2, sibs, width, rows) * factor_mask
+    factor = jnp.broadcast_to(factor.reshape(2 * wide, rows), (nrows // 2, 2 * wide, rows))
+    factor = exchange(factor, ROW[:2]).reshape(2, 2, nyl * wide, rows)
 
     ainv = ainv[None]
     for axis in ("xh", "xl", "core"):

time: 147 us -> 128 us (0.87)
  starting transfers between devices: 82.5 us -> 64.3 us
    all_to_all x4, starting transfers between devices: 46 us -> 29.9 us  [exchange(): return lax.all_to_all(blocks, axes, split_axis=0, concat_axis=0, tiled=True)]
    all_to_all x4, waiting for transfers between devices: 14.5 us -> 22.9 us  [exchange(): return lax.all_to_all(blocks, axes, split_axis=0, concat_axis=0, tiled=True)]
    ppermute x6, waiting for transfers between devices: 16.4 us -> 9.77 us  [doubled(): other = lax.ppermute(block, axis, [(0, 1), (1, 0)])]
    ppermute x1, waiting for transfers between devices: 3.37 us -> 0.76 us  [shards(): panel_far = lax.ppermute(panel_all, 'xl', [(0, 1), (1, 0)])]
    ppermute x6, starting transfers between devices: 21.8 us -> 19.5 us  [doubled(): other = lax.ppermute(block, axis, [(0, 1), (1, 0)])]
    ppermute x1 -> x2, starting transfers between devices: 6.72 us -> 8.77 us  [the longest x1 6.85 us: shards(): same = lax.ppermute(panel, ROW + COL, digit_swap(0))]
    ppermute x1, starting transfers between devices: 4 us -> 2.2 us  [shards(): panel_far = lax.ppermute(panel_all, 'xl', [(0, 1), (1, 0)])]
  transfers between devices with their start and end apart: 14 -> 15, of which waited for: 7 -> 8; matrix products, arithmetic and copies ran while one was open for 3% -> 4% of each run, Pallas kernels for 0% -> 0%
where the time goes in v10:
time: 128 us; the launch traced here: 127 us
  starting transfers between devices  64.3 us (50%)
  waiting for transfers between devices  47.6 us (37%)
  local copies, waits for them, and re-layouts  8.29 us (6%)
  matrix products  3.31 us (3%)
  other arithmetic  2.3 us (2%)
    all_to_all x4, starting transfers between devices, exchange(): return lax.all_to_all(blocks, axes, split_axis=0, concat_axis=0, tiled=True)  29.9 us
    all_to_all x4, waiting for transfers between devices, exchange(): return lax.all_to_all(blocks, axes, split_axis=0, concat_axis=0, tiled=True)  22.9 us
    ppermute x6, starting transfers between devices, doubled(): other = lax.ppermute(block, axis, [(0, 1), (1, 0)])  19.5 us
    ppermute x1, waiting for transfers between devices, shards(): ainv_ki = lax.ppermute(half, ROW + COL, transposed(nrows))  13.9 us
    ppermute x6, waiting for transfers between devices, doubled(): other = lax.ppermute(block, axis, [(0, 1), (1, 0)])  9.77 us
    ppermute x1, starting transfers between devices, shards(): same = lax.ppermute(panel, ROW + COL, digit_swap(0))  6.85 us
  transfers between devices with their start and end apart: 15, of which 8 were waited for; matrix products, arithmetic and copies ran while one was open for 4% of the time, Pallas kernels for 0%

profile of v10, /device:TPU:12, one launch (start us, length us, event | category | flops | bytes accessed | tf_op | source)
XLA Modules:
  0.0 127.0 jit_solution(2803359114067824753)
XLA Ops:
  0.6 0.0 copy-start
  0.6 6.9 %collective-permute-start = (f32[48,256]{1,0:T(8,128)}, f32[48,256]{1,0:T(8,128)S(1)}, u32[]{:S(2)}, u32[]{:S(2)}) collective-permute-start(f32[48,256]{1,0:T(8,128)} %bitcast.116), channel_id=1, source_target_pairs={{0,0},{1,1},{2,32},{3,33},{4,64},{5,65},{6,96},{7,97},{8,8},{9,9},... | collective-permute-start | bytes 147464 | tf_op jit(solution)/shard_map/ppermute | solution.py:73
  7.5 1.9 %collective-permute-start.1 = (f32[48,256]{1,0:T(8,128)}, f32[48,256]{1,0:T(8,128)S(1)}, u32[]{:S(2)}, u32[]{:S(2)}) collective-permute-start(f32[48,256]{1,0:T(8,128)} %bitcast.117), channel_id=1, source_target_pairs={{0,32},{1,33},{2,0},{3,1},{4,96},{5,97},{6,64},{7,65},{8,40},{9,41... | collective-permute-start | bytes 147464 | tf_op jit(solution)/shard_map/ppermute | solution.py:74
  9.4 2.9 %collective-permute-start.2 = (f32[1,256,128]{2,1,0:T(8,128)}, f32[1,256,128]{2,1,0:T(8,128)S(1)}, u32[]{:S(2)}, u32[]{:S(2)}) collective-permute-start(f32[1,256,128]{2,1,0:T(8,128)} %bitcast.112), channel_id=1, source_target_pairs={{0,16},{16,0},{1,17},{17,1},{2,18},{18,2},{3,19},{19,3},{4,20},{20... | collective-permute-start | bytes 393224 | tf_op jit(solution)/shard_map/ppermute | solution.py:31
  12.4 3.8 %collective-permute-start.6 = (f32[1,48,256]{2,1,0:T(8,128)}, f32[1,48,256]{2,1,0:T(8,128)S(1)}, u32[]{:S(2)}, u32[]{:S(2)}) collective-permute-start(f32[1,48,256]{2,1,0:T(8,128)} %bitcast.118), channel_id=1, source_target_pairs={{0,4},{4,0},{1,5},{5,1},{2,6},{6,2},{3,7},{7,3},{8,12},{12,8},{9,1... | collective-permute-start | bytes 147464 | tf_op jit(solution)/shard_map/ppermute | solution.py:31
  16.2 0.6 copy-done.4
  16.8 0.1 iota_compare_fusion.1
  16.9 0.1 fusion.25
  17.0 0.1 constant_dynamic-slice_fusion.2
  17.1 0.1 broadcast_bitcast_fusion.1
  17.2 2.4 %collective-permute-done.6 = f32[1,48,256]{2,1,0:T(8,128)S(1)} collective-permute-done((f32[1,48,256]{2,1,0:T(8,128)}, f32[1,48,256]{2,1,0:T(8,128)S(1)}, u32[]{:S(2)}, u32[]{:S(2)}) %collective-permute-start.6) | collective-permute-done | bytes 49184 | tf_op jit(solution)/shard_map/ppermute | solution.py:31
  19.6 0.0 copy-start.1
  19.6 3.6 %collective-permute-start.7 = (f32[2,48,256]{2,1,0:T(8,128)S(1)}, f32[2,48,256]{2,1,0:T(8,128)S(1)}, u32[]{:S(2)}, u32[]{:S(2)}) collective-permute-start(f32[2,48,256]{2,1,0:T(8,128)S(1)} %pad_maximum_fusion.7), channel_id=1, source_target_pairs={{0,2},{2,0},{1,3},{3,1},{4,6},{6,4},{5,7},{7,5},{8,10},{10,8},{9,1... | collective-permute-start | bytes 294920 | tf_op jit(solution)/shard_map/ppermute | solution.py:31
  23.3 0.0 collective-permute-done.1
  23.3 0.0 collective-permute-done.2
  23.4 3.8 %collective-permute-start.3 = (f32[2,256,128]{2,1,0:T(8,128)S(1)}, f32[2,256,128]{2,1,0:T(8,128)S(1)}, u32[]{:S(2)}, u32[]{:S(2)}) collective-permute-start(f32[2,256,128]{2,1,0:T(8,128)S(1)} %pad_maximum_fusion.4), channel_id=1, source_target_pairs={{0,8},{8,0},{1,9},{9,1},{2,10},{10,2},{3,11},{11,3},{4,12},{12,4},... | collective-permute-start | bytes 786440 | tf_op jit(solution)/shard_map/ppermute | solution.py:31
  27.2 1.0 broadcast_in_dim.22
  28.1 10.3 %all-to-all-start = ((f32[8,96,256]{2,1,0:T(8,128)}), f32[8,96,256]{2,1,0:T(8,128)S(1)}, u32[]{:S(2)}, u32[]{:S(2)}) async-start(f32[8,96,256]{2,1,0:T(8,128)} %broadcast_in_dim.22), calls=%async_computation | async-start | bytes 1572864 | tf_op jit(solution)/shard_map/all_to_all | solution.py:27
  38.4 0.0 collective-permute-done.7
  38.6 1.9 %collective-permute-start.4 = (f32[4,256,128]{2,1,0:T(8,128)S(1)}, f32[4,256,128]{2,1,0:T(8,128)S(1)}, u32[]{:S(2)}, u32[]{:S(2)}) collective-permute-start(f32[4,256,128]{2,1,0:T(8,128)S(1)} %pad_maximum_fusion), channel_id=1, source_target_pairs={{0,1},{1,0},{2,3},{3,2},{4,5},{5,4},{6,7},{7,6},{8,9},{9,8},{10,11... | collective-permute-start | bytes 1572872 | tf_op jit(solution)/shard_map/ppermute | solution.py:31
  40.5 3.4 %collective-permute-start.8 = (f32[4,48,256]{2,1,0:T(8,128)S(1)}, f32[4,48,256]{2,1,0:T(8,128)}, u32[]{:S(2)}, u32[]{:S(2)}) collective-permute-start(f32[4,48,256]{2,1,0:T(8,128)S(1)} %pad_maximum_fusion.6), channel_id=1, source_target_pairs={{0,16},{16,0},{1,17},{17,1},{2,18},{18,2},{3,19},{19,3},{4,20},{20... | collective-permute-start | bytes 589832 | tf_op jit(solution)/shard_map/ppermute | solution.py:31
  44.0 7.4 %collective-permute-done.8 = f32[4,48,256]{2,1,0:T(8,128)} collective-permute-done((f32[4,48,256]{2,1,0:T(8,128)S(1)}, f32[4,48,256]{2,1,0:T(8,128)}, u32[]{:S(2)}, u32[]{:S(2)}) %collective-permute-start.8) | collective-permute-done | bytes 196640 | tf_op jit(solution)/shard_map/ppermute | solution.py:31
  51.3 1.0 broadcast_select_fusion.5
  52.3 0.1 broadcast_select_fusion
  52.4 6.9 %all-to-all-done = f32[8,96,256]{2,1,0:T(8,128)S(1)} async-done(((f32[8,96,256]{2,1,0:T(8,128)}), f32[8,96,256]{2,1,0:T(8,128)S(1)}, u32[]{:S(2)}, u32[]{:S(2)}) %all-to-all-start) | async-done | bytes 786464 | tf_op jit(solution)/shard_map/all_to_all | solution.py:27
  59.3 0.4 fusion.12
  59.8 0.4 convolution_add_fusion.2
  60.2 0.4 convolution_add_fusion.1
  60.6 1.1 convolution_add_fusion
  61.7 5.0 %all-to-all-start.1 = ((f32[4,48,256]{2,1,0:T(8,128)}), f32[4,48,256]{2,1,0:T(8,128)S(1)}, u32[]{:S(2)}, u32[]{:S(2)}) async-start(f32[4,48,256]{2,1,0:T(8,128)} %bitcast.16), calls=%async_computation.1 | async-start | bytes 393216 | tf_op jit(solution)/shard_map/all_to_all | solution.py:27
  66.8 2.2 %collective-permute-start.9 = (f32[8,48,256]{2,1,0:T(8,128)S(1)}, f32[8,48,256]{2,1,0:T(8,128)S(1)}, u32[]{:S(2)}, u32[]{:S(2)}) collective-permute-start(f32[8,48,256]{2,1,0:T(8,128)S(1)} %pad_maximum_fusion.1), channel_id=1, source_target_pairs={{0,8},{8,0},{1,9},{9,1},{2,10},{10,2},{3,11},{11,3},{4,12},{12,4},... | collective-permute-start | bytes 1179656 | tf_op jit(solution)/shard_map/ppermute | solution.py:90
  69.0 0.1 broadcast_bitcast_fusion
  69.1 3.4 %all-to-all-done.1 = f32[4,48,256]{2,1,0:T(8,128)S(1)} async-done(((f32[4,48,256]{2,1,0:T(8,128)}), f32[4,48,256]{2,1,0:T(8,128)S(1)}, u32[]{:S(2)}, u32[]{:S(2)}) %all-to-all-start.1) | async-done | bytes 196640 | tf_op jit(solution)/shard_map/all_to_all | solution.py:27
  72.5 1.9 %collective-permute-start.5 = (f32[48,256]{1,0:T(8,128)S(1)}, f32[48,256]{1,0:T(8,128)S(1)}, u32[]{:S(2)}, u32[]{:S(2)}) collective-permute-start(f32[48,256]{1,0:T(8,128)S(1)} %reduce_sum.18), channel_id=1, source_target_pairs={{0,1},{1,0},{2,3},{3,2},{4,5},{5,4},{6,7},{7,6},{8,9},{9,8},{10,11... | collective-permute-start | bytes 147464 | tf_op jit(solution)/shard_map/ppermute | solution.py:101
  74.4 0.1 constant_dynamic-slice_fusion.3
  74.5 0.1 copy.63
  74.6 0.3 mul.106
  75.0 0.2 mul.107
  75.2 0.1 reshape.90
  75.3 0.3 collective-permute-done.5
  75.6 0.1 copy.62
  75.7 0.8 collective-permute-done.9
  76.5 0.5 fusion
  76.9 0.5 select_bitcast_fusion.1
  77.5 0.9 all_to_all.27
  78.3 6.9 %all-to-all-start.2 = ((f32[16,1,1536]{2,1,0:T(1,128)}), f32[16,1,1536]{2,1,0:T(1,128)S(1)}, u32[]{:S(2)}, u32[]{:S(2)}) async-start(f32[16,1,1536]{2,1,0:T(1,128)} %all_to_all.27), calls=%async_computation.2 | async-start | bytes 196608 | tf_op jit(solution)/shard_map/all_to_all | solution.py:27
  85.2 0.1 copy.64
  85.4 0.1 copy.65
  85.5 12.6 %all-to-all-done.2 = f32[16,1,1536]{2,1,0:T(1,128)S(1)} async-done(((f32[16,1,1536]{2,1,0:T(1,128)}), f32[16,1,1536]{2,1,0:T(1,128)S(1)}, u32[]{:S(2)}, u32[]{:S(2)}) %all-to-all-start.2) | async-done | bytes 98336 | tf_op jit(solution)/shard_map/all_to_all | solution.py:27
  98.0 0.1 reduce_sum.19
  98.2 0.9 all_to_all.24
  99.0 7.7 %all-to-all-start.3 = ((f32[32,1,1920]{2,1,0:T(1,128)}), f32[32,1,1920]{2,1,0:T(1,128)S(1)}, u32[]{:S(2)}, u32[]{:S(2)}) async-start(f32[32,1,1920]{2,1,0:T(1,128)} %all_to_all.24), calls=%async_computation.3 | async-start | bytes 491520 | tf_op jit(solution)/shard_map/all_to_all | solution.py:27
  106.7 2.1 %collective-permute-start.10 = (f32[3,32,128]{2,1,0:T(8,128)S(1)}, f32[3,32,128]{2,1,0:T(8,128)S(1)}, u32[]{:S(2)}, u32[]{:S(2)}) collective-permute-start(f32[3,32,128]{2,1,0:T(8,128)S(1)} %constant_dynamic-slice_fusion), channel_id=1, source_target_pairs={{0,0},{1,1},{2,32},{3,33},{4,64},{5,65},{6,96},{7,97},{8,128},{9,1... | collective-permute-start | bytes 147464 | tf_op jit(solution)/shard_map/ppermute | solution.py:121
  108.9 0.2 dynamic-slice_reduce_fusion
  109.1 13.9 %collective-permute-done.10 = f32[3,32,128]{2,1,0:T(8,128)S(1)} collective-permute-done((f32[3,32,128]{2,1,0:T(8,128)S(1)}, f32[3,32,128]{2,1,0:T(8,128)S(1)}, u32[]{:S(2)}, u32[]{:S(2)}) %collective-permute-start.10) | collective-permute-done | bytes 49184 | tf_op jit(solution)/shard_map/ppermute | solution.py:121
  122.9 0.7 broadcast_multiply_fusion
  123.6 0.3 copy.66
  124.0 0.1 slice.51
  124.1 0.2 copy.67
  124.3 0.8 reshape.100
  125.1 0.2 copy.68
  125.3 0.2 reshape.101
  125.6 0.5 copy.69
  126.0 1.0 reshape.102
  (36 shorter events, 0.4 us)
Async XLA Ops:
  0.6 73.8 %copy-start = (f32[3,32,512]{2,1,0:T(8,128)S(1)}, f32[3,32,512]{2,1,0:T(8,128)}, u32[]{:S(2)}) copy-start(f32[3,32,512]{2,1,0:T(8,128)} %param.7) | copy-start | bytes 589828
  0.6 22.6 %collective-permute-start = (f32[48,256]{1,0:T(8,128)}, f32[48,256]{1,0:T(8,128)S(1)}, u32[]{:S(2)}, u32[]{:S(2)}) collective-permute-start(f32[48,256]{1,0:T(8,128)} %bitcast.116), channel_id=1, source_target_pairs={{0,0},{1,1},{2,32},{3,33},{4,64},{5,65},{6,96},{7,97},{8,8},{9,9},... | collective-permute-start | bytes 147464 | tf_op jit(solution)/shard_map/ppermute | solution.py:73
  7.5 15.8 %collective-permute-start.1 = (f32[48,256]{1,0:T(8,128)}, f32[48,256]{1,0:T(8,128)S(1)}, u32[]{:S(2)}, u32[]{:S(2)}) collective-permute-start(f32[48,256]{1,0:T(8,128)} %bitcast.117), channel_id=1, source_target_pairs={{0,32},{1,33},{2,0},{3,1},{4,96},{5,97},{6,64},{7,65},{8,40},{9,41... | collective-permute-start | bytes 147464 | tf_op jit(solution)/shard_map/ppermute | solution.py:74
  9.4 13.9 %collective-permute-start.2 = (f32[1,256,128]{2,1,0:T(8,128)}, f32[1,256,128]{2,1,0:T(8,128)S(1)}, u32[]{:S(2)}, u32[]{:S(2)}) collective-permute-start(f32[1,256,128]{2,1,0:T(8,128)} %bitcast.112), channel_id=1, source_target_pairs={{0,16},{16,0},{1,17},{17,1},{2,18},{18,2},{3,19},{19,3},{4,20},{20... | collective-permute-start | bytes 393224 | tf_op jit(solution)/shard_map/ppermute | solution.py:31
  12.4 7.2 %collective-permute-start.6 = (f32[1,48,256]{2,1,0:T(8,128)}, f32[1,48,256]{2,1,0:T(8,128)S(1)}, u32[]{:S(2)}, u32[]{:S(2)}) collective-permute-start(f32[1,48,256]{2,1,0:T(8,128)} %bitcast.118), channel_id=1, source_target_pairs={{0,4},{4,0},{1,5},{5,1},{2,6},{6,2},{3,7},{7,3},{8,12},{12,8},{9,1... | collective-permute-start | bytes 147464 | tf_op jit(solution)/shard_map/ppermute | solution.py:31
  16.2 0.7 copy-start.4
  16.2 0.7 copy-start.3
  16.2 3.4 %copy-start.2 = (f32[256,3,16]{0,2,1:T(8,128)S(1)}, f32[256,3,16]{0,2,1:T(8,128)}, u32[]{:S(2)}) copy-start(f32[256,3,16]{0,2,1:T(8,128)} %param.6) | copy-start | bytes 147460
  19.6 3.7 %copy-start.1 = (f32[256,128]{1,0:T(8,128)S(1)}, f32[256,128]{1,0:T(8,128)}, u32[]{:S(2)}) copy-start(f32[256,128]{1,0:T(8,128)} %param.5) | copy-start | bytes 393220
  19.6 18.9 %collective-permute-start.7 = (f32[2,48,256]{2,1,0:T(8,128)S(1)}, f32[2,48,256]{2,1,0:T(8,128)S(1)}, u32[]{:S(2)}, u32[]{:S(2)}) collective-permute-start(f32[2,48,256]{2,1,0:T(8,128)S(1)} %pad_maximum_fusion.7), channel_id=1, source_target_pairs={{0,2},{2,0},{1,3},{3,1},{4,6},{6,4},{5,7},{7,5},{8,10},{10,8},{9,1... | collective-permute-start | bytes 294920 | tf_op jit(solution)/shard_map/ppermute | solution.py:31
  23.4 15.1 %collective-permute-start.3 = (f32[2,256,128]{2,1,0:T(8,128)S(1)}, f32[2,256,128]{2,1,0:T(8,128)S(1)}, u32[]{:S(2)}, u32[]{:S(2)}) collective-permute-start(f32[2,256,128]{2,1,0:T(8,128)S(1)} %pad_maximum_fusion.4), channel_id=1, source_target_pairs={{0,8},{8,0},{1,9},{9,1},{2,10},{10,2},{3,11},{11,3},{4,12},{12,4},... | collective-permute-start | bytes 786440 | tf_op jit(solution)/shard_map/ppermute | solution.py:31
  28.1 31.2 %all-to-all-start = ((f32[8,96,256]{2,1,0:T(8,128)}), f32[8,96,256]{2,1,0:T(8,128)S(1)}, u32[]{:S(2)}, u32[]{:S(2)}) async-start(f32[8,96,256]{2,1,0:T(8,128)} %broadcast_in_dim.22), calls=%async_computation | async-start | bytes 1572864 | tf_op jit(solution)/shard_map/all_to_all | solution.py:27
  38.6 13.7 %collective-permute-start.4 = (f32[4,256,128]{2,1,0:T(8,128)S(1)}, f32[4,256,128]{2,1,0:T(8,128)S(1)}, u32[]{:S(2)}, u32[]{:S(2)}) collective-permute-start(f32[4,256,128]{2,1,0:T(8,128)S(1)} %pad_maximum_fusion), channel_id=1, source_target_pairs={{0,1},{1,0},{2,3},{3,2},{4,5},{5,4},{6,7},{7,6},{8,9},{9,8},{10,11... | collective-permute-start | bytes 1572872 | tf_op jit(solution)/shard_map/ppermute | solution.py:31
  40.5 10.8 %collective-permute-start.8 = (f32[4,48,256]{2,1,0:T(8,128)S(1)}, f32[4,48,256]{2,1,0:T(8,128)}, u32[]{:S(2)}, u32[]{:S(2)}) collective-permute-start(f32[4,48,256]{2,1,0:T(8,128)S(1)} %pad_maximum_fusion.6), channel_id=1, source_target_pairs={{0,16},{16,0},{1,17},{17,1},{2,18},{18,2},{3,19},{19,3},{4,20},{20... | collective-permute-start | bytes 589832 | tf_op jit(solution)/shard_map/ppermute | solution.py:31
  61.7 10.7 %all-to-all-start.1 = ((f32[4,48,256]{2,1,0:T(8,128)}), f32[4,48,256]{2,1,0:T(8,128)S(1)}, u32[]{:S(2)}, u32[]{:S(2)}) async-start(f32[4,48,256]{2,1,0:T(8,128)} %bitcast.16), calls=%async_computation.1 | async-start | bytes 393216 | tf_op jit(solution)/shard_map/all_to_all | solution.py:27
  66.8 9.7 %collective-permute-start.9 = (f32[8,48,256]{2,1,0:T(8,128)S(1)}, f32[8,48,256]{2,1,0:T(8,128)S(1)}, u32[]{:S(2)}, u32[]{:S(2)}) collective-permute-start(f32[8,48,256]{2,1,0:T(8,128)S(1)} %pad_maximum_fusion.1), channel_id=1, source_target_pairs={{0,8},{8,0},{1,9},{9,1},{2,10},{10,2},{3,11},{11,3},{4,12},{12,4},... | collective-permute-start | bytes 1179656 | tf_op jit(solution)/shard_map/ppermute | solution.py:90
  72.5 3.1 %collective-permute-start.5 = (f32[48,256]{1,0:T(8,128)S(1)}, f32[48,256]{1,0:T(8,128)S(1)}, u32[]{:S(2)}, u32[]{:S(2)}) collective-permute-start(f32[48,256]{1,0:T(8,128)S(1)} %reduce_sum.18), channel_id=1, source_target_pairs={{0,1},{1,0},{2,3},{3,2},{4,5},{5,4},{6,7},{7,6},{8,9},{9,8},{10,11... | collective-permute-start | bytes 147464 | tf_op jit(solution)/shard_map/ppermute | solution.py:101
  78.3 19.7 %all-to-all-start.2 = ((f32[16,1,1536]{2,1,0:T(1,128)}), f32[16,1,1536]{2,1,0:T(1,128)S(1)}, u32[]{:S(2)}, u32[]{:S(2)}) async-start(f32[16,1,1536]{2,1,0:T(1,128)} %all_to_all.27), calls=%async_computation.2 | async-start | bytes 196608 | tf_op jit(solution)/shard_map/all_to_all | solution.py:27
  99.0 24.6 %all-to-all-start.3 = ((f32[32,1,1920]{2,1,0:T(1,128)}), f32[32,1,1920]{2,1,0:T(1,128)S(1)}, u32[]{:S(2)}, u32[]{:S(2)}) async-start(f32[32,1,1920]{2,1,0:T(1,128)} %all_to_all.24), calls=%async_computation.3 | async-start | bytes 491520 | tf_op jit(solution)/shard_map/all_to_all | solution.py:27
  106.7 16.2 %collective-permute-start.10 = (f32[3,32,128]{2,1,0:T(8,128)S(1)}, f32[3,32,128]{2,1,0:T(8,128)S(1)}, u32[]{:S(2)}, u32[]{:S(2)}) collective-permute-start(f32[3,32,128]{2,1,0:T(8,128)S(1)} %constant_dynamic-slice_fusion), channel_id=1, source_target_pairs={{0,0},{1,1},{2,32},{3,33},{4,64},{5,65},{6,96},{7,97},{8,128},{9,1... | collective-permute-start | bytes 147464 | tf_op jit(solution)/shard_map/ppermute | solution.py:121

commit v11 on v10

--- a/solution.py
+++ b/solution.py
@@ -124,12 +124,15 @@
 
     share = rows // ncols
     split = -plain.reshape(sibs, width, rows) * own_mask
-    split = split.reshape(wide, ncols, share).transpose(1, 0, 2).reshape(ncols, wide * share)
-    joined = jnp.concatenate([jnp.broadcast_to(diag, (ncols, diag.size)), split], 1)
+    split = split.reshape(wide, ncols, share).transpose(1, 0, 2).reshape(ncols, -1, TILE)
+    diag = diag.reshape(-1, TILE)
+    mid = diag.shape[0]
+    joined = jnp.concatenate([jnp.broadcast_to(diag, (ncols, *diag.shape)), split], 1)
+    joined = jnp.pad(joined, ((0, 0), (0, -joined.shape[1] % 8), (0, 0)))
     joined = exchange(joined, COL)
-    diag = joined[:, : own.size].reshape(nchips, NCORE, sibs, width, NCORE * width)
+    diag = joined[:, :mid].reshape(nchips, NCORE, sibs, width, NCORE * width)
     ainv_kk = diag.transpose(2, 1, 3, 0, 4).reshape(kk_inverse.shape)
-    split = joined[:, own.size :].reshape(ncols, sibs, width, share)
+    split = joined[:, mid : mid + wide * share // TILE].reshape(ncols, sibs, width, share)
     ainv_ik = split.transpose(3, 1, 0, 2).reshape(share, sibs, -1)
     return ainv_ik, ainv_kk, ainv_ki
 

time: 128 us -> 127 us (level)
  local copies, waits for them, and re-layouts: 8.29 us -> 6.94 us
where the time goes in v11:
time: 127 us; the launch traced here: 126 us
  starting transfers between devices  64.3 us (51%)
  waiting for transfers between devices  47.7 us (38%)
  local copies, waits for them, and re-layouts  6.94 us (5%)
  matrix products  3.31 us (3%)
  other arithmetic  3.02 us (2%)
    all_to_all x4, starting transfers between devices, exchange(): return lax.all_to_all(blocks, axes, split_axis=0, concat_axis=0, tiled=True)  29.9 us
    all_to_all x4, waiting for transfers between devices, exchange(): return lax.all_to_all(blocks, axes, split_axis=0, concat_axis=0, tiled=True)  22.8 us
    ppermute x6, starting transfers between devices, doubled(): other = lax.ppermute(block, axis, [(0, 1), (1, 0)])  19.5 us
    ppermute x1, waiting for transfers between devices, shards(): ainv_ki = lax.ppermute(half, ROW + COL, transposed(nrows))  14 us
    ppermute x6, waiting for transfers between devices, doubled(): other = lax.ppermute(block, axis, [(0, 1), (1, 0)])  9.77 us
    ppermute x1, starting transfers between devices, shards(): same = lax.ppermute(panel, ROW + COL, digit_swap(0))  6.85 us
  transfers between devices with their start and end apart: 15, of which 8 were waited for; matrix products, arithmetic and copies ran while one was open for 4% of the time, Pallas kernels for 0%

profile of v11, /device:TPU:12, one launch (start us, length us, event | category | flops | bytes accessed | tf_op | source)
XLA Modules:
  0.0 126.3 jit_solution(4589856484013817276)
XLA Ops:
  0.6 0.0 copy-start
  0.6 6.9 %collective-permute-start = (f32[48,256]{1,0:T(8,128)}, f32[48,256]{1,0:T(8,128)S(1)}, u32[]{:S(2)}, u32[]{:S(2)}) collective-permute-start(f32[48,256]{1,0:T(8,128)} %bitcast.117), channel_id=1, source_target_pairs={{0,0},{1,1},{2,32},{3,33},{4,64},{5,65},{6,96},{7,97},{8,8},{9,9},... | collective-permute-start | bytes 147464 | tf_op jit(solution)/shard_map/ppermute | solution.py:73
  7.5 1.9 %collective-permute-start.1 = (f32[48,256]{1,0:T(8,128)}, f32[48,256]{1,0:T(8,128)S(1)}, u32[]{:S(2)}, u32[]{:S(2)}) collective-permute-start(f32[48,256]{1,0:T(8,128)} %bitcast.118), channel_id=1, source_target_pairs={{0,32},{1,33},{2,0},{3,1},{4,96},{5,97},{6,64},{7,65},{8,40},{9,41... | collective-permute-start | bytes 147464 | tf_op jit(solution)/shard_map/ppermute | solution.py:74
  9.4 2.9 %collective-permute-start.2 = (f32[1,256,128]{2,1,0:T(8,128)}, f32[1,256,128]{2,1,0:T(8,128)S(1)}, u32[]{:S(2)}, u32[]{:S(2)}) collective-permute-start(f32[1,256,128]{2,1,0:T(8,128)} %bitcast.113), channel_id=1, source_target_pairs={{0,16},{16,0},{1,17},{17,1},{2,18},{18,2},{3,19},{19,3},{4,20},{20... | collective-permute-start | bytes 393224 | tf_op jit(solution)/shard_map/ppermute | solution.py:31
  12.4 3.8 %collective-permute-start.6 = (f32[1,48,256]{2,1,0:T(8,128)}, f32[1,48,256]{2,1,0:T(8,128)S(1)}, u32[]{:S(2)}, u32[]{:S(2)}) collective-permute-start(f32[1,48,256]{2,1,0:T(8,128)} %bitcast.119), channel_id=1, source_target_pairs={{0,4},{4,0},{1,5},{5,1},{2,6},{6,2},{3,7},{7,3},{8,12},{12,8},{9,1... | collective-permute-start | bytes 147464 | tf_op jit(solution)/shard_map/ppermute | solution.py:31
  16.2 0.6 copy-done.4
  16.8 0.1 iota_compare_fusion.2
  16.9 0.1 fusion.25
  17.0 0.1 constant_dynamic-slice_fusion.2
  17.1 0.1 broadcast_bitcast_fusion.1
  17.2 2.4 %collective-permute-done.6 = f32[1,48,256]{2,1,0:T(8,128)S(1)} collective-permute-done((f32[1,48,256]{2,1,0:T(8,128)}, f32[1,48,256]{2,1,0:T(8,128)S(1)}, u32[]{:S(2)}, u32[]{:S(2)}) %collective-permute-start.6) | collective-permute-done | bytes 49184 | tf_op jit(solution)/shard_map/ppermute | solution.py:31
  19.6 0.0 copy-start.1
  19.6 3.6 %collective-permute-start.7 = (f32[2,48,256]{2,1,0:T(8,128)S(1)}, f32[2,48,256]{2,1,0:T(8,128)S(1)}, u32[]{:S(2)}, u32[]{:S(2)}) collective-permute-start(f32[2,48,256]{2,1,0:T(8,128)S(1)} %pad_maximum_fusion.6), channel_id=1, source_target_pairs={{0,2},{2,0},{1,3},{3,1},{4,6},{6,4},{5,7},{7,5},{8,10},{10,8},{9,1... | collective-permute-start | bytes 294920 | tf_op jit(solution)/shard_map/ppermute | solution.py:31
  23.3 0.0 collective-permute-done.1
  23.3 0.0 collective-permute-done.2
  23.4 3.8 %collective-permute-start.3 = (f32[2,256,128]{2,1,0:T(8,128)S(1)}, f32[2,256,128]{2,1,0:T(8,128)S(1)}, u32[]{:S(2)}, u32[]{:S(2)}) collective-permute-start(f32[2,256,128]{2,1,0:T(8,128)S(1)} %pad_maximum_fusion.4), channel_id=1, source_target_pairs={{0,8},{8,0},{1,9},{9,1},{2,10},{10,2},{3,11},{11,3},{4,12},{12,4},... | collective-permute-start | bytes 786440 | tf_op jit(solution)/shard_map/ppermute | solution.py:31
  27.2 1.0 broadcast_in_dim.22
  28.1 10.3 %all-to-all-start = ((f32[8,96,256]{2,1,0:T(8,128)}), f32[8,96,256]{2,1,0:T(8,128)S(1)}, u32[]{:S(2)}, u32[]{:S(2)}) async-start(f32[8,96,256]{2,1,0:T(8,128)} %broadcast_in_dim.22), calls=%async_computation | async-start | bytes 1572864 | tf_op jit(solution)/shard_map/all_to_all | solution.py:27
  38.4 0.0 collective-permute-done.7
  38.5 0.0 collective-permute-done.3
  38.6 1.9 %collective-permute-start.4 = (f32[4,256,128]{2,1,0:T(8,128)S(1)}, f32[4,256,128]{2,1,0:T(8,128)S(1)}, u32[]{:S(2)}, u32[]{:S(2)}) collective-permute-start(f32[4,256,128]{2,1,0:T(8,128)S(1)} %pad_maximum_fusion), channel_id=1, source_target_pairs={{0,1},{1,0},{2,3},{3,2},{4,5},{5,4},{6,7},{7,6},{8,9},{9,8},{10,11... | collective-permute-start | bytes 1572872 | tf_op jit(solution)/shard_map/ppermute | solution.py:31
  40.5 3.4 %collective-permute-start.8 = (f32[4,48,256]{2,1,0:T(8,128)S(1)}, f32[4,48,256]{2,1,0:T(8,128)}, u32[]{:S(2)}, u32[]{:S(2)}) collective-permute-start(f32[4,48,256]{2,1,0:T(8,128)S(1)} %pad_maximum_fusion.5), channel_id=1, source_target_pairs={{0,16},{16,0},{1,17},{17,1},{2,18},{18,2},{3,19},{19,3},{4,20},{20... | collective-permute-start | bytes 589832 | tf_op jit(solution)/shard_map/ppermute | solution.py:31
  44.0 7.4 %collective-permute-done.8 = f32[4,48,256]{2,1,0:T(8,128)} collective-permute-done((f32[4,48,256]{2,1,0:T(8,128)S(1)}, f32[4,48,256]{2,1,0:T(8,128)}, u32[]{:S(2)}, u32[]{:S(2)}) %collective-permute-start.8) | collective-permute-done | bytes 196640 | tf_op jit(solution)/shard_map/ppermute | solution.py:31
  51.3 1.0 broadcast_select_fusion.5
  52.3 0.1 broadcast_select_fusion
  52.4 6.9 %all-to-all-done = f32[8,96,256]{2,1,0:T(8,128)S(1)} async-done(((f32[8,96,256]{2,1,0:T(8,128)}), f32[8,96,256]{2,1,0:T(8,128)S(1)}, u32[]{:S(2)}, u32[]{:S(2)}) %all-to-all-start) | async-done | bytes 786464 | tf_op jit(solution)/shard_map/all_to_all | solution.py:27
  59.3 0.4 fusion.12
  59.8 0.4 convolution_add_fusion.2
  60.2 0.4 convolution_add_fusion.1
  60.6 1.1 convolution_add_fusion
  61.7 5.0 %all-to-all-start.1 = ((f32[4,48,256]{2,1,0:T(8,128)}), f32[4,48,256]{2,1,0:T(8,128)S(1)}, u32[]{:S(2)}, u32[]{:S(2)}) async-start(f32[4,48,256]{2,1,0:T(8,128)} %bitcast.16), calls=%async_computation.1 | async-start | bytes 393216 | tf_op jit(solution)/shard_map/all_to_all | solution.py:27
  66.8 2.2 %collective-permute-start.9 = (f32[8,48,256]{2,1,0:T(8,128)S(1)}, f32[8,48,256]{2,1,0:T(8,128)S(1)}, u32[]{:S(2)}, u32[]{:S(2)}) collective-permute-start(f32[8,48,256]{2,1,0:T(8,128)S(1)} %pad_maximum_fusion.1), channel_id=1, source_target_pairs={{0,8},{8,0},{1,9},{9,1},{2,10},{10,2},{3,11},{11,3},{4,12},{12,4},... | collective-permute-start | bytes 1179656 | tf_op jit(solution)/shard_map/ppermute | solution.py:90
  69.0 0.1 broadcast_bitcast_fusion
  69.1 3.4 %all-to-all-done.1 = f32[4,48,256]{2,1,0:T(8,128)S(1)} async-done(((f32[4,48,256]{2,1,0:T(8,128)}), f32[4,48,256]{2,1,0:T(8,128)S(1)}, u32[]{:S(2)}, u32[]{:S(2)}) %all-to-all-start.1) | async-done | bytes 196640 | tf_op jit(solution)/shard_map/all_to_all | solution.py:27
  72.5 1.9 %collective-permute-start.5 = (f32[48,256]{1,0:T(8,128)S(1)}, f32[48,256]{1,0:T(8,128)S(1)}, u32[]{:S(2)}, u32[]{:S(2)}) collective-permute-start(f32[48,256]{1,0:T(8,128)S(1)} %reduce_sum.20), channel_id=1, source_target_pairs={{0,1},{1,0},{2,3},{3,2},{4,5},{5,4},{6,7},{7,6},{8,9},{9,8},{10,11... | collective-permute-start | bytes 147464 | tf_op jit(solution)/shard_map/ppermute | solution.py:101
  74.4 0.1 constant_dynamic-slice_fusion.3
  74.5 0.1 reshape.91
  74.6 0.1 copy.62
  74.7 0.3 mul.106
  75.1 0.2 mul.107
  75.3 0.3 collective-permute-done.5
  75.6 0.9 collective-permute-done.9
  76.5 0.5 fusion
  76.9 0.5 select_bitcast_fusion.1
  77.5 0.9 all_to_all.20
  78.3 6.9 %all-to-all-start.2 = ((f32[16,1,1536]{2,1,0:T(1,128)}), f32[16,1,1536]{2,1,0:T(1,128)S(1)}, u32[]{:S(2)}, u32[]{:S(2)}) async-start(f32[16,1,1536]{2,1,0:T(1,128)} %all_to_all.20), calls=%async_computation.2 | async-start | bytes 196608 | tf_op jit(solution)/shard_map/all_to_all | solution.py:27
  85.2 0.1 copy.61
  85.3 0.1 copy.63
  85.5 0.1 copy.64
  85.6 12.5 %all-to-all-done.2 = f32[16,1,1536]{2,1,0:T(1,128)S(1)} async-done(((f32[16,1,1536]{2,1,0:T(1,128)}), f32[16,1,1536]{2,1,0:T(1,128)S(1)}, u32[]{:S(2)}, u32[]{:S(2)}) %all-to-all-start.2) | async-done | bytes 98336 | tf_op jit(solution)/shard_map/all_to_all | solution.py:27
  98.0 0.1 reduce_sum.21
  98.2 0.7 select_maximum_fusion
  98.9 7.7 %all-to-all-start.3 = ((f32[32,16,128]{2,1,0:T(8,128)}), f32[32,16,128]{2,1,0:T(8,128)S(1)}, u32[]{:S(2)}, u32[]{:S(2)}) async-start(f32[32,16,128]{2,1,0:T(8,128)} %select_maximum_fusion), calls=%async_computation.3 | async-start | bytes 524288 | tf_op jit(solution)/shard_map/all_to_all | solution.py:27
  106.6 2.0 %collective-permute-start.10 = (f32[3,32,128]{2,1,0:T(8,128)S(1)}, f32[3,32,128]{2,1,0:T(8,128)S(1)}, u32[]{:S(2)}, u32[]{:S(2)}) collective-permute-start(f32[3,32,128]{2,1,0:T(8,128)S(1)} %constant_dynamic-slice_fusion), channel_id=1, source_target_pairs={{0,0},{1,1},{2,32},{3,33},{4,64},{5,65},{6,96},{7,97},{8,128},{9,1... | collective-permute-start | bytes 147464 | tf_op jit(solution)/shard_map/ppermute | solution.py:121
  108.7 0.2 dynamic-slice_reduce_fusion
  108.9 14.0 %collective-permute-done.10 = f32[3,32,128]{2,1,0:T(8,128)S(1)} collective-permute-done((f32[3,32,128]{2,1,0:T(8,128)S(1)}, f32[3,32,128]{2,1,0:T(8,128)S(1)}, u32[]{:S(2)}, u32[]{:S(2)}) %collective-permute-start.10) | collective-permute-done | bytes 49184 | tf_op jit(solution)/shard_map/ppermute | solution.py:121
  122.8 0.7 broadcast_multiply_fusion
  123.5 0.0 all-to-all-done.3
  123.5 0.2 reshape.102
  123.7 0.5 copy.67
  124.2 1.0 reshape.103
  125.2 0.1 copy.69
  125.3 0.2 copy.66
  125.5 0.8 reshape.101
  (33 shorter events, 0.4 us)
Async XLA Ops:
  0.6 73.8 %copy-start = (f32[3,32,512]{2,1,0:T(8,128)S(1)}, f32[3,32,512]{2,1,0:T(8,128)}, u32[]{:S(2)}) copy-start(f32[3,32,512]{2,1,0:T(8,128)} %param.7) | copy-start | bytes 589828
  0.6 22.6 %collective-permute-start = (f32[48,256]{1,0:T(8,128)}, f32[48,256]{1,0:T(8,128)S(1)}, u32[]{:S(2)}, u32[]{:S(2)}) collective-permute-start(f32[48,256]{1,0:T(8,128)} %bitcast.117), channel_id=1, source_target_pairs={{0,0},{1,1},{2,32},{3,33},{4,64},{5,65},{6,96},{7,97},{8,8},{9,9},... | collective-permute-start | bytes 147464 | tf_op jit(solution)/shard_map/ppermute | solution.py:73
  7.5 15.8 %collective-permute-start.1 = (f32[48,256]{1,0:T(8,128)}, f32[48,256]{1,0:T(8,128)S(1)}, u32[]{:S(2)}, u32[]{:S(2)}) collective-permute-start(f32[48,256]{1,0:T(8,128)} %bitcast.118), channel_id=1, source_target_pairs={{0,32},{1,33},{2,0},{3,1},{4,96},{5,97},{6,64},{7,65},{8,40},{9,41... | collective-permute-start | bytes 147464 | tf_op jit(solution)/shard_map/ppermute | solution.py:74
  9.4 13.9 %collective-permute-start.2 = (f32[1,256,128]{2,1,0:T(8,128)}, f32[1,256,128]{2,1,0:T(8,128)S(1)}, u32[]{:S(2)}, u32[]{:S(2)}) collective-permute-start(f32[1,256,128]{2,1,0:T(8,128)} %bitcast.113), channel_id=1, source_target_pairs={{0,16},{16,0},{1,17},{17,1},{2,18},{18,2},{3,19},{19,3},{4,20},{20... | collective-permute-start | bytes 393224 | tf_op jit(solution)/shard_map/ppermute | solution.py:31
  12.4 7.2 %collective-permute-start.6 = (f32[1,48,256]{2,1,0:T(8,128)}, f32[1,48,256]{2,1,0:T(8,128)S(1)}, u32[]{:S(2)}, u32[]{:S(2)}) collective-permute-start(f32[1,48,256]{2,1,0:T(8,128)} %bitcast.119), channel_id=1, source_target_pairs={{0,4},{4,0},{1,5},{5,1},{2,6},{6,2},{3,7},{7,3},{8,12},{12,8},{9,1... | collective-permute-start | bytes 147464 | tf_op jit(solution)/shard_map/ppermute | solution.py:31
  16.2 0.7 copy-start.4
  16.2 0.7 copy-start.3
  16.2 3.4 %copy-start.2 = (f32[256,3,16]{0,2,1:T(8,128)S(1)}, f32[256,3,16]{0,2,1:T(8,128)}, u32[]{:S(2)}) copy-start(f32[256,3,16]{0,2,1:T(8,128)} %param.6) | copy-start | bytes 147460
  19.6 3.7 %copy-start.1 = (f32[256,128]{1,0:T(8,128)S(1)}, f32[256,128]{1,0:T(8,128)}, u32[]{:S(2)}) copy-start(f32[256,128]{1,0:T(8,128)} %param.5) | copy-start | bytes 393220
  19.6 18.9 %collective-permute-start.7 = (f32[2,48,256]{2,1,0:T(8,128)S(1)}, f32[2,48,256]{2,1,0:T(8,128)S(1)}, u32[]{:S(2)}, u32[]{:S(2)}) collective-permute-start(f32[2,48,256]{2,1,0:T(8,128)S(1)} %pad_maximum_fusion.6), channel_id=1, source_target_pairs={{0,2},{2,0},{1,3},{3,1},{4,6},{6,4},{5,7},{7,5},{8,10},{10,8},{9,1... | collective-permute-start | bytes 294920 | tf_op jit(solution)/shard_map/ppermute | solution.py:31
  23.4 15.1 %collective-permute-start.3 = (f32[2,256,128]{2,1,0:T(8,128)S(1)}, f32[2,256,128]{2,1,0:T(8,128)S(1)}, u32[]{:S(2)}, u32[]{:S(2)}) collective-permute-start(f32[2,256,128]{2,1,0:T(8,128)S(1)} %pad_maximum_fusion.4), channel_id=1, source_target_pairs={{0,8},{8,0},{1,9},{9,1},{2,10},{10,2},{3,11},{11,3},{4,12},{12,4},... | collective-permute-start | bytes 786440 | tf_op jit(solution)/shard_map/ppermute | solution.py:31
  28.1 31.2 %all-to-all-start = ((f32[8,96,256]{2,1,0:T(8,128)}), f32[8,96,256]{2,1,0:T(8,128)S(1)}, u32[]{:S(2)}, u32[]{:S(2)}) async-start(f32[8,96,256]{2,1,0:T(8,128)} %broadcast_in_dim.22), calls=%async_computation | async-start | bytes 1572864 | tf_op jit(solution)/shard_map/all_to_all | solution.py:27
  38.6 13.7 %collective-permute-start.4 = (f32[4,256,128]{2,1,0:T(8,128)S(1)}, f32[4,256,128]{2,1,0:T(8,128)S(1)}, u32[]{:S(2)}, u32[]{:S(2)}) collective-permute-start(f32[4,256,128]{2,1,0:T(8,128)S(1)} %pad_maximum_fusion), channel_id=1, source_target_pairs={{0,1},{1,0},{2,3},{3,2},{4,5},{5,4},{6,7},{7,6},{8,9},{9,8},{10,11... | collective-permute-start | bytes 1572872 | tf_op jit(solution)/shard_map/ppermute | solution.py:31
  40.5 10.8 %collective-permute-start.8 = (f32[4,48,256]{2,1,0:T(8,128)S(1)}, f32[4,48,256]{2,1,0:T(8,128)}, u32[]{:S(2)}, u32[]{:S(2)}) collective-permute-start(f32[4,48,256]{2,1,0:T(8,128)S(1)} %pad_maximum_fusion.5), channel_id=1, source_target_pairs={{0,16},{16,0},{1,17},{17,1},{2,18},{18,2},{3,19},{19,3},{4,20},{20... | collective-permute-start | bytes 589832 | tf_op jit(solution)/shard_map/ppermute | solution.py:31
  61.7 10.7 %all-to-all-start.1 = ((f32[4,48,256]{2,1,0:T(8,128)}), f32[4,48,256]{2,1,0:T(8,128)S(1)}, u32[]{:S(2)}, u32[]{:S(2)}) async-start(f32[4,48,256]{2,1,0:T(8,128)} %bitcast.16), calls=%async_computation.1 | async-start | bytes 393216 | tf_op jit(solution)/shard_map/all_to_all | solution.py:27
  66.8 9.7 %collective-permute-start.9 = (f32[8,48,256]{2,1,0:T(8,128)S(1)}, f32[8,48,256]{2,1,0:T(8,128)S(1)}, u32[]{:S(2)}, u32[]{:S(2)}) collective-permute-start(f32[8,48,256]{2,1,0:T(8,128)S(1)} %pad_maximum_fusion.1), channel_id=1, source_target_pairs={{0,8},{8,0},{1,9},{9,1},{2,10},{10,2},{3,11},{11,3},{4,12},{12,4},... | collective-permute-start | bytes 1179656 | tf_op jit(solution)/shard_map/ppermute | solution.py:90
  72.5 3.1 %collective-permute-start.5 = (f32[48,256]{1,0:T(8,128)S(1)}, f32[48,256]{1,0:T(8,128)S(1)}, u32[]{:S(2)}, u32[]{:S(2)}) collective-permute-start(f32[48,256]{1,0:T(8,128)S(1)} %reduce_sum.20), channel_id=1, source_target_pairs={{0,1},{1,0},{2,3},{3,2},{4,5},{5,4},{6,7},{7,6},{8,9},{9,8},{10,11... | collective-permute-start | bytes 147464 | tf_op jit(solution)/shard_map/ppermute | solution.py:101
  78.3 19.7 %all-to-all-start.2 = ((f32[16,1,1536]{2,1,0:T(1,128)}), f32[16,1,1536]{2,1,0:T(1,128)S(1)}, u32[]{:S(2)}, u32[]{:S(2)}) async-start(f32[16,1,1536]{2,1,0:T(1,128)} %all_to_all.20), calls=%async_computation.2 | async-start | bytes 196608 | tf_op jit(solution)/shard_map/all_to_all | solution.py:27
  98.9 24.6 %all-to-all-start.3 = ((f32[32,16,128]{2,1,0:T(8,128)}), f32[32,16,128]{2,1,0:T(8,128)S(1)}, u32[]{:S(2)}, u32[]{:S(2)}) async-start(f32[32,16,128]{2,1,0:T(8,128)} %select_maximum_fusion), calls=%async_computation.3 | async-start | bytes 524288 | tf_op jit(solution)/shard_map/all_to_all | solution.py:27
  106.6 16.2 %collective-permute-start.10 = (f32[3,32,128]{2,1,0:T(8,128)S(1)}, f32[3,32,128]{2,1,0:T(8,128)S(1)}, u32[]{:S(2)}, u32[]{:S(2)}) collective-permute-start(f32[3,32,128]{2,1,0:T(8,128)S(1)} %constant_dynamic-slice_fusion), channel_id=1, source_target_pairs={{0,0},{1,1},{2,32},{3,33},{4,64},{5,65},{6,96},{7,97},{8,128},{9,1... | collective-permute-start | bytes 147464 | tf_op jit(solution)/shard_map/ppermute | solution.py:121

commit v12 on v11

--- a/solution.py
+++ b/solution.py
@@ -97,13 +97,11 @@
                 factor[high, low], block, (((1,), (1,)), ((), ())), precision=HIGHEST
             )
     product = exchange(product.reshape(nyl, wide, rows), COL[2:4])
-    plain = jnp.sum(product, axis=0)
+    plain = jnp.sum(product, axis=0).reshape(sibs, width, rows) * -own_mask
     other = lax.ppermute(plain, "core", [(0, 1), (1, 0)])
     pair = [jnp.where(core == 0, plain, other), jnp.where(core == 0, other, plain)]
-    pair = [block.reshape(sibs, width, rows) for block in pair]
-    pair = -jnp.concatenate(pair, 1)
+    pair = jnp.concatenate(pair, 1)
     half = lax.dynamic_slice_in_dim(pair, core * cols, cols, 2)
-    pair = pair * own_mask
 
     terms = []
     for source in (panel_all, panel_far):
@@ -123,8 +121,8 @@
     ainv_ki = ainv_ki * tile[:, :, None]
 
     share = rows // ncols
-    split = -plain.reshape(sibs, width, rows) * own_mask
-    split = split.reshape(wide, ncols, share).transpose(1, 0, 2).reshape(ncols, -1, TILE)
+    split = plain.reshape(wide, ncols, share)
+    split = split.transpose(1, 0, 2).reshape(ncols, -1, TILE)
     diag = diag.reshape(-1, TILE)
     mid = diag.shape[0]
     joined = jnp.concatenate([jnp.broadcast_to(diag, (ncols, *diag.shape)), split], 1)

time: 127 us -> 120 us (0.945)
  waiting for transfers between devices: 47.7 us -> 40.4 us
    ppermute x6, waiting for transfers between devices: 9.77 us -> 1.33 us  [doubled(): other = lax.ppermute(block, axis, [(0, 1), (1, 0)])]
    ppermute x1, waiting for transfers between devices: 0.85 us -> 3.6 us  [shards(): panel_far = lax.ppermute(panel_all, 'xl', [(0, 1), (1, 0)])]
    all_to_all x4, waiting for transfers between devices: 22.8 us -> 20.2 us  [exchange(): return lax.all_to_all(blocks, axes, split_axis=0, concat_axis=0, tiled=True)]
    ppermute x1, starting transfers between devices: 2.2 us -> 4 us  [shards(): panel_far = lax.ppermute(panel_all, 'xl', [(0, 1), (1, 0)])]
    all_to_all x4, starting transfers between devices: 29.9 us -> 28.5 us  [exchange(): return lax.all_to_all(blocks, axes, split_axis=0, concat_axis=0, tiled=True)]
  transfers between devices with their start and end apart: 15 -> 15, of which waited for: 8 -> 8; matrix products, arithmetic and copies ran while one was open for 4% -> 6% of each run, Pallas kernels for 0% -> 0%
where the time goes in v12:
time: 120 us; the launch traced here: 119 us
  starting transfers between devices  64.3 us (54%)
  waiting for transfers between devices  40.4 us (34%)
  local copies, waits for them, and re-layouts  6.87 us (6%)
  matrix products  3.29 us (3%)
  other arithmetic  3.1 us (3%)
    all_to_all x4, starting transfers between devices, exchange(): return lax.all_to_all(blocks, axes, split_axis=0, concat_axis=0, tiled=True)  28.5 us
    all_to_all x4, waiting for transfers between devices, exchange(): return lax.all_to_all(blocks, axes, split_axis=0, concat_axis=0, tiled=True)  20.2 us
    ppermute x6, starting transfers between devices, doubled(): other = lax.ppermute(block, axis, [(0, 1), (1, 0)])  19.1 us
    ppermute x1, waiting for transfers between devices, shards(): ainv_ki = lax.ppermute(half, ROW + COL, transposed(nrows))  14.1 us
    ppermute x1, starting transfers between devices, shards(): same = lax.ppermute(panel, ROW + COL, digit_swap(0))  6.85 us
    ppermute x1, starting transfers between devices, shards(): panel_far = lax.ppermute(panel_all, 'xl', [(0, 1), (1, 0)])  4 us
    ppermute x1, waiting for transfers between devices, shards(): panel_far = lax.ppermute(panel_all, 'xl', [(0, 1), (1, 0)])  3.6 us
  transfers between devices with their start and end apart: 15, of which 8 were waited for; matrix products, arithmetic and copies ran while one was open for 6% of the time, Pallas kernels for 0%

profile of v12, /device:TPU:12, one launch (start us, length us, event | category | flops | bytes accessed | tf_op | source)
XLA Modules:
  0.0 119.1 jit_solution(15588486248268017458)
XLA Ops:
  0.6 0.0 copy-start
  0.6 6.9 %collective-permute-start = (f32[48,256]{1,0:T(8,128)}, f32[48,256]{1,0:T(8,128)S(1)}, u32[]{:S(2)}, u32[]{:S(2)}) collective-permute-start(f32[48,256]{1,0:T(8,128)} %bitcast.111), channel_id=1, source_target_pairs={{0,0},{1,1},{2,32},{3,33},{4,64},{5,65},{6,96},{7,97},{8,8},{9,9},... | collective-permute-start | bytes 147464 | tf_op jit(solution)/shard_map/ppermute | solution.py:73
  7.5 1.9 %collective-permute-start.1 = (f32[48,256]{1,0:T(8,128)}, f32[48,256]{1,0:T(8,128)S(1)}, u32[]{:S(2)}, u32[]{:S(2)}) collective-permute-start(f32[48,256]{1,0:T(8,128)} %bitcast.112), channel_id=1, source_target_pairs={{0,32},{1,33},{2,0},{3,1},{4,96},{5,97},{6,64},{7,65},{8,40},{9,41... | collective-permute-start | bytes 147464 | tf_op jit(solution)/shard_map/ppermute | solution.py:74
  9.4 2.9 %collective-permute-start.2 = (f32[1,256,128]{2,1,0:T(8,128)}, f32[1,256,128]{2,1,0:T(8,128)S(1)}, u32[]{:S(2)}, u32[]{:S(2)}) collective-permute-start(f32[1,256,128]{2,1,0:T(8,128)} %bitcast.107), channel_id=1, source_target_pairs={{0,16},{16,0},{1,17},{17,1},{2,18},{18,2},{3,19},{19,3},{4,20},{20... | collective-permute-start | bytes 393224 | tf_op jit(solution)/shard_map/ppermute | solution.py:31
  12.4 3.8 %collective-permute-start.6 = (f32[1,48,256]{2,1,0:T(8,128)}, f32[1,48,256]{2,1,0:T(8,128)S(1)}, u32[]{:S(2)}, u32[]{:S(2)}) collective-permute-start(f32[1,48,256]{2,1,0:T(8,128)} %bitcast.113), channel_id=1, source_target_pairs={{0,4},{4,0},{1,5},{5,1},{2,6},{6,2},{3,7},{7,3},{8,12},{12,8},{9,1... | collective-permute-start | bytes 147464 | tf_op jit(solution)/shard_map/ppermute | solution.py:31
  16.2 0.6 copy-done.4
  16.8 0.1 iota_compare_fusion.2
  16.9 0.1 fusion.23
  17.0 0.1 constant_dynamic-slice_fusion
  17.1 0.1 broadcast_bitcast_fusion.1
  17.2 0.0 collective-permute-done
  17.2 1.0 collective-permute-done.1
  18.2 1.0 broadcast_in_dim.22
  19.1 10.4 %all-to-all-start = ((f32[8,96,256]{2,1,0:T(8,128)}), f32[8,96,256]{2,1,0:T(8,128)S(1)}, u32[]{:S(2)}, u32[]{:S(2)}) async-start(f32[8,96,256]{2,1,0:T(8,128)} %broadcast_in_dim.22), calls=%async_computation | async-start | bytes 1572864 | tf_op jit(solution)/shard_map/all_to_all | solution.py:27
  29.6 0.0 collective-permute-done.2
  29.6 0.0 copy-start.2
  29.7 2.6 %collective-permute-start.3 = (f32[2,256,128]{2,1,0:T(8,128)S(1)}, f32[2,256,128]{2,1,0:T(8,128)S(1)}, u32[]{:S(2)}, u32[]{:S(2)}) collective-permute-start(f32[2,256,128]{2,1,0:T(8,128)S(1)} %pad_maximum_fusion.4), channel_id=1, source_target_pairs={{0,8},{8,0},{1,9},{9,1},{2,10},{10,2},{3,11},{11,3},{4,12},{12,4},... | collective-permute-start | bytes 786440 | tf_op jit(solution)/shard_map/ppermute | solution.py:31
  32.2 0.0 collective-permute-done.6
  32.3 4.3 %collective-permute-start.7 = (f32[2,48,256]{2,1,0:T(8,128)S(1)}, f32[2,48,256]{2,1,0:T(8,128)S(1)}, u32[]{:S(2)}, u32[]{:S(2)}) collective-permute-start(f32[2,48,256]{2,1,0:T(8,128)S(1)} %pad_maximum_fusion.7), channel_id=1, source_target_pairs={{0,2},{2,0},{1,3},{3,1},{4,6},{6,4},{5,7},{7,5},{8,10},{10,8},{9,1... | collective-permute-start | bytes 294920 | tf_op jit(solution)/shard_map/ppermute | solution.py:31
  36.6 1.3 %collective-permute-done.3 = f32[2,256,128]{2,1,0:T(8,128)S(1)} collective-permute-done((f32[2,256,128]{2,1,0:T(8,128)S(1)}, f32[2,256,128]{2,1,0:T(8,128)S(1)}, u32[]{:S(2)}, u32[]{:S(2)}) %collective-permute-start.3) | collective-permute-done | bytes 262176 | tf_op jit(solution)/shard_map/ppermute | solution.py:31
  38.0 1.9 %collective-permute-start.4 = (f32[4,256,128]{2,1,0:T(8,128)S(1)}, f32[4,256,128]{2,1,0:T(8,128)S(1)}, u32[]{:S(2)}, u32[]{:S(2)}) collective-permute-start(f32[4,256,128]{2,1,0:T(8,128)S(1)} %pad_maximum_fusion), channel_id=1, source_target_pairs={{0,1},{1,0},{2,3},{3,2},{4,5},{5,4},{6,7},{7,6},{8,9},{9,8},{10,11... | collective-permute-start | bytes 1572872 | tf_op jit(solution)/shard_map/ppermute | solution.py:31
  39.9 0.1 broadcast_bitcast_fusion
  40.0 0.0 collective-permute-done.7
  40.1 3.6 %collective-permute-start.8 = (f32[4,48,256]{2,1,0:T(8,128)S(1)}, f32[4,48,256]{2,1,0:T(8,128)}, u32[]{:S(2)}, u32[]{:S(2)}) collective-permute-start(f32[4,48,256]{2,1,0:T(8,128)S(1)} %pad_maximum_fusion.5), channel_id=1, source_target_pairs={{0,16},{16,0},{1,17},{17,1},{2,18},{18,2},{3,19},{19,3},{4,20},{20... | collective-permute-start | bytes 589832 | tf_op jit(solution)/shard_map/ppermute | solution.py:31
  43.7 0.1 broadcast_select_fusion
  43.8 7.0 %all-to-all-done = f32[8,96,256]{2,1,0:T(8,128)S(1)} async-done(((f32[8,96,256]{2,1,0:T(8,128)}), f32[8,96,256]{2,1,0:T(8,128)S(1)}, u32[]{:S(2)}, u32[]{:S(2)}) %all-to-all-start) | async-done | bytes 786464 | tf_op jit(solution)/shard_map/all_to_all | solution.py:27
  50.8 0.4 fusion.12
  51.2 0.4 convolution_add_fusion.2
  51.6 0.4 convolution_add_fusion.1
  52.1 1.1 convolution_add_fusion
  53.2 5.1 %all-to-all-start.1 = ((f32[4,48,256]{2,1,0:T(8,128)}), f32[4,48,256]{2,1,0:T(8,128)S(1)}, u32[]{:S(2)}, u32[]{:S(2)}) async-start(f32[4,48,256]{2,1,0:T(8,128)} %bitcast.16), calls=%async_computation.1 | async-start | bytes 393216 | tf_op jit(solution)/shard_map/all_to_all | solution.py:27
  58.3 0.0 collective-permute-done.8
  58.3 1.0 broadcast_select_fusion.5
  59.3 4.0 %collective-permute-start.9 = (f32[8,48,256]{2,1,0:T(8,128)S(1)}, f32[8,48,256]{2,1,0:T(8,128)S(1)}, u32[]{:S(2)}, u32[]{:S(2)}) collective-permute-start(f32[8,48,256]{2,1,0:T(8,128)S(1)} %pad_maximum_fusion.1), channel_id=1, source_target_pairs={{0,8},{8,0},{1,9},{9,1},{2,10},{10,2},{3,11},{11,3},{4,12},{12,4},... | collective-permute-start | bytes 1179656 | tf_op jit(solution)/shard_map/ppermute | solution.py:90
  63.3 0.7 all-to-all-done.1
  64.0 1.9 %collective-permute-start.5 = (f32[3,16,256]{2,1,0:T(8,128)S(1)}, f32[3,16,256]{2,1,0:T(8,128)S(1)}, u32[]{:S(2)}, u32[]{:S(2)}) collective-permute-start(f32[3,16,256]{2,1,0:T(8,128)S(1)} %broadcast_multiply_fusion.1), channel_id=1, source_target_pairs={{0,1},{1,0},{2,3},{3,2},{4,5},{5,4},{6,7},{7,6},{8,9},{9,8},{10,11... | collective-permute-start | bytes 147464 | tf_op jit(solution)/shard_map/ppermute | solution.py:101
  65.9 0.1 constant_dynamic-slice_fusion.1
  66.0 0.1 copy.69
  66.1 0.1 reshape.95
  66.2 0.3 mul.95.clone
  66.6 0.2 mul.97
  66.8 0.1 copy.60
  66.9 0.2 collective-permute-done.5
  67.1 3.6 %collective-permute-done.9 = f32[8,48,256]{2,1,0:T(8,128)S(1)} collective-permute-done((f32[8,48,256]{2,1,0:T(8,128)S(1)}, f32[8,48,256]{2,1,0:T(8,128)S(1)}, u32[]{:S(2)}, u32[]{:S(2)}) %collective-permute-start.9) | collective-permute-done | bytes 393248 | tf_op jit(solution)/shard_map/ppermute | solution.py:90
  70.7 0.5 fusion
  71.2 0.5 select_bitcast_fusion.1
  71.7 0.9 all_to_all.20
  72.6 5.4 %all-to-all-start.2 = ((f32[16,1,1536]{2,1,0:T(1,128)}), f32[16,1,1536]{2,1,0:T(1,128)S(1)}, u32[]{:S(2)}, u32[]{:S(2)}) async-start(f32[16,1,1536]{2,1,0:T(1,128)} %all_to_all.20), calls=%async_computation.2 | async-start | bytes 196608 | tf_op jit(solution)/shard_map/all_to_all | solution.py:27
  78.0 0.1 copy.62
  78.1 0.1 copy.63
  78.2 12.5 %all-to-all-done.2 = f32[16,1,1536]{2,1,0:T(1,128)S(1)} async-done(((f32[16,1,1536]{2,1,0:T(1,128)}), f32[16,1,1536]{2,1,0:T(1,128)S(1)}, u32[]{:S(2)}, u32[]{:S(2)}) %all-to-all-start.2) | async-done | bytes 98336 | tf_op jit(solution)/shard_map/all_to_all | solution.py:27
  90.8 0.1 reduce_sum.21
  90.9 0.7 select_maximum_fusion
  91.6 7.7 %all-to-all-start.3 = ((f32[32,16,128]{2,1,0:T(8,128)}), f32[32,16,128]{2,1,0:T(8,128)S(1)}, u32[]{:S(2)}, u32[]{:S(2)}) async-start(f32[32,16,128]{2,1,0:T(8,128)} %select_maximum_fusion), calls=%async_computation.3 | async-start | bytes 524288 | tf_op jit(solution)/shard_map/all_to_all | solution.py:27
  99.3 1.9 %collective-permute-start.10 = (f32[3,32,128]{2,1,0:T(8,128)S(1)}, f32[3,32,128]{2,1,0:T(8,128)S(1)}, u32[]{:S(2)}, u32[]{:S(2)}) collective-permute-start(f32[3,32,128]{2,1,0:T(8,128)S(1)} %fusion.21), channel_id=1, source_target_pairs={{0,0},{1,1},{2,32},{3,33},{4,64},{5,65},{6,96},{7,97},{8,128},{9,1... | collective-permute-start | bytes 147464 | tf_op jit(solution)/shard_map/ppermute | solution.py:119
  101.3 0.2 dynamic-slice_reduce_fusion
  101.5 14.1 %collective-permute-done.10 = f32[3,32,128]{2,1,0:T(8,128)S(1)} collective-permute-done((f32[3,32,128]{2,1,0:T(8,128)S(1)}, f32[3,32,128]{2,1,0:T(8,128)S(1)}, u32[]{:S(2)}, u32[]{:S(2)}) %collective-permute-start.10) | collective-permute-done | bytes 49184 | tf_op jit(solution)/shard_map/ppermute | solution.py:119
  115.5 0.7 broadcast_multiply_fusion
  116.2 0.2 reshape.106
  116.4 0.5 copy.66
  116.9 1.0 reshape.107
  117.9 0.1 copy.68
  118.0 0.2 copy.65
  118.2 0.8 reshape.105
  (33 shorter events, 0.4 us)
Async XLA Ops:
  0.6 65.3 %copy-start = (f32[3,32,512]{2,1,0:T(8,128)S(1)}, f32[3,32,512]{2,1,0:T(8,128)}, u32[]{:S(2)}) copy-start(f32[3,32,512]{2,1,0:T(8,128)} %param.7) | copy-start | bytes 589828
  0.6 16.5 %collective-permute-start = (f32[48,256]{1,0:T(8,128)}, f32[48,256]{1,0:T(8,128)S(1)}, u32[]{:S(2)}, u32[]{:S(2)}) collective-permute-start(f32[48,256]{1,0:T(8,128)} %bitcast.111), channel_id=1, source_target_pairs={{0,0},{1,1},{2,32},{3,33},{4,64},{5,65},{6,96},{7,97},{8,8},{9,9},... | collective-permute-start | bytes 147464 | tf_op jit(solution)/shard_map/ppermute | solution.py:73
  7.5 10.6 %collective-permute-start.1 = (f32[48,256]{1,0:T(8,128)}, f32[48,256]{1,0:T(8,128)S(1)}, u32[]{:S(2)}, u32[]{:S(2)}) collective-permute-start(f32[48,256]{1,0:T(8,128)} %bitcast.112), channel_id=1, source_target_pairs={{0,32},{1,33},{2,0},{3,1},{4,96},{5,97},{6,64},{7,65},{8,40},{9,41... | collective-permute-start | bytes 147464 | tf_op jit(solution)/shard_map/ppermute | solution.py:74
  9.4 20.1 %collective-permute-start.2 = (f32[1,256,128]{2,1,0:T(8,128)}, f32[1,256,128]{2,1,0:T(8,128)S(1)}, u32[]{:S(2)}, u32[]{:S(2)}) collective-permute-start(f32[1,256,128]{2,1,0:T(8,128)} %bitcast.107), channel_id=1, source_target_pairs={{0,16},{16,0},{1,17},{17,1},{2,18},{18,2},{3,19},{19,3},{4,20},{20... | collective-permute-start | bytes 393224 | tf_op jit(solution)/shard_map/ppermute | solution.py:31
  12.4 19.9 %collective-permute-start.6 = (f32[1,48,256]{2,1,0:T(8,128)}, f32[1,48,256]{2,1,0:T(8,128)S(1)}, u32[]{:S(2)}, u32[]{:S(2)}) collective-permute-start(f32[1,48,256]{2,1,0:T(8,128)} %bitcast.113), channel_id=1, source_target_pairs={{0,4},{4,0},{1,5},{5,1},{2,6},{6,2},{3,7},{7,3},{8,12},{12,8},{9,1... | collective-permute-start | bytes 147464 | tf_op jit(solution)/shard_map/ppermute | solution.py:31
  16.2 0.7 copy-start.4
  16.2 0.7 copy-start.3
  19.1 10.4 %copy-start.1 = (f32[256,128]{1,0:T(8,128)S(1)}, f32[256,128]{1,0:T(8,128)}, u32[]{:S(2)}) copy-start(f32[256,128]{1,0:T(8,128)} %param.5) | copy-start | bytes 393220
  19.1 31.6 %all-to-all-start = ((f32[8,96,256]{2,1,0:T(8,128)}), f32[8,96,256]{2,1,0:T(8,128)S(1)}, u32[]{:S(2)}, u32[]{:S(2)}) async-start(f32[8,96,256]{2,1,0:T(8,128)} %broadcast_in_dim.22), calls=%async_computation | async-start | bytes 1572864 | tf_op jit(solution)/shard_map/all_to_all | solution.py:27
  29.6 2.6 %copy-start.2 = (f32[256,3,16]{0,2,1:T(8,128)S(1)}, f32[256,3,16]{0,2,1:T(8,128)}, u32[]{:S(2)}) copy-start(f32[256,3,16]{0,2,1:T(8,128)} %param.6) | copy-start | bytes 147460
  29.7 8.3 %collective-permute-start.3 = (f32[2,256,128]{2,1,0:T(8,128)S(1)}, f32[2,256,128]{2,1,0:T(8,128)S(1)}, u32[]{:S(2)}, u32[]{:S(2)}) collective-permute-start(f32[2,256,128]{2,1,0:T(8,128)S(1)} %pad_maximum_fusion.4), channel_id=1, source_target_pairs={{0,8},{8,0},{1,9},{9,1},{2,10},{10,2},{3,11},{11,3},{4,12},{12,4},... | collective-permute-start | bytes 786440 | tf_op jit(solution)/shard_map/ppermute | solution.py:31
  32.3 7.7 %collective-permute-start.7 = (f32[2,48,256]{2,1,0:T(8,128)S(1)}, f32[2,48,256]{2,1,0:T(8,128)S(1)}, u32[]{:S(2)}, u32[]{:S(2)}) collective-permute-start(f32[2,48,256]{2,1,0:T(8,128)S(1)} %pad_maximum_fusion.7), channel_id=1, source_target_pairs={{0,2},{2,0},{1,3},{3,1},{4,6},{6,4},{5,7},{7,5},{8,10},{10,8},{9,1... | collective-permute-start | bytes 294920 | tf_op jit(solution)/shard_map/ppermute | solution.py:31
  38.0 5.7 %collective-permute-start.4 = (f32[4,256,128]{2,1,0:T(8,128)S(1)}, f32[4,256,128]{2,1,0:T(8,128)S(1)}, u32[]{:S(2)}, u32[]{:S(2)}) collective-permute-start(f32[4,256,128]{2,1,0:T(8,128)S(1)} %pad_maximum_fusion), channel_id=1, source_target_pairs={{0,1},{1,0},{2,3},{3,2},{4,5},{5,4},{6,7},{7,6},{8,9},{9,8},{10,11... | collective-permute-start | bytes 1572872 | tf_op jit(solution)/shard_map/ppermute | solution.py:31
  40.1 18.2 %collective-permute-start.8 = (f32[4,48,256]{2,1,0:T(8,128)S(1)}, f32[4,48,256]{2,1,0:T(8,128)}, u32[]{:S(2)}, u32[]{:S(2)}) collective-permute-start(f32[4,48,256]{2,1,0:T(8,128)S(1)} %pad_maximum_fusion.5), channel_id=1, source_target_pairs={{0,16},{16,0},{1,17},{17,1},{2,18},{18,2},{3,19},{19,3},{4,20},{20... | collective-permute-start | bytes 589832 | tf_op jit(solution)/shard_map/ppermute | solution.py:31
  53.2 10.8 %all-to-all-start.1 = ((f32[4,48,256]{2,1,0:T(8,128)}), f32[4,48,256]{2,1,0:T(8,128)S(1)}, u32[]{:S(2)}, u32[]{:S(2)}) async-start(f32[4,48,256]{2,1,0:T(8,128)} %bitcast.16), calls=%async_computation.1 | async-start | bytes 393216 | tf_op jit(solution)/shard_map/all_to_all | solution.py:27
  59.3 11.5 %collective-permute-start.9 = (f32[8,48,256]{2,1,0:T(8,128)S(1)}, f32[8,48,256]{2,1,0:T(8,128)S(1)}, u32[]{:S(2)}, u32[]{:S(2)}) collective-permute-start(f32[8,48,256]{2,1,0:T(8,128)S(1)} %pad_maximum_fusion.1), channel_id=1, source_target_pairs={{0,8},{8,0},{1,9},{9,1},{2,10},{10,2},{3,11},{11,3},{4,12},{12,4},... | collective-permute-start | bytes 1179656 | tf_op jit(solution)/shard_map/ppermute | solution.py:90
  64.0 3.1 %collective-permute-start.5 = (f32[3,16,256]{2,1,0:T(8,128)S(1)}, f32[3,16,256]{2,1,0:T(8,128)S(1)}, u32[]{:S(2)}, u32[]{:S(2)}) collective-permute-start(f32[3,16,256]{2,1,0:T(8,128)S(1)} %broadcast_multiply_fusion.1), channel_id=1, source_target_pairs={{0,1},{1,0},{2,3},{3,2},{4,5},{5,4},{6,7},{7,6},{8,9},{9,8},{10,11... | collective-permute-start | bytes 147464 | tf_op jit(solution)/shard_map/ppermute | solution.py:101
  72.6 18.2 %all-to-all-start.2 = ((f32[16,1,1536]{2,1,0:T(1,128)}), f32[16,1,1536]{2,1,0:T(1,128)S(1)}, u32[]{:S(2)}, u32[]{:S(2)}) async-start(f32[16,1,1536]{2,1,0:T(1,128)} %all_to_all.20), calls=%async_computation.2 | async-start | bytes 196608 | tf_op jit(solution)/shard_map/all_to_all | solution.py:27
  91.6 24.6 %all-to-all-start.3 = ((f32[32,16,128]{2,1,0:T(8,128)}), f32[32,16,128]{2,1,0:T(8,128)S(1)}, u32[]{:S(2)}, u32[]{:S(2)}) async-start(f32[32,16,128]{2,1,0:T(8,128)} %select_maximum_fusion), calls=%async_computation.3 | async-start | bytes 524288 | tf_op jit(solution)/shard_map/all_to_all | solution.py:27
  99.3 16.2 %collective-permute-start.10 = (f32[3,32,128]{2,1,0:T(8,128)S(1)}, f32[3,32,128]{2,1,0:T(8,128)S(1)}, u32[]{:S(2)}, u32[]{:S(2)}) collective-permute-start(f32[3,32,128]{2,1,0:T(8,128)S(1)} %fusion.21), channel_id=1, source_target_pairs={{0,0},{1,1},{2,32},{3,33},{4,64},{5,65},{6,96},{7,97},{8,128},{9,1... | collective-permute-start | bytes 147464 | tf_op jit(solution)/shard_map/ppermute | solution.py:119

commit v13 on v12

--- a/solution.py
+++ b/solution.py
@@ -111,10 +111,13 @@
     first = jnp.where(xl == 0, terms[0], terms[1])
     second = jnp.where(xl == 0, terms[1], terms[0])
     term = jnp.stack([first, second], 1)
-    term = exchange(term.reshape(nrows, -1), ROW)
+    term = term.reshape(nrows, -1, TILE)
+    mid = term.shape[1]
+    term = jnp.pad(term, ((0, 0), (0, -mid % 8), (0, 0)))
+    term = exchange(term, ROW)
     own = lax.dynamic_slice_in_dim(kk_inverse, core * width, width, 1)
     own = lax.dynamic_slice_in_dim(own, lax.axis_index(COL[:4]) * NCORE * width, NCORE * width, 2)
-    diag = own.reshape(-1) - jnp.sum(term, axis=0)
+    diag = own.reshape(mid, TILE) - jnp.sum(term, axis=0)[:mid]
 
     ainv_ki = lax.ppermute(half, ROW + COL, transposed(nrows))
     tile = lax.dynamic_slice_in_dim(tile_mask, lax.axis_index(COL), 1, 1)
@@ -123,8 +126,6 @@
     share = rows // ncols
     split = plain.reshape(wide, ncols, share)
     split = split.transpose(1, 0, 2).reshape(ncols, -1, TILE)
-    diag = diag.reshape(-1, TILE)
-    mid = diag.shape[0]
     joined = jnp.concatenate([jnp.broadcast_to(diag, (ncols, *diag.shape)), split], 1)
     joined = jnp.pad(joined, ((0, 0), (0, -joined.shape[1] % 8), (0, 0)))
     joined = exchange(joined, COL)

time: 120 us -> 120 us (level)
  no operation moved by 1% of the time
where the time goes in v13:
time: 120 us; the launch traced here: 119 us
  starting transfers between devices  64.4 us (54%)
  waiting for transfers between devices  40.4 us (34%)
  local copies, waits for them, and re-layouts  6.83 us (6%)
  matrix products  3.29 us (3%)
  other arithmetic  3.06 us (3%)
    all_to_all x4, starting transfers between devices, exchange(): return lax.all_to_all(blocks, axes, split_axis=0, concat_axis=0, tiled=True)  28.5 us
    all_to_all x4, waiting for transfers between devices, exchange(): return lax.all_to_all(blocks, axes, split_axis=0, concat_axis=0, tiled=True)  19.4 us
    ppermute x6, starting transfers between devices, doubled(): other = lax.ppermute(block, axis, [(0, 1), (1, 0)])  19.1 us
    ppermute x1, waiting for transfers between devices, shards(): ainv_ki = lax.ppermute(half, ROW + COL, transposed(nrows))  14 us
    ppermute x1, starting transfers between devices, shards(): same = lax.ppermute(panel, ROW + COL, digit_swap(0))  6.85 us
    ppermute x1, starting transfers between devices, shards(): panel_far = lax.ppermute(panel_all, 'xl', [(0, 1), (1, 0)])  4 us
    ppermute x1, waiting for transfers between devices, shards(): panel_far = lax.ppermute(panel_all, 'xl', [(0, 1), (1, 0)])  3.6 us
  transfers between devices with their start and end apart: 15, of which 8 were waited for; matrix products, arithmetic and copies ran while one was open for 6% of the time, Pallas kernels for 0%

profile of v13, /device:TPU:12, one launch (start us, length us, event | category | flops | bytes accessed | tf_op | source)
XLA Modules:
  0.0 119.1 jit_solution(11250266908047853108)
XLA Ops:
  0.6 0.0 copy-start
  0.6 6.9 %collective-permute-start = (f32[48,256]{1,0:T(8,128)}, f32[48,256]{1,0:T(8,128)S(1)}, u32[]{:S(2)}, u32[]{:S(2)}) collective-permute-start(f32[48,256]{1,0:T(8,128)} %bitcast.109), channel_id=1, source_target_pairs={{0,0},{1,1},{2,32},{3,33},{4,64},{5,65},{6,96},{7,97},{8,8},{9,9},... | collective-permute-start | bytes 147464 | tf_op jit(solution)/shard_map/ppermute | solution.py:73
  7.5 1.9 %collective-permute-start.1 = (f32[48,256]{1,0:T(8,128)}, f32[48,256]{1,0:T(8,128)S(1)}, u32[]{:S(2)}, u32[]{:S(2)}) collective-permute-start(f32[48,256]{1,0:T(8,128)} %bitcast.110), channel_id=1, source_target_pairs={{0,32},{1,33},{2,0},{3,1},{4,96},{5,97},{6,64},{7,65},{8,40},{9,41... | collective-permute-start | bytes 147464 | tf_op jit(solution)/shard_map/ppermute | solution.py:74
  9.4 2.9 %collective-permute-start.2 = (f32[1,256,128]{2,1,0:T(8,128)}, f32[1,256,128]{2,1,0:T(8,128)S(1)}, u32[]{:S(2)}, u32[]{:S(2)}) collective-permute-start(f32[1,256,128]{2,1,0:T(8,128)} %bitcast.105), channel_id=1, source_target_pairs={{0,16},{16,0},{1,17},{17,1},{2,18},{18,2},{3,19},{19,3},{4,20},{20... | collective-permute-start | bytes 393224 | tf_op jit(solution)/shard_map/ppermute | solution.py:31
  12.4 3.8 %collective-permute-start.6 = (f32[1,48,256]{2,1,0:T(8,128)}, f32[1,48,256]{2,1,0:T(8,128)S(1)}, u32[]{:S(2)}, u32[]{:S(2)}) collective-permute-start(f32[1,48,256]{2,1,0:T(8,128)} %bitcast.111), channel_id=1, source_target_pairs={{0,4},{4,0},{1,5},{5,1},{2,6},{6,2},{3,7},{7,3},{8,12},{12,8},{9,1... | collective-permute-start | bytes 147464 | tf_op jit(solution)/shard_map/ppermute | solution.py:31
  16.2 0.6 copy-done.4
  16.8 0.1 iota_compare_fusion.2
  16.9 0.1 fusion.23
  17.0 0.1 constant_dynamic-slice_fusion
  17.1 0.1 broadcast_bitcast_fusion.1
  17.2 0.0 collective-permute-done
  17.2 1.0 collective-permute-done.1
  18.2 1.0 broadcast_in_dim.22
  19.1 10.4 %all-to-all-start = ((f32[8,96,256]{2,1,0:T(8,128)}), f32[8,96,256]{2,1,0:T(8,128)S(1)}, u32[]{:S(2)}, u32[]{:S(2)}) async-start(f32[8,96,256]{2,1,0:T(8,128)} %broadcast_in_dim.22), calls=%async_computation | async-start | bytes 1572864 | tf_op jit(solution)/shard_map/all_to_all | solution.py:27
  29.6 0.0 collective-permute-done.2
  29.6 0.0 copy-start.2
  29.7 2.6 %collective-permute-start.3 = (f32[2,256,128]{2,1,0:T(8,128)S(1)}, f32[2,256,128]{2,1,0:T(8,128)S(1)}, u32[]{:S(2)}, u32[]{:S(2)}) collective-permute-start(f32[2,256,128]{2,1,0:T(8,128)S(1)} %pad_maximum_fusion.4), channel_id=1, source_target_pairs={{0,8},{8,0},{1,9},{9,1},{2,10},{10,2},{3,11},{11,3},{4,12},{12,4},... | collective-permute-start | bytes 786440 | tf_op jit(solution)/shard_map/ppermute | solution.py:31
  32.2 0.0 collective-permute-done.6
  32.3 4.3 %collective-permute-start.7 = (f32[2,48,256]{2,1,0:T(8,128)S(1)}, f32[2,48,256]{2,1,0:T(8,128)S(1)}, u32[]{:S(2)}, u32[]{:S(2)}) collective-permute-start(f32[2,48,256]{2,1,0:T(8,128)S(1)} %pad_maximum_fusion.7), channel_id=1, source_target_pairs={{0,2},{2,0},{1,3},{3,1},{4,6},{6,4},{5,7},{7,5},{8,10},{10,8},{9,1... | collective-permute-start | bytes 294920 | tf_op jit(solution)/shard_map/ppermute | solution.py:31
  36.6 1.3 %collective-permute-done.3 = f32[2,256,128]{2,1,0:T(8,128)S(1)} collective-permute-done((f32[2,256,128]{2,1,0:T(8,128)S(1)}, f32[2,256,128]{2,1,0:T(8,128)S(1)}, u32[]{:S(2)}, u32[]{:S(2)}) %collective-permute-start.3) | collective-permute-done | bytes 262176 | tf_op jit(solution)/shard_map/ppermute | solution.py:31
  38.0 1.9 %collective-permute-start.4 = (f32[4,256,128]{2,1,0:T(8,128)S(1)}, f32[4,256,128]{2,1,0:T(8,128)S(1)}, u32[]{:S(2)}, u32[]{:S(2)}) collective-permute-start(f32[4,256,128]{2,1,0:T(8,128)S(1)} %pad_maximum_fusion), channel_id=1, source_target_pairs={{0,1},{1,0},{2,3},{3,2},{4,5},{5,4},{6,7},{7,6},{8,9},{9,8},{10,11... | collective-permute-start | bytes 1572872 | tf_op jit(solution)/shard_map/ppermute | solution.py:31
  39.9 0.1 broadcast_bitcast_fusion
  40.1 3.6 %collective-permute-start.8 = (f32[4,48,256]{2,1,0:T(8,128)S(1)}, f32[4,48,256]{2,1,0:T(8,128)}, u32[]{:S(2)}, u32[]{:S(2)}) collective-permute-start(f32[4,48,256]{2,1,0:T(8,128)S(1)} %pad_maximum_fusion.5), channel_id=1, source_target_pairs={{0,16},{16,0},{1,17},{17,1},{2,18},{18,2},{3,19},{19,3},{4,20},{20... | collective-permute-start | bytes 589832 | tf_op jit(solution)/shard_map/ppermute | solution.py:31
  43.7 0.1 broadcast_select_fusion
  43.8 7.0 %all-to-all-done = f32[8,96,256]{2,1,0:T(8,128)S(1)} async-done(((f32[8,96,256]{2,1,0:T(8,128)}), f32[8,96,256]{2,1,0:T(8,128)S(1)}, u32[]{:S(2)}, u32[]{:S(2)}) %all-to-all-start) | async-done | bytes 786464 | tf_op jit(solution)/shard_map/all_to_all | solution.py:27
  50.8 0.4 fusion.12
  51.2 0.4 convolution_add_fusion.2
  51.6 0.4 convolution_add_fusion.1
  52.1 1.1 convolution_add_fusion
  53.2 5.1 %all-to-all-start.1 = ((f32[4,48,256]{2,1,0:T(8,128)}), f32[4,48,256]{2,1,0:T(8,128)S(1)}, u32[]{:S(2)}, u32[]{:S(2)}) async-start(f32[4,48,256]{2,1,0:T(8,128)} %bitcast.16), calls=%async_computation.1 | async-start | bytes 393216 | tf_op jit(solution)/shard_map/all_to_all | solution.py:27
  58.3 0.0 collective-permute-done.8
  58.3 1.0 broadcast_select_fusion.5
  59.3 4.0 %collective-permute-start.9 = (f32[8,48,256]{2,1,0:T(8,128)S(1)}, f32[8,48,256]{2,1,0:T(8,128)S(1)}, u32[]{:S(2)}, u32[]{:S(2)}) collective-permute-start(f32[8,48,256]{2,1,0:T(8,128)S(1)} %pad_maximum_fusion.1), channel_id=1, source_target_pairs={{0,8},{8,0},{1,9},{9,1},{2,10},{10,2},{3,11},{11,3},{4,12},{12,4},... | collective-permute-start | bytes 1179656 | tf_op jit(solution)/shard_map/ppermute | solution.py:90
  63.3 0.7 all-to-all-done.1
  64.0 1.9 %collective-permute-start.5 = (f32[3,16,256]{2,1,0:T(8,128)S(1)}, f32[3,16,256]{2,1,0:T(8,128)S(1)}, u32[]{:S(2)}, u32[]{:S(2)}) collective-permute-start(f32[3,16,256]{2,1,0:T(8,128)S(1)} %broadcast_multiply_fusion.1), channel_id=1, source_target_pairs={{0,1},{1,0},{2,3},{3,2},{4,5},{5,4},{6,7},{7,6},{8,9},{9,8},{10,11... | collective-permute-start | bytes 147464 | tf_op jit(solution)/shard_map/ppermute | solution.py:101
  65.9 1.2 collective-permute-done.5
  67.1 3.6 %collective-permute-done.9 = f32[8,48,256]{2,1,0:T(8,128)S(1)} collective-permute-done((f32[8,48,256]{2,1,0:T(8,128)S(1)}, f32[8,48,256]{2,1,0:T(8,128)S(1)}, u32[]{:S(2)}, u32[]{:S(2)}) %collective-permute-start.9) | collective-permute-done | bytes 393248 | tf_op jit(solution)/shard_map/ppermute | solution.py:90
  70.7 0.5 fusion
  71.2 0.5 select_bitcast_fusion.1
  71.7 0.1 reshape.98
  71.9 0.7 pad.8
  72.5 5.4 %all-to-all-start.2 = ((f32[16,16,128]{2,1,0:T(8,128)}), f32[16,16,128]{2,1,0:T(8,128)S(1)}, u32[]{:S(2)}, u32[]{:S(2)}) async-start(f32[16,16,128]{2,1,0:T(8,128)} %pad.8), calls=%async_computation.2 | async-start | bytes 262144 | tf_op jit(solution)/shard_map/all_to_all | solution.py:27
  77.9 0.1 constant_dynamic-slice_fusion.1
  78.0 0.1 copy.66
  78.1 0.1 reshape.91
  78.2 0.3 mul.95.clone
  78.6 0.2 mul.97
  78.8 0.1 copy.57
  78.9 0.1 copy.59
  79.1 0.1 copy.60
  79.2 11.7 %all-to-all-done.2 = f32[16,16,128]{2,1,0:T(8,128)S(1)} async-done(((f32[16,16,128]{2,1,0:T(8,128)}), f32[16,16,128]{2,1,0:T(8,128)S(1)}, u32[]{:S(2)}, u32[]{:S(2)}) %all-to-all-start.2) | async-done | bytes 131104 | tf_op jit(solution)/shard_map/all_to_all | solution.py:27
  91.0 0.7 select_maximum_fusion
  91.7 7.7 %all-to-all-start.3 = ((f32[32,16,128]{2,1,0:T(8,128)}), f32[32,16,128]{2,1,0:T(8,128)S(1)}, u32[]{:S(2)}, u32[]{:S(2)}) async-start(f32[32,16,128]{2,1,0:T(8,128)} %select_maximum_fusion), calls=%async_computation.3 | async-start | bytes 524288 | tf_op jit(solution)/shard_map/all_to_all | solution.py:27
  99.4 2.0 %collective-permute-start.10 = (f32[3,32,128]{2,1,0:T(8,128)S(1)}, f32[3,32,128]{2,1,0:T(8,128)S(1)}, u32[]{:S(2)}, u32[]{:S(2)}) collective-permute-start(f32[3,32,128]{2,1,0:T(8,128)S(1)} %fusion.21), channel_id=1, source_target_pairs={{0,0},{1,1},{2,32},{3,33},{4,64},{5,65},{6,96},{7,97},{8,128},{9,1... | collective-permute-start | bytes 147464 | tf_op jit(solution)/shard_map/ppermute | solution.py:122
  101.5 0.2 dynamic-slice_reduce_fusion
  101.7 14.0 %collective-permute-done.10 = f32[3,32,128]{2,1,0:T(8,128)S(1)} collective-permute-done((f32[3,32,128]{2,1,0:T(8,128)S(1)}, f32[3,32,128]{2,1,0:T(8,128)S(1)}, u32[]{:S(2)}, u32[]{:S(2)}) %collective-permute-start.10) | collective-permute-done | bytes 49184 | tf_op jit(solution)/shard_map/ppermute | solution.py:122
  115.6 0.7 broadcast_multiply_fusion
  116.3 0.0 all-to-all-done.3
  116.3 0.2 reshape.103
  116.5 0.5 copy.63
  117.0 1.0 reshape.104
  118.0 0.1 copy.65
  118.1 0.2 copy.62
  118.3 0.8 reshape.102
  (34 shorter events, 0.4 us)
Async XLA Ops:
  0.6 77.3 %copy-start = (f32[3,32,512]{2,1,0:T(8,128)S(1)}, f32[3,32,512]{2,1,0:T(8,128)}, u32[]{:S(2)}) copy-start(f32[3,32,512]{2,1,0:T(8,128)} %param.7) | copy-start | bytes 589828
  0.6 16.5 %collective-permute-start = (f32[48,256]{1,0:T(8,128)}, f32[48,256]{1,0:T(8,128)S(1)}, u32[]{:S(2)}, u32[]{:S(2)}) collective-permute-start(f32[48,256]{1,0:T(8,128)} %bitcast.109), channel_id=1, source_target_pairs={{0,0},{1,1},{2,32},{3,33},{4,64},{5,65},{6,96},{7,97},{8,8},{9,9},... | collective-permute-start | bytes 147464 | tf_op jit(solution)/shard_map/ppermute | solution.py:73
  7.5 10.6 %collective-permute-start.1 = (f32[48,256]{1,0:T(8,128)}, f32[48,256]{1,0:T(8,128)S(1)}, u32[]{:S(2)}, u32[]{:S(2)}) collective-permute-start(f32[48,256]{1,0:T(8,128)} %bitcast.110), channel_id=1, source_target_pairs={{0,32},{1,33},{2,0},{3,1},{4,96},{5,97},{6,64},{7,65},{8,40},{9,41... | collective-permute-start | bytes 147464 | tf_op jit(solution)/shard_map/ppermute | solution.py:74
  9.4 20.1 %collective-permute-start.2 = (f32[1,256,128]{2,1,0:T(8,128)}, f32[1,256,128]{2,1,0:T(8,128)S(1)}, u32[]{:S(2)}, u32[]{:S(2)}) collective-permute-start(f32[1,256,128]{2,1,0:T(8,128)} %bitcast.105), channel_id=1, source_target_pairs={{0,16},{16,0},{1,17},{17,1},{2,18},{18,2},{3,19},{19,3},{4,20},{20... | collective-permute-start | bytes 393224 | tf_op jit(solution)/shard_map/ppermute | solution.py:31
  12.4 19.9 %collective-permute-start.6 = (f32[1,48,256]{2,1,0:T(8,128)}, f32[1,48,256]{2,1,0:T(8,128)S(1)}, u32[]{:S(2)}, u32[]{:S(2)}) collective-permute-start(f32[1,48,256]{2,1,0:T(8,128)} %bitcast.111), channel_id=1, source_target_pairs={{0,4},{4,0},{1,5},{5,1},{2,6},{6,2},{3,7},{7,3},{8,12},{12,8},{9,1... | collective-permute-start | bytes 147464 | tf_op jit(solution)/shard_map/ppermute | solution.py:31
  16.2 0.7 copy-start.4
  16.2 0.7 copy-start.3
  19.1 10.4 %copy-start.1 = (f32[256,128]{1,0:T(8,128)S(1)}, f32[256,128]{1,0:T(8,128)}, u32[]{:S(2)}) copy-start(f32[256,128]{1,0:T(8,128)} %param.5) | copy-start | bytes 393220
  19.1 31.6 %all-to-all-start = ((f32[8,96,256]{2,1,0:T(8,128)}), f32[8,96,256]{2,1,0:T(8,128)S(1)}, u32[]{:S(2)}, u32[]{:S(2)}) async-start(f32[8,96,256]{2,1,0:T(8,128)} %broadcast_in_dim.22), calls=%async_computation | async-start | bytes 1572864 | tf_op jit(solution)/shard_map/all_to_all | solution.py:27
  29.6 2.6 %copy-start.2 = (f32[256,3,16]{0,2,1:T(8,128)S(1)}, f32[256,3,16]{0,2,1:T(8,128)}, u32[]{:S(2)}) copy-start(f32[256,3,16]{0,2,1:T(8,128)} %param.6) | copy-start | bytes 147460
  29.7 8.3 %collective-permute-start.3 = (f32[2,256,128]{2,1,0:T(8,128)S(1)}, f32[2,256,128]{2,1,0:T(8,128)S(1)}, u32[]{:S(2)}, u32[]{:S(2)}) collective-permute-start(f32[2,256,128]{2,1,0:T(8,128)S(1)} %pad_maximum_fusion.4), channel_id=1, source_target_pairs={{0,8},{8,0},{1,9},{9,1},{2,10},{10,2},{3,11},{11,3},{4,12},{12,4},... | collective-permute-start | bytes 786440 | tf_op jit(solution)/shard_map/ppermute | solution.py:31
  32.3 7.7 %collective-permute-start.7 = (f32[2,48,256]{2,1,0:T(8,128)S(1)}, f32[2,48,256]{2,1,0:T(8,128)S(1)}, u32[]{:S(2)}, u32[]{:S(2)}) collective-permute-start(f32[2,48,256]{2,1,0:T(8,128)S(1)} %pad_maximum_fusion.7), channel_id=1, source_target_pairs={{0,2},{2,0},{1,3},{3,1},{4,6},{6,4},{5,7},{7,5},{8,10},{10,8},{9,1... | collective-permute-start | bytes 294920 | tf_op jit(solution)/shard_map/ppermute | solution.py:31
  38.0 5.7 %collective-permute-start.4 = (f32[4,256,128]{2,1,0:T(8,128)S(1)}, f32[4,256,128]{2,1,0:T(8,128)S(1)}, u32[]{:S(2)}, u32[]{:S(2)}) collective-permute-start(f32[4,256,128]{2,1,0:T(8,128)S(1)} %pad_maximum_fusion), channel_id=1, source_target_pairs={{0,1},{1,0},{2,3},{3,2},{4,5},{5,4},{6,7},{7,6},{8,9},{9,8},{10,11... | collective-permute-start | bytes 1572872 | tf_op jit(solution)/shard_map/ppermute | solution.py:31
  40.1 18.2 %collective-permute-start.8 = (f32[4,48,256]{2,1,0:T(8,128)S(1)}, f32[4,48,256]{2,1,0:T(8,128)}, u32[]{:S(2)}, u32[]{:S(2)}) collective-permute-start(f32[4,48,256]{2,1,0:T(8,128)S(1)} %pad_maximum_fusion.5), channel_id=1, source_target_pairs={{0,16},{16,0},{1,17},{17,1},{2,18},{18,2},{3,19},{19,3},{4,20},{20... | collective-permute-start | bytes 589832 | tf_op jit(solution)/shard_map/ppermute | solution.py:31
  53.2 10.8 %all-to-all-start.1 = ((f32[4,48,256]{2,1,0:T(8,128)}), f32[4,48,256]{2,1,0:T(8,128)S(1)}, u32[]{:S(2)}, u32[]{:S(2)}) async-start(f32[4,48,256]{2,1,0:T(8,128)} %bitcast.16), calls=%async_computation.1 | async-start | bytes 393216 | tf_op jit(solution)/shard_map/all_to_all | solution.py:27
  59.3 11.5 %collective-permute-start.9 = (f32[8,48,256]{2,1,0:T(8,128)S(1)}, f32[8,48,256]{2,1,0:T(8,128)S(1)}, u32[]{:S(2)}, u32[]{:S(2)}) collective-permute-start(f32[8,48,256]{2,1,0:T(8,128)S(1)} %pad_maximum_fusion.1), channel_id=1, source_target_pairs={{0,8},{8,0},{1,9},{9,1},{2,10},{10,2},{3,11},{11,3},{4,12},{12,4},... | collective-permute-start | bytes 1179656 | tf_op jit(solution)/shard_map/ppermute | solution.py:90
  64.0 3.1 %collective-permute-start.5 = (f32[3,16,256]{2,1,0:T(8,128)S(1)}, f32[3,16,256]{2,1,0:T(8,128)S(1)}, u32[]{:S(2)}, u32[]{:S(2)}) collective-permute-start(f32[3,16,256]{2,1,0:T(8,128)S(1)} %broadcast_multiply_fusion.1), channel_id=1, source_target_pairs={{0,1},{1,0},{2,3},{3,2},{4,5},{5,4},{6,7},{7,6},{8,9},{9,8},{10,11... | collective-permute-start | bytes 147464 | tf_op jit(solution)/shard_map/ppermute | solution.py:101
  72.5 18.4 %all-to-all-start.2 = ((f32[16,16,128]{2,1,0:T(8,128)}), f32[16,16,128]{2,1,0:T(8,128)S(1)}, u32[]{:S(2)}, u32[]{:S(2)}) async-start(f32[16,16,128]{2,1,0:T(8,128)} %pad.8), calls=%async_computation.2 | async-start | bytes 262144 | tf_op jit(solution)/shard_map/all_to_all | solution.py:27
  91.7 24.6 %all-to-all-start.3 = ((f32[32,16,128]{2,1,0:T(8,128)}), f32[32,16,128]{2,1,0:T(8,128)S(1)}, u32[]{:S(2)}, u32[]{:S(2)}) async-start(f32[32,16,128]{2,1,0:T(8,128)} %select_maximum_fusion), calls=%async_computation.3 | async-start | bytes 524288 | tf_op jit(solution)/shard_map/all_to_all | solution.py:27
  99.4 16.2 %collective-permute-start.10 = (f32[3,32,128]{2,1,0:T(8,128)S(1)}, f32[3,32,128]{2,1,0:T(8,128)S(1)}, u32[]{:S(2)}, u32[]{:S(2)}) collective-permute-start(f32[3,32,128]{2,1,0:T(8,128)S(1)} %fusion.21), channel_id=1, source_target_pairs={{0,0},{1,1},{2,32},{3,33},{4,64},{5,65},{6,96},{7,97},{8,128},{9,1... | collective-permute-start | bytes 147464 | tf_op jit(solution)/shard_map/ppermute | solution.py:122
